TPU v7x, 512 devices: a whole 4x8x8 slice. The times are simulated.
512 devices in a mesh: cell: 32 (over y_hi, z, core), gene: 16 (over y_lo, x).
Axes of the slice: x: 4, y: 8 (y_hi: 2, y_lo: 4; y = y_hi * 4 + y_lo), z: 8, core: 2. Of those that a mesh axis runs over, the one named last changes fastest.
Arguments:
- counts: int32 [8192, 16384], P('cell', 'gene'), may hold values from 0 to 54, as said below
- cell_totals: int32 [8192], P('cell'), may hold values from 32768 to 294912, as said below
- gene_totals: int32 [16384], P('gene'), may hold values from 997 to 2991, as said below
- test_matrix: bfloat16 [16384, 96], P('gene', 'cell'), may hold values from -0.046875 to 0.046875
Outputs:
- sketch: bfloat16 [8192, 96], P('cell')
- gene_panel: bfloat16 [16384, 96], P('gene')
Inputs may be any that keep to these rules, and one draw needn't show every extreme that they name: counts are nonnegative. `cell_totals`: cell totals are positive. `gene_totals`: gene totals are positive.
All inputs are finite; a program needn't handle non-finite values.
Results may differ from a plain program's by a relative error of at most 0.03.
Values may be sent and summed in bfloat16 or wider, within the bound.
No kernel may reach another device: no remote copies, remote signals or barrier semaphores. Data moves between devices by JAX's collectives and lax.ppermute only.
A program may use at most 64 MiB of HBM per device.

v0:
```python
import math

import jax
import jax.numpy as jnp
from jax import lax
from jax.sharding import PartitionSpec as P

ITERS = 3


def pearson(counts, cell_totals, fraction):
    expected = cell_totals.astype(jnp.float32)[:, None] * fraction[None, :]
    spread = jnp.sqrt(expected + expected * expected / 100.0)
    return ((counts.astype(jnp.float32) - expected) / spread).astype(jnp.bfloat16)


def transposed_product(left, right):
    return lax.dot_general(
        left, right, (((0,), (0,)), ((), ())), preferred_element_type=jnp.float32
    )


def shards(counts, cell_totals, gene_totals, test_matrix):
    cell_rows = counts.shape[0]
    gene_cols = counts.shape[1]
    scale = 1.0 / math.sqrt(cell_rows * lax.axis_size("cell") + gene_cols * lax.axis_size("gene"))
    total = lax.psum(jnp.sum(gene_totals), "gene")
    fraction = gene_totals.astype(jnp.float32) / total.astype(jnp.float32)
    stored = pearson(counts, cell_totals, fraction)

    def cell_side(panel, factor):
        partial_sum = jnp.dot(stored, panel, preferred_element_type=jnp.float32)
        return (
            lax.psum(partial_sum.astype(jnp.bfloat16), "gene").astype(jnp.float32) * factor
        ).astype(jnp.bfloat16)

    def gene_side(sketch):
        partial_sum = transposed_product(stored, sketch)
        return (
            lax.psum(partial_sum.astype(jnp.bfloat16), "cell").astype(jnp.float32) * scale
        ).astype(jnp.bfloat16)

    test_block = lax.all_gather(test_matrix, "cell", axis=1, tiled=True)
    sketch = cell_side(test_block, 1.0)
    for step in range(ITERS):
        panel = gene_side(sketch)
        sketch = cell_side(panel, scale)
    gene_panel = gene_side(sketch)
    return (sketch, gene_panel)


def solution(mesh):
    in_specs = (P("cell", "gene"), P("cell"), P("gene"), P("gene", "cell"))
    out_specs = (P("cell", None), P("gene", None))
    return jax.shard_map(shards, mesh=mesh, in_specs=in_specs, out_specs=out_specs, check_vma=False)
```

profile of v0, /device:TPU:1, one launch (start us, length us, event | category | flops | bytes accessed | tf_op | source)
XLA Modules:
  0.0 1696.3 jit_solution(1794556545460910786)
XLA Ops:
  7.2 0.0 all-reduce.5.cloned.1.call-start
  7.2 0.0 copy-start.3
  7.2 1.3 reduce_sum.9
  8.5 0.0 copy-start.1
  8.6 0.0 copy-start.2
  8.6 13.9 psum.63
  23.1 0.0 copy-done.3
  23.2 0.0 copy-done.1
  23.2 0.0 copy-done.2
  23.2 62.6 %all-gather = bf16[32,3,1024]{2,1,0:T(4,128)(2,1)S(1)} all-gather(bf16[1,3,1024]{2,1,0:T(4,128)(2,1)S(1)} %bitcast.14), channel_id=1, replica_groups=mesh['cell'=32,'gene'=16] {'cell'}, dimensions={0}, use_global_device_ids=true | all-gather | bytes 202752 | tf_op jit(solution)/shard_map/all_gather | solution.py:43
  85.8 0.2 reshape.7
  85.9 1.6 fusion.1
  87.5 0.3 convolution_convert_fusion.7
  87.8 63.7 %psum.64 = bf16[256,96]{0,1:T(8,128)(2,1)S(1)} all-reduce(bf16[256,96]{0,1:T(8,128)(2,1)S(1)} %convolution_convert_fusion.7), channel_id=1, replica_groups=mesh['cell'=32,'gene'=16] {'gene'}, use_global_device_ids=true, to_apply=%region_2.0 | all-reduce | flops 24576 | bytes 98304 | tf_op jit(solution)/shard_map/psum | solution.py:34
  151.5 0.9 convolution_convert_fusion.3
  152.4 0.0 all-reduce.5.cloned.1.call-update
  152.4 0.0 all-reduce.7.cloned.1.call-start
  152.5 330.0 %all-reduce.5.cloned.1.call-done = bf16[1024,96]{0,1:T(8,128)(2,1)} async-done(((bf16[1024,96]{0,1:T(8,128)(2,1)}), bf16[1024,96]{0,1:T(8,128)(2,1)}) %all-reduce.5.cloned.1.call-update) | async-done | bytes 196624 | tf_op jit(solution)/shard_map/psum | solution.py:40
  482.5 1.2 convolution_convert_fusion.6
  483.8 63.0 %psum.66 = bf16[256,96]{0,1:T(8,128)(2,1)S(1)} all-reduce(bf16[256,96]{0,1:T(8,128)(2,1)S(1)} %convolution_convert_fusion.6), channel_id=1, replica_groups=mesh['cell'=32,'gene'=16] {'gene'}, use_global_device_ids=true, to_apply=%region_4.0 | all-reduce | flops 24576 | bytes 98304 | tf_op jit(solution)/shard_map/psum | solution.py:34
  546.8 0.9 convolution_convert_fusion.2
  547.7 0.0 all-reduce.7.cloned.1.call-update
  547.7 0.0 all-reduce.9.cloned.1.call-start
  547.8 336.6 %all-reduce.7.cloned.1.call-done = bf16[1024,96]{0,1:T(8,128)(2,1)} async-done(((bf16[1024,96]{0,1:T(8,128)(2,1)}), bf16[1024,96]{0,1:T(8,128)(2,1)}) %all-reduce.7.cloned.1.call-update) | async-done | bytes 196624 | tf_op jit(solution)/shard_map/psum | solution.py:40
  884.4 1.2 convolution_convert_fusion.5
  885.6 63.0 %psum.68 = bf16[256,96]{0,1:T(8,128)(2,1)S(1)} all-reduce(bf16[256,96]{0,1:T(8,128)(2,1)S(1)} %convolution_convert_fusion.5), channel_id=1, replica_groups=mesh['cell'=32,'gene'=16] {'gene'}, use_global_device_ids=true, to_apply=%region_6.0 | all-reduce | flops 24576 | bytes 98304 | tf_op jit(solution)/shard_map/psum | solution.py:34
  948.6 0.9 convolution_convert_fusion.1
  949.6 0.0 all-reduce.9.cloned.1.call-update
  949.6 0.0 all-reduce.11.cloned.1.call-start
  949.6 336.6 %all-reduce.9.cloned.1.call-done = bf16[1024,96]{0,1:T(8,128)(2,1)} async-done(((bf16[1024,96]{0,1:T(8,128)(2,1)}), bf16[1024,96]{0,1:T(8,128)(2,1)}) %all-reduce.9.cloned.1.call-update) | async-done | bytes 196624 | tf_op jit(solution)/shard_map/psum | solution.py:40
  1286.2 1.2 convolution_convert_fusion.4
  1287.5 63.0 %psum.70 = bf16[256,96]{0,1:T(8,128)(2,1)S(1)} all-reduce(bf16[256,96]{0,1:T(8,128)(2,1)S(1)} %convolution_convert_fusion.4), channel_id=1, replica_groups=mesh['cell'=32,'gene'=16] {'gene'}, use_global_device_ids=true, to_apply=%region_8.0 | all-reduce | flops 24576 | bytes 98304 | tf_op jit(solution)/shard_map/psum | solution.py:34
  1350.5 0.0 copy-start
  1350.5 0.9 convolution_convert_fusion
  1351.4 0.0 copy-done
  1351.4 0.0 all-reduce.11.cloned.1.call-update
  1351.4 336.7 %all-reduce.11.cloned.1.call-done = bf16[1024,96]{0,1:T(8,128)(2,1)} async-done(((bf16[1024,96]{0,1:T(8,128)(2,1)}), bf16[1024,96]{0,1:T(8,128)(2,1)}) %all-reduce.11.cloned.1.call-update) | async-done | bytes 196624 | tf_op jit(solution)/shard_map/psum | solution.py:40
  1688.1 1.6 multiply_convert_fusion
  (3 shorter events, 0.0 us)
Async XLA Ops:
  7.2 475.4 %all-reduce.5.cloned.1.call-start = ((), (), s32[]{:S(2)}) async-start(), calls=%async_computation | async-start | bytes 393216 | tf_op jit(solution)/shard_map/psum | solution.py:40
  7.2 15.9 copy-start.3
  8.5 14.6 copy-start.1
  8.6 14.6 copy-start.2
  152.4 731.9 %all-reduce.7.cloned.1.call-start = ((), (), s32[]{:S(2)}) async-start(), calls=%async_computation.1 | async-start | bytes 393216 | tf_op jit(solution)/shard_map/psum | solution.py:40
  547.7 738.5 %all-reduce.9.cloned.1.call-start = ((), (), s32[]{:S(2)}) async-start(), calls=%async_computation.2 | async-start | bytes 393216 | tf_op jit(solution)/shard_map/psum | solution.py:40
  949.6 738.5 %all-reduce.11.cloned.1.call-start = ((), (), s32[]{:S(2)}) async-start(), calls=%async_computation.3 | async-start | bytes 393216 | tf_op jit(solution)/shard_map/psum | solution.py:40
  1350.5 0.9 copy-start
Sparse Core Ops, SparseCore 0:
  152.6 329.9 all-reduce.4
  547.8 336.4 all-reduce.6
  949.7 336.4 all-reduce.8
  1351.6 336.4 all-reduce.10
where the time goes:
time: 1700 us
  waiting for transfers between devices  1340 us (79%)
  blocking collectives  329 us (19%)
    psum x4, waiting for transfers between devices, gene_side(): lax.psum(partial_sum.astype(jnp.bfloat16), 'cell').astype(jnp.float32)  1340 us
    psum x4, blocking collectives, cell_side(): lax.psum(partial_sum.astype(jnp.bfloat16), 'gene').astype(jnp.float32)  253 us
    all_gather x1, blocking collectives, shards(): test_block = lax.all_gather(test_matrix, 'cell', axis=1, tiled=True)  62.6 us
  transfers between devices with their start and end apart: 4, of which 4 were waited for; matrix products, arithmetic and copies ran while one was open for 0% of the time, Pallas kernels for 0%

commit v1 on v0

v1 whole, which is shorter than its diff:
```python
import math

import jax
import jax.numpy as jnp
import numpy as np
from jax import lax
from jax.sharding import Mesh, PartitionSpec as P

ITERS = 3
Y_HI, Z, CORE, Y_LO, X = 2, 8, 2, 4, 4
F32, BF16 = jnp.float32, jnp.bfloat16


def spread(x, axis, n):
    return lax.all_to_all(jnp.broadcast_to(x[None], (n,) + x.shape), axis, 0, 0, tiled=True)


def gather_sum(x, axis, n, factor=None):
    total = jnp.sum(spread(x, axis, n).astype(F32), axis=0)
    if factor is not None:
        total = total * factor
    return total.astype(BF16)


def shards(counts, cell_totals, gene_totals, test_matrix):
    rows, cols = counts.shape
    scale = 1.0 / math.sqrt(rows * Y_HI * Z * CORE + cols * Y_LO * X)

    swap = [(0, 1), (1, 0)]
    mine = counts.astype(BF16)
    other = lax.ppermute(mine, "y_hi", swap)
    hi = lax.axis_index("y_hi")

    totals = lax.all_to_all(
        jnp.broadcast_to(jnp.sum(gene_totals)[None, None], (Y_LO * X, 1)), ("y_lo", "x"), 0, 0, tiled=True
    )
    total = jnp.sum(totals)
    fraction = gene_totals.astype(F32) / total.astype(F32)
    test = spread(test_matrix.T, "z", Z).reshape(Z * test_matrix.shape[1], cols)
    both_totals = lax.all_gather(lax.all_gather(cell_totals, "core"), "y_hi")

    def resid(block, totals):
        expected = totals.astype(F32)[:, None] * fraction[None, :]
        return (
            (block.astype(F32) - expected) / jnp.sqrt(expected + expected * expected / 100.0)
        ).astype(BF16)

    core = lax.axis_index("core")
    low = jnp.where(hi == 0, mine, other)
    high = jnp.where(hi == 0, other, mine)
    pair = jnp.stack([resid(low, both_totals[0, core]), resid(high, both_totals[1, core])])
    stored = lax.all_to_all(
        jnp.broadcast_to(pair[None], (CORE,) + pair.shape), "core", 0, 0, tiled=True
    )
    stored = stored.reshape(CORE * Y_HI * rows, cols)

    def cell_side(panel, factor):
        part = lax.dot_general(
            panel, stored, (((1,), (1,)), ((), ())), preferred_element_type=F32
        ).astype(BF16)
        return gather_sum(gather_sum(part, "x", X), "y_lo", Y_LO, factor)

    def gene_side(sketch):
        part = jnp.dot(sketch, stored, preferred_element_type=F32).astype(BF16)
        return gather_sum(part, "z", Z, scale)

    sketch = cell_side(test, 1.0)
    for step in range(ITERS):
        panel = gene_side(sketch)
        sketch = cell_side(panel, scale)
    gene_panel = gene_side(sketch)

    width = sketch.shape[0]
    parts = sketch.reshape(width, CORE * Y_HI, rows).transpose(1, 0, 2)
    send = jnp.concatenate(
        [parts, jnp.broadcast_to(gene_panel[None], (CORE * Y_HI, width, cols))], axis=2
    )
    got = lax.all_to_all(send, ("core", "y_hi"), 0, 0, tiled=True)
    got = got.reshape(CORE, Y_HI, Z, width // Z, rows + cols).transpose(1, 2, 0, 3, 4)
    got = got.reshape(CORE * Y_HI * width, rows + cols)
    return (got[:, :rows].T, got[:, rows:].T)


def solution(mesh):
    fine = Mesh(
        np.asarray(mesh.devices).reshape(Y_HI, Z, CORE, Y_LO, X), ("y_hi", "z", "core", "y_lo", "x")
    )
    cell, gene = ("y_hi", "z", "core"), ("y_lo", "x")
    in_specs = (P(cell, gene), P(cell), P(gene), P(gene, cell))
    out_specs = (P(cell, None), P(gene, None))
    return jax.shard_map(shards, mesh=fine, in_specs=in_specs, out_specs=out_specs, check_vma=False)
```

time: 1700 us -> 221 us (0.13)
  waiting for transfers between devices: 1340 us -> 24.7 us
  blocking collectives: 329 us -> 150 us
  starting transfers between devices: 0.16 us -> 26.2 us
    psum x4 -> x0, waiting for transfers between devices: 1340 us -> none  [gene_side(): lax.psum(partial_sum.astype(jnp.bfloat16), 'cell').astype(jnp.float32)]
    psum x5 -> x0, blocking collectives: 267 us -> none  [the longest x4 253 us: cell_side(): lax.psum(partial_sum.astype(jnp.bfloat16), 'gene').astype(jnp.float32)]
    all_to_all x0 -> x13, blocking collectives: none -> 140 us  [the longest x11 107 us: spread(): lax.all_to_all(jnp.broadcast_to(x[None], (n,) + x.shape), axis, 0, 0, til...]
    all_gather x1 -> x2, blocking collectives: 62.6 us -> 10.5 us  [shards(): both_totals = lax.all_gather(lax.all_gather(cell_totals, 'core'), 'y_hi')]
    all_to_all x0 -> x3, waiting for transfers between devices: none -> 24.7 us  [the longest x2 15.8 us: spread(): lax.all_to_all(jnp.broadcast_to(x[None], (n,) + x.shape), axis, 0, 0, til...]
    all_to_all x0 -> x3, starting transfers between devices: none -> 18 us  [the longest x2 13.5 us: spread(): lax.all_to_all(jnp.broadcast_to(x[None], (n,) + x.shape), axis, 0, 0, til...]
  transfers between devices with their start and end apart: 4 -> 4, of which waited for: 4 -> 3; matrix products, arithmetic and copies ran while one was open for 0% -> 2% of each run, Pallas kernels for 0% -> 0%
where the time goes in v1:
time: 221 us; the launch traced here: 218 us
  blocking collectives  150 us (68%)
  starting transfers between devices  26.2 us (12%)
  waiting for transfers between devices  24.7 us (11%)
  local copies, waits for them, and re-layouts  5.88 us (3%)
  other arithmetic  5.39 us (2%)
  matrix products  4.19 us (2%)
    all_to_all x11, blocking collectives, spread(): lax.all_to_all(jnp.broadcast_to(x[None], (n,) + x.shape), axis, 0, 0, til...  107 us
    all_to_all x1, blocking collectives, shards(): got = lax.all_to_all(send, ('core', 'y_hi'), 0, 0, tiled=True)  25.8 us
    all_to_all x2, waiting for transfers between devices, spread(): lax.all_to_all(jnp.broadcast_to(x[None], (n,) + x.shape), axis, 0, 0, til...  15.8 us
    all_to_all x2, starting transfers between devices, spread(): lax.all_to_all(jnp.broadcast_to(x[None], (n,) + x.shape), axis, 0, 0, til...  13.5 us
    all_gather x2, blocking collectives, shards(): both_totals = lax.all_gather(lax.all_gather(cell_totals, 'core'), 'y_hi')  10.5 us
    all_to_all x1, waiting for transfers between devices, shards(): lax.all_to_all(jnp.broadcast_to(jnp.sum(gene_totals)[None, None], (Y_LO *...  8.9 us
    ppermute x1, starting transfers between devices, shards(): other = lax.ppermute(mine, 'y_hi', swap)  8.28 us
    all_to_all x1, blocking collectives, shards(): lax.all_to_all(jnp.broadcast_to(pair[None], (CORE,) + pair.shape), 'core'...  7.48 us
  transfers between devices with their start and end apart: 4, of which 3 were waited for; matrix products, arithmetic and copies ran while one was open for 2% of the time, Pallas kernels for 0%

profile of v1, /device:TPU:1, one launch (start us, length us, event | category | flops | bytes accessed | tf_op | source)
XLA Modules:
  0.0 218.4 jit_solution(13233982785836875830)
XLA Ops:
  0.6 1.4 convert_element_type.128
  2.0 8.3 %collective-permute-start = (bf16[256,1024]{1,0:T(8,128)(2,1)S(1)}, bf16[256,1024]{1,0:T(8,128)(2,1)S(1)}, u32[]{:S(2)}, u32[]{:S(2)}) collective-permute-start(bf16[256,1024]{1,0:T(8,128)(2,1)S(1)} %convert_element_type.128), channel_id=1, source_target_pairs={{0,256},{256,0},{1,257},{257,1},{2,258},{258,2},{3,259},{259,3},{4... | collective-permute-start | bytes 1572872 | tf_op jit(solution)/shard_map/ppermute | solution.py:31
  10.3 1.3 reduce_sum.141
  11.7 1.2 broadcast_in_dim.32
  12.9 4.5 %all-to-all-start = ((s32[16,1,1]{2,1,0:T(1,128)}), s32[16,1,1]{2,1,0:T(1,128)S(1)}, u32[]{:S(2)}, u32[]{:S(2)}) async-start(s32[16,1,1]{2,1,0:T(1,128)} %broadcast_in_dim.32), calls=%async_computation | async-start | bytes 16384 | tf_op jit(solution)/shard_map/all_to_all | solution.py:34
  17.4 2.9 %all-gather.2 = s32[2,1,256]{2,1,0:T(1,128)S(1)} all-gather(s32[1,1,256]{2,1,0:T(1,128)} %bitcast.45), channel_id=2, replica_groups=mesh['y_hi'=2,'z'=8,'core'=2,'y_lo'=4,'x'=4] {'core'}, dimensions={0}, use_global_device_ids=true | all-gather | bytes 3072 | tf_op jit(solution)/shard_map/all_gather | solution.py:40
  20.3 7.6 %all-gather.3 = s32[2,2,256]{2,1,0:T(2,128)S(1)} all-gather(s32[1,2,256]{2,1,0:T(2,128)S(1)} %copy.21), channel_id=3, replica_groups=mesh['y_hi'=2,'z'=8,'core'=2,'y_lo'=4,'x'=4] {'y_hi'}, dimensions={0}, use_global_device_ids=true | all-gather | bytes 6144 | tf_op jit(solution)/shard_map/all_gather | solution.py:40
  27.9 8.9 %all-to-all-done = s32[16,1,1]{2,1,0:T(1,128)S(1)} async-done(((s32[16,1,1]{2,1,0:T(1,128)}), s32[16,1,1]{2,1,0:T(1,128)S(1)}, u32[]{:S(2)}, u32[]{:S(2)}) %all-to-all-start) | async-done | bytes 96 | tf_op jit(solution)/shard_map/all_to_all | solution.py:34
  36.8 1.3 broadcast_in_dim.34
  38.1 10.0 %all-to-all-start.2 = ((bf16[8,3,1024]{2,1,0:T(4,128)(2,1)}), bf16[8,3,1024]{2,1,0:T(4,128)(2,1)S(1)}, u32[]{:S(2)}, u32[]{:S(2)}) async-start(bf16[8,3,1024]{2,1,0:T(4,128)(2,1)} %broadcast_in_dim.34), calls=%async_computation.2 | async-start | bytes 131072 | tf_op jit(solution)/shard_map/all_to_all | solution.py:15
  48.2 0.6 reduce_sum.142
  49.5 0.7 convert_divide_fusion
  50.2 5.2 %all-to-all-done.2 = bf16[8,3,1024]{2,1,0:T(4,128)(2,1)S(1)} async-done(((bf16[8,3,1024]{2,1,0:T(4,128)(2,1)}), bf16[8,3,1024]{2,1,0:T(4,128)(2,1)S(1)}, u32[]{:S(2)}, u32[]{:S(2)}) %all-to-all-start.2) | async-done | bytes 49184 | tf_op jit(solution)/shard_map/all_to_all | solution.py:15
  55.5 0.7 fusion.10
  56.2 0.1 pad_maximum_fusion
  56.3 0.2 broadcast_in_dim.33
  56.6 7.5 %all_to_all.81 = bf16[2,2,256,1024]{3,2,1,0:T(8,128)(2,1)S(1)} all-to-all(bf16[2,2,256,1024]{3,2,1,0:T(8,128)(2,1)S(1)} %broadcast_in_dim.33), channel_id=1, replica_groups=mesh['y_hi'=2,'z'=8,'core'=2,'y_lo'=4,'x'=4] {'core'}, dimensions={0} | all-to-all | bytes 4194304 | tf_op jit(solution)/shard_map/all_to_all | solution.py:52
  64.1 0.6 fusion
  64.7 7.8 %all_to_all.82 = bf16[4,24,1024]{2,1,0:T(8,128)(2,1)S(1)} all-to-all(bf16[4,24,1024]{2,1,0:T(8,128)(2,1)S(1)} %broadcast_in_dim.35), channel_id=1, replica_groups=mesh['y_hi'=2,'z'=8,'core'=2,'y_lo'=4,'x'=4] {'x'}, dimensions={0} | all-to-all | bytes 393216 | tf_op jit(solution)/shard_map/all_to_all | solution.py:15
  72.6 9.3 %all_to_all.83 = bf16[4,24,1024]{2,1,0:T(8,128)(2,1)S(1)} all-to-all(bf16[4,24,1024]{2,1,0:T(8,128)(2,1)S(1)} %broadcast_in_dim.36), channel_id=1, replica_groups=mesh['y_hi'=2,'z'=8,'core'=2,'y_lo'=4,'x'=4] {'y_lo'}, dimensions={0} | all-to-all | bytes 393216 | tf_op jit(solution)/shard_map/all_to_all | solution.py:15
  82.0 0.4 convolution_convert_fusion.6
  82.4 13.7 %all_to_all.84 = bf16[8,24,1024]{2,1,0:T(8,128)(2,1)S(1)} all-to-all(bf16[8,24,1024]{2,1,0:T(8,128)(2,1)S(1)} %broadcast_in_dim.37), channel_id=1, replica_groups=mesh['y_hi'=2,'z'=8,'core'=2,'y_lo'=4,'x'=4] {'z'}, dimensions={0} | all-to-all | bytes 786432 | tf_op jit(solution)/shard_map/all_to_all | solution.py:15
  96.1 0.1 convert_reduce_fusion.3
  96.1 0.7 convolution_convert_fusion.5
  96.8 7.5 %all_to_all.85 = bf16[4,24,1024]{2,1,0:T(8,128)(2,1)S(1)} all-to-all(bf16[4,24,1024]{2,1,0:T(8,128)(2,1)S(1)} %broadcast_in_dim.38), channel_id=1, replica_groups=mesh['y_hi'=2,'z'=8,'core'=2,'y_lo'=4,'x'=4] {'x'}, dimensions={0} | all-to-all | bytes 393216 | tf_op jit(solution)/shard_map/all_to_all | solution.py:15
  104.4 9.9 %all_to_all.86 = bf16[4,24,1024]{2,1,0:T(8,128)(2,1)S(1)} all-to-all(bf16[4,24,1024]{2,1,0:T(8,128)(2,1)S(1)} %broadcast_in_dim.39), channel_id=1, replica_groups=mesh['y_hi'=2,'z'=8,'core'=2,'y_lo'=4,'x'=4] {'y_lo'}, dimensions={0} | all-to-all | bytes 393216 | tf_op jit(solution)/shard_map/all_to_all | solution.py:15
  114.3 0.4 convolution_convert_fusion.4
  114.8 13.9 %all_to_all.87 = bf16[8,24,1024]{2,1,0:T(8,128)(2,1)S(1)} all-to-all(bf16[8,24,1024]{2,1,0:T(8,128)(2,1)S(1)} %broadcast_in_dim.40), channel_id=1, replica_groups=mesh['y_hi'=2,'z'=8,'core'=2,'y_lo'=4,'x'=4] {'z'}, dimensions={0} | all-to-all | bytes 786432 | tf_op jit(solution)/shard_map/all_to_all | solution.py:15
  128.7 0.1 convert_reduce_fusion.2
  128.7 0.7 convolution_convert_fusion.3
  129.4 7.5 %all_to_all.88 = bf16[4,24,1024]{2,1,0:T(8,128)(2,1)S(1)} all-to-all(bf16[4,24,1024]{2,1,0:T(8,128)(2,1)S(1)} %broadcast_in_dim.41), channel_id=1, replica_groups=mesh['y_hi'=2,'z'=8,'core'=2,'y_lo'=4,'x'=4] {'x'}, dimensions={0} | all-to-all | bytes 393216 | tf_op jit(solution)/shard_map/all_to_all | solution.py:15
  137.0 8.0 %all_to_all.89 = bf16[4,24,1024]{2,1,0:T(8,128)(2,1)S(1)} all-to-all(bf16[4,24,1024]{2,1,0:T(8,128)(2,1)S(1)} %broadcast_in_dim.42), channel_id=1, replica_groups=mesh['y_hi'=2,'z'=8,'core'=2,'y_lo'=4,'x'=4] {'y_lo'}, dimensions={0} | all-to-all | bytes 393216 | tf_op jit(solution)/shard_map/all_to_all | solution.py:15
  145.1 0.4 convolution_convert_fusion.2
  145.5 13.1 %all_to_all.90 = bf16[8,24,1024]{2,1,0:T(8,128)(2,1)S(1)} all-to-all(bf16[8,24,1024]{2,1,0:T(8,128)(2,1)S(1)} %broadcast_in_dim.43), channel_id=1, replica_groups=mesh['y_hi'=2,'z'=8,'core'=2,'y_lo'=4,'x'=4] {'z'}, dimensions={0} | all-to-all | bytes 786432 | tf_op jit(solution)/shard_map/all_to_all | solution.py:15
  158.7 0.7 convolution_convert_fusion.1
  159.4 7.8 %all_to_all.91 = bf16[4,24,1024]{2,1,0:T(8,128)(2,1)S(1)} all-to-all(bf16[4,24,1024]{2,1,0:T(8,128)(2,1)S(1)} %broadcast_in_dim.44), channel_id=1, replica_groups=mesh['y_hi'=2,'z'=8,'core'=2,'y_lo'=4,'x'=4] {'x'}, dimensions={0} | all-to-all | bytes 393216 | tf_op jit(solution)/shard_map/all_to_all | solution.py:15
  167.3 8.0 %all_to_all.92 = bf16[4,24,1024]{2,1,0:T(8,128)(2,1)S(1)} all-to-all(bf16[4,24,1024]{2,1,0:T(8,128)(2,1)S(1)} %broadcast_in_dim.45), channel_id=1, replica_groups=mesh['y_hi'=2,'z'=8,'core'=2,'y_lo'=4,'x'=4] {'y_lo'}, dimensions={0} | all-to-all | bytes 393216 | tf_op jit(solution)/shard_map/all_to_all | solution.py:15
  175.4 0.4 convolution_convert_fusion
  175.8 0.8 broadcast_in_dim.46
  176.5 3.5 %all-to-all-start.14 = ((bf16[8,24,1024]{2,1,0:T(8,128)(2,1)}), bf16[8,24,1024]{2,1,0:T(8,128)(2,1)S(1)}, u32[]{:S(2)}, u32[]{:S(2)}) async-start(bf16[8,24,1024]{2,1,0:T(8,128)(2,1)} %broadcast_in_dim.46), calls=%async_computation.14 | async-start | bytes 786432 | tf_op jit(solution)/shard_map/all_to_all | solution.py:15
  180.1 10.6 %all-to-all-done.14 = bf16[8,24,1024]{2,1,0:T(8,128)(2,1)S(1)} async-done(((bf16[8,24,1024]{2,1,0:T(8,128)(2,1)}), bf16[8,24,1024]{2,1,0:T(8,128)(2,1)S(1)}, u32[]{:S(2)}, u32[]{:S(2)}) %all-to-all-start.14) | async-done | bytes 393248 | tf_op jit(solution)/shard_map/all_to_all | solution.py:15
  190.8 25.8 %all_to_all.93 = bf16[4,24,1280]{2,1,0:T(8,128)(2,1)S(1)} all-to-all(bf16[4,24,1280]{2,1,0:T(8,128)(2,1)S(1)} %pad_maximum_fusion.1), channel_id=1, replica_groups=mesh['y_hi'=2,'z'=8,'core'=2,'y_lo'=4,'x'=4] {'core','y_hi'}, dimensions={0} | all-to-all | bytes 491520 | tf_op jit(solution)/shard_map/all_to_all | solution.py:78
  216.5 0.1 copy.24
  216.6 0.1 reshape.60
  216.7 0.1 copy.25
  216.9 0.2 reshape.61
  217.1 0.7 slice_bitcast_fusion
  217.8 0.6 slice_bitcast_fusion.1
  (33 shorter events, 0.8 us)
Async XLA Ops:
  0.6 54.8 %copy-start = (s32[256,1024]{1,0:T(8,128)S(1)}, s32[256,1024]{1,0:T(8,128)}, u32[]{:S(2)}) copy-start(s32[256,1024]{1,0:T(8,128)} %param.4) | copy-start | bytes 3145732
  2.0 53.4 %collective-permute-start = (bf16[256,1024]{1,0:T(8,128)(2,1)S(1)}, bf16[256,1024]{1,0:T(8,128)(2,1)S(1)}, u32[]{:S(2)}, u32[]{:S(2)}) collective-permute-start(bf16[256,1024]{1,0:T(8,128)(2,1)S(1)} %convert_element_type.128), channel_id=1, source_target_pairs={{0,256},{256,0},{1,257},{257,1},{2,258},{258,2},{3,259},{259,3},{4... | collective-permute-start | bytes 1572872 | tf_op jit(solution)/shard_map/ppermute | solution.py:31
  12.9 23.9 %all-to-all-start = ((s32[16,1,1]{2,1,0:T(1,128)}), s32[16,1,1]{2,1,0:T(1,128)S(1)}, u32[]{:S(2)}, u32[]{:S(2)}) async-start(s32[16,1,1]{2,1,0:T(1,128)} %broadcast_in_dim.32), calls=%async_computation | async-start | bytes 16384 | tf_op jit(solution)/shard_map/all_to_all | solution.py:34
  38.1 17.3 %all-to-all-start.2 = ((bf16[8,3,1024]{2,1,0:T(4,128)(2,1)}), bf16[8,3,1024]{2,1,0:T(4,128)(2,1)S(1)}, u32[]{:S(2)}, u32[]{:S(2)}) async-start(bf16[8,3,1024]{2,1,0:T(4,128)(2,1)} %broadcast_in_dim.34), calls=%async_computation.2 | async-start | bytes 131072 | tf_op jit(solution)/shard_map/all_to_all | solution.py:15
  176.5 14.1 %all-to-all-start.14 = ((bf16[8,24,1024]{2,1,0:T(8,128)(2,1)}), bf16[8,24,1024]{2,1,0:T(8,128)(2,1)S(1)}, u32[]{:S(2)}, u32[]{:S(2)}) async-start(bf16[8,24,1024]{2,1,0:T(8,128)(2,1)} %broadcast_in_dim.46), calls=%async_computation.14 | async-start | bytes 786432 | tf_op jit(solution)/shard_map/all_to_all | solution.py:15

commit v2 on v1

--- a/solution.py
+++ b/solution.py
@@ -8,6 +8,8 @@
 
 ITERS = 3
 Y_HI, Z, CORE, Y_LO, X = 2, 8, 2, 4, 4
+BLOCKS = CORE * Y_HI
+EXTRA = 8
 F32, BF16 = jnp.float32, jnp.bfloat16
 
 
@@ -26,33 +28,27 @@
     rows, cols = counts.shape
     scale = 1.0 / math.sqrt(rows * Y_HI * Z * CORE + cols * Y_LO * X)
 
-    swap = [(0, 1), (1, 0)]
-    mine = counts.astype(BF16)
-    other = lax.ppermute(mine, "y_hi", swap)
-    hi = lax.axis_index("y_hi")
+    pieces = jnp.stack([cell_totals >> shift & 2047 for shift in (0, 11, 22)])
+    extra = jnp.zeros((EXTRA, cols), jnp.int16).at[:3, :rows].set(pieces.astype(jnp.int16))
+    mine = jnp.concatenate([counts.astype(jnp.int16), extra])
+    other = lax.ppermute(mine, "y_hi", [(0, 1), (1, 0)])
 
     totals = lax.all_to_all(
-        jnp.broadcast_to(jnp.sum(gene_totals)[None, None], (Y_LO * X, 1)), ("y_lo", "x"), 0, 0, tiled=True
+        jnp.broadcast_to(gene_totals[None], (Y_LO * X, cols)), ("y_lo", "x"), 0, 0, tiled=True
     )
     total = jnp.sum(totals)
     fraction = gene_totals.astype(F32) / total.astype(F32)
     test = spread(test_matrix.T, "z", Z).reshape(Z * test_matrix.shape[1], cols)
-    both_totals = lax.all_gather(lax.all_gather(cell_totals, "core"), "y_hi")
 
-    def resid(block, totals):
-        expected = totals.astype(F32)[:, None] * fraction[None, :]
-        return (
-            (block.astype(F32) - expected) / jnp.sqrt(expected + expected * expected / 100.0)
-        ).astype(BF16)
-
-    core = lax.axis_index("core")
-    low = jnp.where(hi == 0, mine, other)
-    high = jnp.where(hi == 0, other, mine)
-    pair = jnp.stack([resid(low, both_totals[0, core]), resid(high, both_totals[1, core])])
-    stored = lax.all_to_all(
-        jnp.broadcast_to(pair[None], (CORE,) + pair.shape), "core", 0, 0, tiled=True
-    )
-    stored = stored.reshape(CORE * Y_HI * rows, cols)
+    blocks = lax.all_gather(jnp.stack([mine, other]), "core").reshape(BLOCKS, rows + EXTRA, cols)
+    pieces = blocks[:, rows : rows + 3, :rows].astype(jnp.int32)
+    owned = (pieces[:, 0] + (pieces[:, 1] << 11) + (pieces[:, 2] << 22)).astype(F32)
+    expected = owned[:, :, None] * fraction[None, None, :]
+    stored = (
+        (blocks[:, :rows].astype(F32) - expected)
+        / jnp.sqrt(expected + expected * expected / 100.0)
+    ).astype(BF16)
+    stored = stored.reshape(BLOCKS * rows, cols)
 
     def cell_side(panel, factor):
         part = lax.dot_general(
@@ -71,13 +67,15 @@
     gene_panel = gene_side(sketch)
 
     width = sketch.shape[0]
-    parts = sketch.reshape(width, CORE * Y_HI, rows).transpose(1, 0, 2)
+    parts = sketch.reshape(width, CORE, Y_HI, rows)
+    parts = jnp.where(lax.axis_index("y_hi") == 0, parts, parts[:, :, ::-1])
+    parts = parts.reshape(width, BLOCKS, rows).transpose(1, 0, 2)
     send = jnp.concatenate(
-        [parts, jnp.broadcast_to(gene_panel[None], (CORE * Y_HI, width, cols))], axis=2
+        [parts, jnp.broadcast_to(gene_panel[None], (BLOCKS, width, cols))], axis=2
     )
     got = lax.all_to_all(send, ("core", "y_hi"), 0, 0, tiled=True)
     got = got.reshape(CORE, Y_HI, Z, width // Z, rows + cols).transpose(1, 2, 0, 3, 4)
-    got = got.reshape(CORE * Y_HI * width, rows + cols)
+    got = got.reshape(BLOCKS * width, rows + cols)
     return (got[:, :rows].T, got[:, rows:].T)
 
 

time: 221 us -> 208 us (0.941)
  starting transfers between devices: 26.2 us -> 16.2 us
  blocking collectives: 150 us -> 158 us
  waiting for transfers between devices: 24.7 us -> 17.4 us
    all_to_all x11 -> x12, blocking collectives: 107 us -> 127 us  [spread(): lax.all_to_all(jnp.broadcast_to(x[None], (n,) + x.shape), axis, 0, 0, til...]
    all_to_all x2 -> x1, starting transfers between devices: 13.5 us -> 3.45 us  [spread(): lax.all_to_all(jnp.broadcast_to(x[None], (n,) + x.shape), axis, 0, 0, til...]
    all_to_all x1 -> x0, blocking collectives: 7.48 us -> none  [shards(): lax.all_to_all(jnp.broadcast_to(pair[None], (CORE,) + pair.shape), 'core'...]
    all_to_all x2 -> x1, waiting for transfers between devices: 15.8 us -> 10.2 us  [spread(): lax.all_to_all(jnp.broadcast_to(x[None], (n,) + x.shape), axis, 0, 0, til...]
    all_gather x2 -> x1, blocking collectives: 10.5 us -> 6.5 us  [shards(): lax.all_gather(jnp.stack([mine, other]), 'core')]
  transfers between devices with their start and end apart: 4 -> 3, of which waited for: 3 -> 2; matrix products, arithmetic and copies ran while one was open for 2% -> 1% of each run, Pallas kernels for 0% -> 0%
where the time goes in v2:
time: 208 us; the launch traced here: 206 us
  blocking collectives  158 us (76%)
  waiting for transfers between devices  17.4 us (8%)
  starting transfers between devices  16.2 us (8%)
  other arithmetic  5.13 us (2%)
  matrix products  4.19 us (2%)
  local copies, waits for them, and re-layouts  4.06 us (2%)
    all_to_all x12, blocking collectives, spread(): lax.all_to_all(jnp.broadcast_to(x[None], (n,) + x.shape), axis, 0, 0, til...  127 us
    all_to_all x1, blocking collectives, shards(): got = lax.all_to_all(send, ('core', 'y_hi'), 0, 0, tiled=True)  24.4 us
    all_to_all x1, waiting for transfers between devices, spread(): lax.all_to_all(jnp.broadcast_to(x[None], (n,) + x.shape), axis, 0, 0, til...  10.2 us
    ppermute x1, starting transfers between devices, shards(): other = lax.ppermute(mine, 'y_hi', [(0, 1), (1, 0)])  8.28 us
    all_to_all x1, waiting for transfers between devices, shards(): lax.all_to_all(jnp.broadcast_to(gene_totals[None], (Y_LO * X, cols)), ('y...  7.2 us
    all_gather x1, blocking collectives, shards(): lax.all_gather(jnp.stack([mine, other]), 'core')  6.5 us
    all_to_all x1, starting transfers between devices, shards(): lax.all_to_all(jnp.broadcast_to(gene_totals[None], (Y_LO * X, cols)), ('y...  4.47 us
  transfers between devices with their start and end apart: 3, of which 2 were waited for; matrix products, arithmetic and copies ran while one was open for 1% of the time, Pallas kernels for 0%

profile of v2, /device:TPU:1, one launch (start us, length us, event | category | flops | bytes accessed | tf_op | source)
XLA Modules:
  0.0 206.2 jit_solution(6324967981498752053)
XLA Ops:
  0.7 0.7 and_convert_fusion.2
  1.4 1.3 convert_element_type.116
  2.7 0.1 fusion.18
  2.8 8.3 %collective-permute-start = (s16[264,1024]{1,0:T(8,128)(2,1)S(1)}, s16[264,1024]{1,0:T(8,128)(2,1)S(1)}, u32[]{:S(2)}, u32[]{:S(2)}) collective-permute-start(s16[264,1024]{1,0:T(8,128)(2,1)S(1)} %get-tuple-element.15), channel_id=1, source_target_pairs={{0,256},{256,0},{1,257},{257,1},{2,258},{258,2},{3,259},{259,3},{4... | collective-permute-start | bytes 1622024 | tf_op jit(solution)/shard_map/ppermute | solution.py:34
  11.1 17.4 %all_to_all.76 = bf16[8,3,1024]{2,1,0:T(4,128)(2,1)S(1)} all-to-all(bf16[8,3,1024]{2,1,0:T(4,128)(2,1)S(1)} %broadcast_in_dim.31), channel_id=1, replica_groups=mesh['y_hi'=2,'z'=8,'core'=2,'y_lo'=4,'x'=4] {'z'}, dimensions={0} | all-to-all | bytes 98304 | tf_op jit(solution)/shard_map/all_to_all | solution.py:17
  28.5 0.7 broadcast_in_dim.30
  29.2 4.5 %all-to-all-start = ((s32[16,1,1024]{2,1,0:T(1,128)}), s32[16,1,1024]{2,1,0:T(1,128)S(1)}, u32[]{:S(2)}, u32[]{:S(2)}) async-start(s32[16,1,1024]{2,1,0:T(1,128)} %broadcast_in_dim.30), calls=%async_computation | async-start | bytes 131072 | tf_op jit(solution)/shard_map/all_to_all | solution.py:36
  33.7 7.2 %all-to-all-done = s32[16,1,1024]{2,1,0:T(1,128)S(1)} async-done(((s32[16,1,1024]{2,1,0:T(1,128)}), s32[16,1,1024]{2,1,0:T(1,128)S(1)}, u32[]{:S(2)}, u32[]{:S(2)}) %all-to-all-start) | async-done | bytes 65568 | tf_op jit(solution)/shard_map/all_to_all | solution.py:36
  40.9 0.8 reduce_sum.132
  42.3 0.0 collective-permute-done
  42.3 0.1 pad_add_fusion
  42.4 6.5 %all-gather.2 = s16[4,264,1024]{2,1,0:T(8,128)(2,1)S(1)} all-gather(s16[2,264,1024]{2,1,0:T(8,128)(2,1)S(1)} %pad_add_fusion), channel_id=2, replica_groups=mesh['y_hi'=2,'z'=8,'core'=2,'y_lo'=4,'x'=4] {'core'}, dimensions={0}, use_global_device_ids=true | all-gather | bytes 3244032 | tf_op jit(solution)/shard_map/all_gather | solution.py:43
  49.0 1.6 fusion.1
  50.5 0.7 fusion.4
  51.2 7.8 %all_to_all.77 = bf16[4,24,1024]{2,1,0:T(8,128)(2,1)S(1)} all-to-all(bf16[4,24,1024]{2,1,0:T(8,128)(2,1)S(1)} %broadcast_in_dim.32), channel_id=1, replica_groups=mesh['y_hi'=2,'z'=8,'core'=2,'y_lo'=4,'x'=4] {'x'}, dimensions={0} | all-to-all | bytes 393216 | tf_op jit(solution)/shard_map/all_to_all | solution.py:17
  59.1 8.0 %all_to_all.78 = bf16[4,24,1024]{2,1,0:T(8,128)(2,1)S(1)} all-to-all(bf16[4,24,1024]{2,1,0:T(8,128)(2,1)S(1)} %broadcast_in_dim.33), channel_id=1, replica_groups=mesh['y_hi'=2,'z'=8,'core'=2,'y_lo'=4,'x'=4] {'y_lo'}, dimensions={0} | all-to-all | bytes 393216 | tf_op jit(solution)/shard_map/all_to_all | solution.py:17
  67.2 0.4 convolution_convert_fusion.6
  67.6 17.9 %all_to_all.79 = bf16[8,24,1024]{2,1,0:T(8,128)(2,1)S(1)} all-to-all(bf16[8,24,1024]{2,1,0:T(8,128)(2,1)S(1)} %broadcast_in_dim.34), channel_id=1, replica_groups=mesh['y_hi'=2,'z'=8,'core'=2,'y_lo'=4,'x'=4] {'z'}, dimensions={0} | all-to-all | bytes 786432 | tf_op jit(solution)/shard_map/all_to_all | solution.py:17
  85.5 0.1 convert_reduce_fusion.3
  85.5 0.7 convolution_convert_fusion.5
  86.2 7.5 %all_to_all.80 = bf16[4,24,1024]{2,1,0:T(8,128)(2,1)S(1)} all-to-all(bf16[4,24,1024]{2,1,0:T(8,128)(2,1)S(1)} %broadcast_in_dim.35), channel_id=1, replica_groups=mesh['y_hi'=2,'z'=8,'core'=2,'y_lo'=4,'x'=4] {'x'}, dimensions={0} | all-to-all | bytes 393216 | tf_op jit(solution)/shard_map/all_to_all | solution.py:17
  93.8 9.0 %all_to_all.81 = bf16[4,24,1024]{2,1,0:T(8,128)(2,1)S(1)} all-to-all(bf16[4,24,1024]{2,1,0:T(8,128)(2,1)S(1)} %broadcast_in_dim.36), channel_id=1, replica_groups=mesh['y_hi'=2,'z'=8,'core'=2,'y_lo'=4,'x'=4] {'y_lo'}, dimensions={0} | all-to-all | bytes 393216 | tf_op jit(solution)/shard_map/all_to_all | solution.py:17
  102.8 0.4 convolution_convert_fusion.4
  103.2 14.7 %all_to_all.82 = bf16[8,24,1024]{2,1,0:T(8,128)(2,1)S(1)} all-to-all(bf16[8,24,1024]{2,1,0:T(8,128)(2,1)S(1)} %broadcast_in_dim.37), channel_id=1, replica_groups=mesh['y_hi'=2,'z'=8,'core'=2,'y_lo'=4,'x'=4] {'z'}, dimensions={0} | all-to-all | bytes 786432 | tf_op jit(solution)/shard_map/all_to_all | solution.py:17
  117.9 0.1 convert_reduce_fusion.2
  118.0 0.7 convolution_convert_fusion.3
  118.7 7.5 %all_to_all.83 = bf16[4,24,1024]{2,1,0:T(8,128)(2,1)S(1)} all-to-all(bf16[4,24,1024]{2,1,0:T(8,128)(2,1)S(1)} %broadcast_in_dim.38), channel_id=1, replica_groups=mesh['y_hi'=2,'z'=8,'core'=2,'y_lo'=4,'x'=4] {'x'}, dimensions={0} | all-to-all | bytes 393216 | tf_op jit(solution)/shard_map/all_to_all | solution.py:17
  126.3 8.0 %all_to_all.84 = bf16[4,24,1024]{2,1,0:T(8,128)(2,1)S(1)} all-to-all(bf16[4,24,1024]{2,1,0:T(8,128)(2,1)S(1)} %broadcast_in_dim.39), channel_id=1, replica_groups=mesh['y_hi'=2,'z'=8,'core'=2,'y_lo'=4,'x'=4] {'y_lo'}, dimensions={0} | all-to-all | bytes 393216 | tf_op jit(solution)/shard_map/all_to_all | solution.py:17
  134.3 0.4 convolution_convert_fusion.2
  134.8 13.1 %all_to_all.85 = bf16[8,24,1024]{2,1,0:T(8,128)(2,1)S(1)} all-to-all(bf16[8,24,1024]{2,1,0:T(8,128)(2,1)S(1)} %broadcast_in_dim.40), channel_id=1, replica_groups=mesh['y_hi'=2,'z'=8,'core'=2,'y_lo'=4,'x'=4] {'z'}, dimensions={0} | all-to-all | bytes 786432 | tf_op jit(solution)/shard_map/all_to_all | solution.py:17
  147.9 0.1 convert_reduce_fusion.1
  148.0 0.7 convolution_convert_fusion.1
  148.7 7.5 %all_to_all.86 = bf16[4,24,1024]{2,1,0:T(8,128)(2,1)S(1)} all-to-all(bf16[4,24,1024]{2,1,0:T(8,128)(2,1)S(1)} %broadcast_in_dim.41), channel_id=1, replica_groups=mesh['y_hi'=2,'z'=8,'core'=2,'y_lo'=4,'x'=4] {'x'}, dimensions={0} | all-to-all | bytes 393216 | tf_op jit(solution)/shard_map/all_to_all | solution.py:17
  156.3 8.2 %all_to_all.87 = bf16[4,24,1024]{2,1,0:T(8,128)(2,1)S(1)} all-to-all(bf16[4,24,1024]{2,1,0:T(8,128)(2,1)S(1)} %broadcast_in_dim.42), channel_id=1, replica_groups=mesh['y_hi'=2,'z'=8,'core'=2,'y_lo'=4,'x'=4] {'y_lo'}, dimensions={0} | all-to-all | bytes 393216 | tf_op jit(solution)/shard_map/all_to_all | solution.py:17
  164.5 0.4 convolution_convert_fusion
  164.9 0.8 broadcast_in_dim.43
  165.7 3.5 %all-to-all-start.13 = ((bf16[8,24,1024]{2,1,0:T(8,128)(2,1)}), bf16[8,24,1024]{2,1,0:T(8,128)(2,1)S(1)}, u32[]{:S(2)}, u32[]{:S(2)}) async-start(bf16[8,24,1024]{2,1,0:T(8,128)(2,1)} %broadcast_in_dim.43), calls=%async_computation.13 | async-start | bytes 786432 | tf_op jit(solution)/shard_map/all_to_all | solution.py:17
  169.2 0.3 rev.3
  169.5 0.1 broadcast_select_fusion
  169.6 10.2 %all-to-all-done.13 = bf16[8,24,1024]{2,1,0:T(8,128)(2,1)S(1)} async-done(((bf16[8,24,1024]{2,1,0:T(8,128)(2,1)}), bf16[8,24,1024]{2,1,0:T(8,128)(2,1)S(1)}, u32[]{:S(2)}, u32[]{:S(2)}) %all-to-all-start.13) | async-done | bytes 393248 | tf_op jit(solution)/shard_map/all_to_all | solution.py:17
  179.8 0.1 convert_reduce_fusion
  179.9 24.4 %all_to_all.88 = bf16[4,24,1280]{2,1,0:T(8,128)(2,1)S(1)} all-to-all(bf16[4,24,1280]{2,1,0:T(8,128)(2,1)S(1)} %pad_maximum_fusion), channel_id=1, replica_groups=mesh['y_hi'=2,'z'=8,'core'=2,'y_lo'=4,'x'=4] {'core','y_hi'}, dimensions={0} | all-to-all | bytes 491520 | tf_op jit(solution)/shard_map/all_to_all | solution.py:76
  204.3 0.1 copy.19
  204.4 0.1 reshape.110
  204.5 0.1 copy.20
  204.7 0.2 reshape.111
  204.9 0.7 slice_bitcast_fusion
  205.6 0.6 slice_bitcast_fusion.1
  (39 shorter events, 0.8 us)
Async XLA Ops:
  0.6 10.5 %copy-start.1 = (bf16[1024,3]{0,1:T(4,128)(2,1)S(1)}, bf16[1024,3]{0,1:T(4,128)(2,1)}, u32[]{:S(2)}) copy-start(bf16[1024,3]{0,1:T(4,128)(2,1)} %param.9) | copy-start | bytes 18436
  0.6 27.9 %copy-start = (s32[1024]{0:T(1024)S(1)}, s32[1024]{0:T(1024)}, u32[]{:S(2)}) copy-start(s32[1024]{0:T(1024)} %param.8) | copy-start | bytes 12292
  2.8 39.5 %collective-permute-start = (s16[264,1024]{1,0:T(8,128)(2,1)S(1)}, s16[264,1024]{1,0:T(8,128)(2,1)S(1)}, u32[]{:S(2)}, u32[]{:S(2)}) collective-permute-start(s16[264,1024]{1,0:T(8,128)(2,1)S(1)} %get-tuple-element.15), channel_id=1, source_target_pairs={{0,256},{256,0},{1,257},{257,1},{2,258},{258,2},{3,259},{259,3},{4... | collective-permute-start | bytes 1622024 | tf_op jit(solution)/shard_map/ppermute | solution.py:34
  29.2 11.7 %all-to-all-start = ((s32[16,1,1024]{2,1,0:T(1,128)}), s32[16,1,1024]{2,1,0:T(1,128)S(1)}, u32[]{:S(2)}, u32[]{:S(2)}) async-start(s32[16,1,1024]{2,1,0:T(1,128)} %broadcast_in_dim.30), calls=%async_computation | async-start | bytes 131072 | tf_op jit(solution)/shard_map/all_to_all | solution.py:36
  165.7 14.1 %all-to-all-start.13 = ((bf16[8,24,1024]{2,1,0:T(8,128)(2,1)}), bf16[8,24,1024]{2,1,0:T(8,128)(2,1)S(1)}, u32[]{:S(2)}, u32[]{:S(2)}) async-start(bf16[8,24,1024]{2,1,0:T(8,128)(2,1)} %broadcast_in_dim.43), calls=%async_computation.13 | async-start | bytes 786432 | tf_op jit(solution)/shard_map/all_to_all | solution.py:17

commit v3 on v2

v3 whole, which is shorter than its diff:
```python
import math

import jax
import jax.numpy as jnp
import numpy as np
from jax import lax
from jax.sharding import Mesh, PartitionSpec as P

ITERS = 3
Y_HI, Z, CORE, Y_LO, X_HI, X_LO = 2, 8, 2, 4, 2, 2
X, BLOCKS, EXTRA = X_HI * X_LO, CORE * Y_HI, 8
F32, BF16, I16 = jnp.float32, jnp.bfloat16, jnp.int16
PAIRS = ((0, 3), (1, 2))


def copies(x, n):
    return jnp.broadcast_to(x[None], (n,) + x.shape)


def spread(x, axis, n):
    return lax.all_to_all(copies(x, n), axis, 0, 0, tiled=True)


def gather_sum(x, axis, n, factor=None):
    got = spread(x, axis, n)
    total = got[0].astype(F32)
    for i in range(1, n):
        total = total + got[i].astype(F32)
    if factor is not None:
        total = total * factor
    return total.astype(BF16)


def shards(counts, cell_totals, gene_totals, test_matrix):
    rows, cols = counts.shape
    scale = 1.0 / math.sqrt(rows * Y_HI * Z * CORE + cols * Y_LO * X)
    x_hi = lax.axis_index("x_hi")

    totals = spread(gene_totals, ("y_lo", "x_hi", "x_lo"), Y_LO * X)
    total = jnp.sum(totals).astype(F32)
    fraction = gene_totals.astype(F32) / total
    place = lax.axis_index(("y_lo", "x_hi", "x_lo"))
    beside = lax.dynamic_index_in_dim(totals, place ^ 3, 0, keepdims=False).astype(F32) / total

    pieces = jnp.stack([cell_totals >> shift & 2047 for shift in (0, 11, 22)])
    extra = jnp.zeros((EXTRA, cols), I16).at[:3, :rows].set(pieces.astype(I16))
    mine = jnp.concatenate([counts.astype(I16), extra])

    def over_y(block):
        return lax.ppermute(block, "y_hi", [(0, 1), (1, 0)])

    def over_x(block):
        return lax.ppermute(block, ("x_hi", "x_lo"), [(i, 3 - i) for i in range(X)])

    def resid(block, fraction):
        both = lax.all_gather(block, "core")
        pieces = both[:, rows : rows + 3, :rows].astype(jnp.int32)
        owned = (pieces[:, 0] + (pieces[:, 1] << 11) + (pieces[:, 2] << 22)).astype(F32)
        expected = owned[:, :, None] * fraction[None, None, :]
        return (
            (both[:, :rows].astype(F32) - expected)
            / jnp.sqrt(expected + expected * expected / 100.0)
        ).astype(BF16)

    other = over_y(mine)
    near = over_x(mine)
    test = spread(test_matrix.T, "z", Z).reshape(Z * test_matrix.shape[1], cols)
    far = over_x(other)

    cells = BLOCKS * rows
    own = jnp.concatenate([resid(mine, fraction), resid(other, fraction)]).reshape(cells, cols)

    def cell_part(panel, stored):
        return lax.dot_general(
            panel, stored, (((1,), (1,)), ((), ())), preferred_element_type=F32
        ).astype(BF16)

    part = gather_sum(cell_part(test, own), ("x_hi", "x_lo"), X)
    width = part.shape[0] // 2
    part = jnp.where(x_hi == 0, part[:width], part[width:])
    sketch = gather_sum(part, "y_lo", Y_LO)

    paired = jnp.concatenate([resid(near, beside), resid(far, beside)]).reshape(cells, cols)
    stored = jnp.concatenate([own, paired], axis=1)

    def gene_side(sketch):
        part = jnp.dot(sketch, stored, preferred_element_type=F32).astype(BF16)
        return gather_sum(part, "z", Z, scale)

    def cell_side(panel):
        return gather_sum(cell_part(panel, stored), ("y_lo", "x_lo"), Y_LO * X_LO, scale)

    for step in range(ITERS):
        sketch = cell_side(gene_side(sketch))
    gene_panel = gene_side(sketch)

    parts = sketch.reshape(width, Y_HI, CORE, rows)
    parts = jnp.where(lax.axis_index("y_hi") == 0, parts, parts[:, ::-1])
    parts = parts.transpose(1, 2, 0, 3)[:, :, None]
    parts = jnp.broadcast_to(parts, (Y_HI, CORE, 2, width, rows))
    halves = gene_panel.reshape(width, 2, cols)
    halves = jnp.where(x_hi == 0, halves, halves[:, ::-1]).transpose(1, 0, 2)
    halves = jnp.broadcast_to(halves, (Y_HI, CORE, 2, width, cols))
    send = jnp.concatenate([parts, halves], axis=4).reshape(BLOCKS * 2, width, rows + cols)
    groups = [
        [(y * CORE + c) * X + x for y in range(Y_HI) for c in range(CORE) for x in pair]
        for pair in PAIRS
    ]
    got = lax.all_to_all(
        send, ("y_hi", "core", "x_hi", "x_lo"), 0, 0, axis_index_groups=groups, tiled=True
    )
    got = got.reshape(Y_HI, CORE, 2, Z // 2, 2 * width // Z, rows + cols).transpose(0, 2, 3, 1, 4, 5)
    got = got.reshape(BLOCKS * 2 * width, rows + cols)
    return (got[:, :rows].T, got[:, rows:].T)


def solution(mesh):
    fine = Mesh(
        np.asarray(mesh.devices).reshape(Y_HI, Z, CORE, Y_LO, X_HI, X_LO),
        ("y_hi", "z", "core", "y_lo", "x_hi", "x_lo"),
    )
    cell, gene = ("y_hi", "z", "core"), ("y_lo", "x_hi", "x_lo")
    in_specs = (P(cell, gene), P(cell), P(gene), P(gene, cell))
    out_specs = (P(cell, None), P(gene, None))
    return jax.shard_map(shards, mesh=fine, in_specs=in_specs, out_specs=out_specs, check_vma=False)
```

time: 208 us -> 227 us (1.091)
  blocking collectives: 158 us -> 127 us
  starting transfers between devices: 16.2 us -> 40.9 us
  waiting for transfers between devices: 17.4 us -> 31.4 us
  matrix products: 4.19 us -> 8.58 us
  other arithmetic: 5.13 us -> 8.04 us
    all_to_all x13 -> x7, blocking collectives: 151 us -> 111 us  [the longest x6 89.9 us: spread(): return lax.all_to_all(copies(x, n), axis, 0, 0, tiled=True)]
    all_to_all x2 -> x5, starting transfers between devices: 7.92 us -> 23.7 us  [spread(): return lax.all_to_all(copies(x, n), axis, 0, 0, tiled=True)]
    all_gather x1 -> x4, blocking collectives: 6.5 us -> 15.9 us  [resid(): both = lax.all_gather(block, 'core')]
    ppermute x1 -> x3, starting transfers between devices: 8.28 us -> 17.2 us  [the longest x2 8.93 us: over_x(): return lax.ppermute(block, ('x_hi', 'x_lo'), [(i, 3 - i) for i in range(X)])]
    ppermute x1 -> x3, waiting for transfers between devices: 0.01 us -> 8.4 us  [the longest x2 8.4 us: over_x(): return lax.ppermute(block, ('x_hi', 'x_lo'), [(i, 3 - i) for i in range(X)])]
    all_to_all x2 -> x5, waiting for transfers between devices: 17.4 us -> 23 us  [spread(): return lax.all_to_all(copies(x, n), axis, 0, 0, tiled=True)]
    dot_general x4, matrix products: 1.56 us -> 4.38 us  [gene_side(): part = jnp.dot(sketch, stored, preferred_element_type=F32).astype(BF16)]
    convert_element_type x4 -> x11, other arithmetic: 2.91 us -> 4.54 us  [the longest x2 3.18 us: resid(): return ((both[:, :rows].astype(F32) - expected) / jnp.sqrt(expected + exp...]
  transfers between devices with their start and end apart: 3 -> 8, of which waited for: 2 -> 5; matrix products, arithmetic and copies ran while one was open for 1% -> 3% of each run, Pallas kernels for 0% -> 0%
where the time goes in v3:
time: 227 us; the launch traced here: 224 us
  blocking collectives  127 us (56%)
  starting transfers between devices  40.9 us (18%)
  waiting for transfers between devices  31.4 us (14%)
  matrix products  8.58 us (4%)
  other arithmetic  8.04 us (4%)
  local copies, waits for them, and re-layouts  6.28 us (3%)
    all_to_all x6, blocking collectives, spread(): return lax.all_to_all(copies(x, n), axis, 0, 0, tiled=True)  89.9 us
    all_to_all x5, starting transfers between devices, spread(): return lax.all_to_all(copies(x, n), axis, 0, 0, tiled=True)  23.7 us
    all_to_all x5, waiting for transfers between devices, spread(): return lax.all_to_all(copies(x, n), axis, 0, 0, tiled=True)  23 us
    all_to_all x1, blocking collectives, shards(): lax.all_to_all(send, ('y_hi', 'core', 'x_hi', 'x_lo'), 0, 0, axis_index_g...  21.3 us
    all_gather x4, blocking collectives, resid(): both = lax.all_gather(block, 'core')  15.9 us
    ppermute x2, starting transfers between devices, over_x(): return lax.ppermute(block, ('x_hi', 'x_lo'), [(i, 3 - i) for i in range(X)])  8.93 us
    ppermute x2, waiting for transfers between devices, over_x(): return lax.ppermute(block, ('x_hi', 'x_lo'), [(i, 3 - i) for i in range(X)])  8.4 us
    ppermute x1, starting transfers between devices, over_y(): return lax.ppermute(block, 'y_hi', [(0, 1), (1, 0)])  8.28 us
  transfers between devices with their start and end apart: 8, of which 5 were waited for; matrix products, arithmetic and copies ran while one was open for 3% of the time, Pallas kernels for 0%

profile of v3, /device:TPU:1, one launch (start us, length us, event | category | flops | bytes accessed | tf_op | source)
XLA Modules:
  0.0 224.0 jit_solution(10441009738866841220)
XLA Ops:
  0.6 0.7 and_convert_fusion.2
  1.4 1.3 convert_element_type.496
  2.7 8.3 %collective-permute-start = (s16[264,1024]{1,0:T(8,128)(2,1)S(1)}, s16[264,1024]{1,0:T(8,128)(2,1)}, u32[]{:S(2)}, u32[]{:S(2)}) collective-permute-start(s16[264,1024]{1,0:T(8,128)(2,1)S(1)} %pad_add_fusion), channel_id=1, source_target_pairs={{0,256},{256,0},{1,257},{257,1},{2,258},{258,2},{3,259},{259,3},{4... | collective-permute-start | bytes 1622024 | tf_op jit(solution)/shard_map/ppermute | solution.py:50
  11.0 4.4 %collective-permute-start.1 = (s16[264,1024]{1,0:T(8,128)(2,1)S(1)}, s16[264,1024]{1,0:T(8,128)(2,1)}, u32[]{:S(2)}, u32[]{:S(2)}) collective-permute-start(s16[264,1024]{1,0:T(8,128)(2,1)S(1)} %pad_add_fusion), channel_id=1, source_target_pairs={{0,3},{1,2},{2,1},{3,0},{4,7},{5,6},{6,5},{7,4},{8,11},{9,10},{10,... | collective-permute-start | bytes 1622024 | tf_op jit(solution)/shard_map/ppermute | solution.py:53
  15.4 0.6 broadcast_in_dim.27
  16.1 10.0 %all-to-all-start.1 = ((bf16[8,3,1024]{2,1,0:T(4,128)(2,1)}), bf16[8,3,1024]{2,1,0:T(4,128)(2,1)S(1)}, u32[]{:S(2)}, u32[]{:S(2)}) async-start(bf16[8,3,1024]{2,1,0:T(4,128)(2,1)} %broadcast_in_dim.27), calls=%async_computation.1 | async-start | bytes 131072 | tf_op jit(solution)/shard_map/all_to_all | solution.py:21
  26.1 3.7 %all-gather.11 = s16[528,1024]{1,0:T(8,128)(2,1)S(1)} all-gather(s16[264,1024]{1,0:T(8,128)(2,1)S(1)} %pad_add_fusion), channel_id=2, replica_groups=mesh['y_hi'=2,'z'=8,'core'=2,'y_lo'=4,'x_hi'=2,'x_lo'=2] {'core'}, dimensions={0}, use_global_device_ids=true | all-gather | bytes 1622016 | tf_op jit(solution)/shard_map/all_gather | solution.py:56
  29.8 3.5 %all-to-all-done.1 = bf16[8,3,1024]{2,1,0:T(4,128)(2,1)S(1)} async-done(((bf16[8,3,1024]{2,1,0:T(4,128)(2,1)}), bf16[8,3,1024]{2,1,0:T(4,128)(2,1)S(1)}, u32[]{:S(2)}, u32[]{:S(2)}) %all-to-all-start.1) | async-done | bytes 49184 | tf_op jit(solution)/shard_map/all_to_all | solution.py:21
  33.3 0.7 broadcast_in_dim.26
  34.0 3.5 %all-to-all-start = ((s32[16,1,1024]{2,1,0:T(1,128)}), s32[16,1,1024]{2,1,0:T(1,128)S(1)}, u32[]{:S(2)}, u32[]{:S(2)}) async-start(s32[16,1,1024]{2,1,0:T(1,128)} %broadcast_in_dim.26), calls=%async_computation | async-start | bytes 131072 | tf_op jit(solution)/shard_map/all_to_all | solution.py:21
  37.6 7.1 %all-to-all-done = s32[16,1,1024]{2,1,0:T(1,128)S(1)} async-done(((s32[16,1,1024]{2,1,0:T(1,128)}), s32[16,1,1024]{2,1,0:T(1,128)S(1)}, u32[]{:S(2)}, u32[]{:S(2)}) %all-to-all-start) | async-done | bytes 65568 | tf_op jit(solution)/shard_map/all_to_all | solution.py:21
  44.7 0.8 reduce_sum.9
  46.2 6.2 %all-gather.9 = s16[528,1024]{1,0:T(8,128)(2,1)S(1)} all-gather(s16[264,1024]{1,0:T(8,128)(2,1)} %collective-permute-done.1), channel_id=4, replica_groups=mesh['y_hi'=2,'z'=8,'core'=2,'y_lo'=4,'x_hi'=2,'x_lo'=2] {'core'}, dimensions={0}, use_global_device_ids=true | all-gather | bytes 1622016 | tf_op jit(solution)/shard_map/all_gather | solution.py:56
  52.4 2.8 %all-gather.10 = s16[528,1024]{1,0:T(8,128)(2,1)S(1)} all-gather(s16[264,1024]{1,0:T(8,128)(2,1)} %collective-permute-done), channel_id=3, replica_groups=mesh['y_hi'=2,'z'=8,'core'=2,'y_lo'=4,'x_hi'=2,'x_lo'=2] {'core'}, dimensions={0}, use_global_device_ids=true | all-gather | bytes 1622016 | tf_op jit(solution)/shard_map/all_gather | solution.py:56
  55.3 1.6 fusion.1
  56.9 0.2 pad_maximum_fusion.1
  57.1 0.7 fusion.16
  57.7 0.7 broadcast_in_dim.28
  58.4 3.4 %all-to-all-start.2 = ((bf16[4,24,1024]{2,1,0:T(8,128)(2,1)}), bf16[4,24,1024]{2,1,0:T(8,128)(2,1)S(1)}, u32[]{:S(2)}, u32[]{:S(2)}) async-start(bf16[4,24,1024]{2,1,0:T(8,128)(2,1)} %broadcast_in_dim.28), calls=%async_computation.2 | async-start | bytes 393216 | tf_op jit(solution)/shard_map/all_to_all | solution.py:21
  61.8 4.5 %collective-permute-start.2 = (s16[264,1024]{1,0:T(8,128)(2,1)}, s16[264,1024]{1,0:T(8,128)(2,1)}, u32[]{:S(2)}, u32[]{:S(2)}) collective-permute-start(s16[264,1024]{1,0:T(8,128)(2,1)} %collective-permute-done), channel_id=1, source_target_pairs={{0,3},{1,2},{2,1},{3,0},{4,7},{5,6},{6,5},{7,4},{8,11},{9,10},{10,... | collective-permute-start | bytes 1622024 | tf_op jit(solution)/shard_map/ppermute | solution.py:53
  66.4 0.8 all-to-all-done.2
  67.2 0.7 broadcast_in_dim.29
  67.9 3.3 %all-to-all-start.3 = ((bf16[4,12,1024]{2,1,0:T(8,128)(2,1)}), bf16[4,12,1024]{2,1,0:T(8,128)(2,1)S(1)}, u32[]{:S(2)}, u32[]{:S(2)}) async-start(bf16[4,12,1024]{2,1,0:T(8,128)(2,1)} %broadcast_in_dim.29), calls=%async_computation.3 | async-start | bytes 262144 | tf_op jit(solution)/shard_map/all_to_all | solution.py:21
  71.2 8.4 %collective-permute-done.2 = s16[264,1024]{1,0:T(8,128)(2,1)} collective-permute-done((s16[264,1024]{1,0:T(8,128)(2,1)}, s16[264,1024]{1,0:T(8,128)(2,1)}, u32[]{:S(2)}, u32[]{:S(2)}) %collective-permute-start.2) | collective-permute-done | bytes 540704 | tf_op jit(solution)/shard_map/ppermute | solution.py:53
  79.6 3.1 %all-gather.8 = s16[528,1024]{1,0:T(8,128)(2,1)S(1)} all-gather(s16[264,1024]{1,0:T(8,128)(2,1)} %collective-permute-done.2), channel_id=5, replica_groups=mesh['y_hi'=2,'z'=8,'core'=2,'y_lo'=4,'x_hi'=2,'x_lo'=2] {'core'}, dimensions={0}, use_global_device_ids=true | all-gather | bytes 1622016 | tf_op jit(solution)/shard_map/all_gather | solution.py:56
  82.8 1.6 fusion.9
  84.4 1.5 pad_maximum_fusion.2
  85.9 2.4 %convolution_convert_fusion.3 = bf16[12,2048]{1,0:T(8,128)(2,1)S(1)} fusion(bf16[4,12,1024]{2,1,0:T(8,128)(2,1)S(1)} %all-to-all-done.3, bf16[1024,1024]{1,0:T(8,128)(2,1)} %bitcast.75, bf16[1024,1024]{1,0:T(8,128)(2,1)S(1)} %bitcast.60), kind=kOutput, calls=%fused_computation.16 | convolution fusion | flops 58843136 | bytes 4341760 | tf_op jit(solution)/shard_map/dot_general | solution.py:87
  88.4 20.4 %all_to_all.61 = bf16[8,12,2048]{2,1,0:T(8,128)(2,1)S(1)} all-to-all(bf16[8,12,2048]{2,1,0:T(8,128)(2,1)S(1)} %broadcast_in_dim.30), channel_id=1, replica_groups=mesh['y_hi'=2,'z'=8,'core'=2,'y_lo'=4,'x_hi'=2,'x_lo'=2] {'z'}, dimensions={0} | all-to-all | bytes 786432 | tf_op jit(solution)/shard_map/all_to_all | solution.py:21
  108.8 1.2 convolution_convert_fusion.7
  110.0 9.7 %all_to_all.62 = bf16[8,12,1024]{2,1,0:T(8,128)(2,1)S(1)} all-to-all(bf16[8,12,1024]{2,1,0:T(8,128)(2,1)S(1)} %broadcast_in_dim.31), channel_id=1, replica_groups=mesh['y_hi'=2,'z'=8,'core'=2,'y_lo'=4,'x_hi'=2,'x_lo'=2] {'y_lo','x_lo'}, dimensions={0} | all-to-all | bytes 393216 | tf_op jit(solution)/shard_map/all_to_all | solution.py:21
  119.7 0.7 convolution_convert_fusion.2
  120.4 16.9 %all_to_all.63 = bf16[8,12,2048]{2,1,0:T(8,128)(2,1)S(1)} all-to-all(bf16[8,12,2048]{2,1,0:T(8,128)(2,1)S(1)} %broadcast_in_dim.32), channel_id=1, replica_groups=mesh['y_hi'=2,'z'=8,'core'=2,'y_lo'=4,'x_hi'=2,'x_lo'=2] {'z'}, dimensions={0} | all-to-all | bytes 786432 | tf_op jit(solution)/shard_map/all_to_all | solution.py:21
  137.3 1.2 convolution_convert_fusion.6
  138.5 13.2 %all_to_all.64 = bf16[8,12,1024]{2,1,0:T(8,128)(2,1)S(1)} all-to-all(bf16[8,12,1024]{2,1,0:T(8,128)(2,1)S(1)} %broadcast_in_dim.33), channel_id=1, replica_groups=mesh['y_hi'=2,'z'=8,'core'=2,'y_lo'=4,'x_hi'=2,'x_lo'=2] {'y_lo','x_lo'}, dimensions={0} | all-to-all | bytes 393216 | tf_op jit(solution)/shard_map/all_to_all | solution.py:21
  151.7 0.7 convolution_convert_fusion.1
  152.4 15.6 %all_to_all.65 = bf16[8,12,2048]{2,1,0:T(8,128)(2,1)S(1)} all-to-all(bf16[8,12,2048]{2,1,0:T(8,128)(2,1)S(1)} %broadcast_in_dim.34), channel_id=1, replica_groups=mesh['y_hi'=2,'z'=8,'core'=2,'y_lo'=4,'x_hi'=2,'x_lo'=2] {'z'}, dimensions={0} | all-to-all | bytes 786432 | tf_op jit(solution)/shard_map/all_to_all | solution.py:21
  168.1 1.2 convolution_convert_fusion.5
  169.3 14.2 %all_to_all.66 = bf16[8,12,1024]{2,1,0:T(8,128)(2,1)S(1)} all-to-all(bf16[8,12,1024]{2,1,0:T(8,128)(2,1)S(1)} %broadcast_in_dim.35), channel_id=1, replica_groups=mesh['y_hi'=2,'z'=8,'core'=2,'y_lo'=4,'x_hi'=2,'x_lo'=2] {'y_lo','x_lo'}, dimensions={0} | all-to-all | bytes 393216 | tf_op jit(solution)/shard_map/all_to_all | solution.py:21
  183.5 0.7 convolution_convert_fusion
  184.2 0.9 broadcast_in_dim.37
  185.0 3.5 %all-to-all-start.10 = ((bf16[8,12,2048]{2,1,0:T(8,128)(2,1)}), bf16[8,12,2048]{2,1,0:T(8,128)(2,1)S(1)}, u32[]{:S(2)}, u32[]{:S(2)}) async-start(bf16[8,12,2048]{2,1,0:T(8,128)(2,1)} %broadcast_in_dim.37), calls=%async_computation.10 | async-start | bytes 1048576 | tf_op jit(solution)/shard_map/all_to_all | solution.py:21
  188.6 11.5 %all-to-all-done.10 = bf16[8,12,2048]{2,1,0:T(8,128)(2,1)S(1)} async-done(((bf16[8,12,2048]{2,1,0:T(8,128)(2,1)}), bf16[8,12,2048]{2,1,0:T(8,128)(2,1)S(1)}, u32[]{:S(2)}, u32[]{:S(2)}) %all-to-all-start.10) | async-done | bytes 393248 | tf_op jit(solution)/shard_map/all_to_all | solution.py:21
  200.2 0.4 rev.7
  200.9 21.3 %all_to_all.67 = bf16[8,12,1280]{2,1,0:T(8,128)(2,1)S(1)} all-to-all(bf16[8,12,1280]{2,1,0:T(8,128)(2,1)S(1)} %bitcast.82), channel_id=1, replica_groups={{0,3,16,19,256,259,272,275},{1,2,17,18,257,258,273,274},{4,7,20,23,260,..., dimensions={0} | all-to-all | bytes 491520 | tf_op jit(solution)/shard_map/all_to_all | solution.py:109
  222.5 0.2 reshape.331
  222.7 0.7 slice_bitcast_fusion
  223.4 0.6 slice_bitcast_fusion.1
  (51 shorter events, 1.2 us)
Async XLA Ops:
  0.6 14.8 %copy-start.2 = (bf16[1024,3]{0,1:T(4,128)(2,1)S(1)}, bf16[1024,3]{0,1:T(4,128)(2,1)}, u32[]{:S(2)}) copy-start(bf16[1024,3]{0,1:T(4,128)(2,1)} %param.9) | copy-start | bytes 18436
  1.3 32.0 %copy-start.1 = (s32[1024]{0:T(1024)S(1)}, s32[1024]{0:T(1024)}, u32[]{:S(2)}) copy-start(s32[1024]{0:T(1024)} %param.8) | copy-start | bytes 12292
  2.7 49.7 %collective-permute-start = (s16[264,1024]{1,0:T(8,128)(2,1)S(1)}, s16[264,1024]{1,0:T(8,128)(2,1)}, u32[]{:S(2)}, u32[]{:S(2)}) collective-permute-start(s16[264,1024]{1,0:T(8,128)(2,1)S(1)} %pad_add_fusion), channel_id=1, source_target_pairs={{0,256},{256,0},{1,257},{257,1},{2,258},{258,2},{3,259},{259,3},{4... | collective-permute-start | bytes 1622024 | tf_op jit(solution)/shard_map/ppermute | solution.py:50
  11.0 35.2 %collective-permute-start.1 = (s16[264,1024]{1,0:T(8,128)(2,1)S(1)}, s16[264,1024]{1,0:T(8,128)(2,1)}, u32[]{:S(2)}, u32[]{:S(2)}) collective-permute-start(s16[264,1024]{1,0:T(8,128)(2,1)S(1)} %pad_add_fusion), channel_id=1, source_target_pairs={{0,3},{1,2},{2,1},{3,0},{4,7},{5,6},{6,5},{7,4},{8,11},{9,10},{10,... | collective-permute-start | bytes 1622024 | tf_op jit(solution)/shard_map/ppermute | solution.py:53
  16.1 17.3 %all-to-all-start.1 = ((bf16[8,3,1024]{2,1,0:T(4,128)(2,1)}), bf16[8,3,1024]{2,1,0:T(4,128)(2,1)S(1)}, u32[]{:S(2)}, u32[]{:S(2)}) async-start(bf16[8,3,1024]{2,1,0:T(4,128)(2,1)} %broadcast_in_dim.27), calls=%async_computation.1 | async-start | bytes 131072 | tf_op jit(solution)/shard_map/all_to_all | solution.py:21
  34.0 10.7 %all-to-all-start = ((s32[16,1,1024]{2,1,0:T(1,128)}), s32[16,1,1024]{2,1,0:T(1,128)S(1)}, u32[]{:S(2)}, u32[]{:S(2)}) async-start(s32[16,1,1024]{2,1,0:T(1,128)} %broadcast_in_dim.26), calls=%async_computation | async-start | bytes 131072 | tf_op jit(solution)/shard_map/all_to_all | solution.py:21
  58.4 8.8 %all-to-all-start.2 = ((bf16[4,24,1024]{2,1,0:T(8,128)(2,1)}), bf16[4,24,1024]{2,1,0:T(8,128)(2,1)S(1)}, u32[]{:S(2)}, u32[]{:S(2)}) async-start(bf16[4,24,1024]{2,1,0:T(8,128)(2,1)} %broadcast_in_dim.28), calls=%async_computation.2 | async-start | bytes 393216 | tf_op jit(solution)/shard_map/all_to_all | solution.py:21
  61.8 17.8 %collective-permute-start.2 = (s16[264,1024]{1,0:T(8,128)(2,1)}, s16[264,1024]{1,0:T(8,128)(2,1)}, u32[]{:S(2)}, u32[]{:S(2)}) collective-permute-start(s16[264,1024]{1,0:T(8,128)(2,1)} %collective-permute-done), channel_id=1, source_target_pairs={{0,3},{1,2},{2,1},{3,0},{4,7},{5,6},{6,5},{7,4},{8,11},{9,10},{10,... | collective-permute-start | bytes 1622024 | tf_op jit(solution)/shard_map/ppermute | solution.py:53
  67.9 18.0 %all-to-all-start.3 = ((bf16[4,12,1024]{2,1,0:T(8,128)(2,1)}), bf16[4,12,1024]{2,1,0:T(8,128)(2,1)S(1)}, u32[]{:S(2)}, u32[]{:S(2)}) async-start(bf16[4,12,1024]{2,1,0:T(8,128)(2,1)} %broadcast_in_dim.29), calls=%async_computation.3 | async-start | bytes 262144 | tf_op jit(solution)/shard_map/all_to_all | solution.py:21
  85.9 22.8 %copy-start = (bf16[4,256,1024]{2,1,0:T(8,128)(2,1)S(1)}, bf16[4,256,1024]{2,1,0:T(8,128)(2,1)}, u32[]{:S(2)}) copy-start(bf16[4,256,1024]{2,1,0:T(8,128)(2,1)} %pad_maximum_fusion.2) | copy-start | bytes 6291460
  185.0 15.1 %all-to-all-start.10 = ((bf16[8,12,2048]{2,1,0:T(8,128)(2,1)}), bf16[8,12,2048]{2,1,0:T(8,128)(2,1)S(1)}, u32[]{:S(2)}, u32[]{:S(2)}) async-start(bf16[8,12,2048]{2,1,0:T(8,128)(2,1)} %broadcast_in_dim.37), calls=%async_computation.10 | async-start | bytes 1048576 | tf_op jit(solution)/shard_map/all_to_all | solution.py:21

commit v4 on v2

v4 whole, which is shorter than its diff:
```python
import math

import jax
import jax.numpy as jnp
import numpy as np
from jax import lax
from jax.sharding import Mesh, PartitionSpec as P

ITERS = 3
Y_HI, Z, CORE, Y_LO, X = 2, 8, 2, 4, 4
BLOCKS = CORE * Y_HI
EXTRA = 8
F32, BF16, I16 = jnp.float32, jnp.bfloat16, jnp.int16


def copies(x, n):
    return jnp.broadcast_to(x[None], (n,) + x.shape)


def spread(x, axis, n):
    return lax.all_to_all(copies(x, n), axis, 0, 0, tiled=True)


def gather_sum(x, axis, n, factor=None):
    got = spread(x, axis, n)
    total = got[0].astype(F32)
    for i in range(1, n):
        total = total + got[i].astype(F32)
    if factor is not None:
        total = total * factor
    return total.astype(BF16)


def shards(counts, cell_totals, gene_totals, test_matrix):
    rows, cols = counts.shape
    scale = 1.0 / math.sqrt(rows * Y_HI * Z * CORE + cols * Y_LO * X)

    everyone = spread(gene_totals, ("y_lo", "x"), Y_LO * X)

    pieces = jnp.stack([cell_totals >> shift & 2047 for shift in (0, 11, 22)])
    extra = jnp.zeros((EXTRA, cols), I16).at[:3, :rows].set(pieces.astype(I16))
    mine = jnp.concatenate([counts.astype(I16), extra])
    other = lax.ppermute(mine, "y_hi", [(0, 1), (1, 0)])

    total = jnp.sum(everyone).astype(F32)
    fraction = gene_totals.astype(F32) / total
    test, fraction = lax.optimization_barrier((test_matrix.T, fraction))
    test = spread(test, "z", Z).reshape(Z * test_matrix.shape[1], cols)

    def resid(block):
        both = lax.all_gather(block, "core")
        pieces = both[:, rows : rows + 3, :rows].astype(jnp.int32)
        owned = (pieces[:, 0] + (pieces[:, 1] << 11) + (pieces[:, 2] << 22)).astype(F32)
        expected = owned[:, :, None] * fraction[None, None, :]
        return (
            (both[:, :rows].astype(F32) - expected)
            / jnp.sqrt(expected + expected * expected / 100.0)
        ).astype(BF16)

    stored = jnp.concatenate([resid(mine), resid(other)]).reshape(BLOCKS * rows, cols)

    def cell_side(panel, factor):
        part = lax.dot_general(
            panel, stored, (((1,), (1,)), ((), ())), preferred_element_type=F32
        ).astype(BF16)
        return gather_sum(gather_sum(part, "x", X), "y_lo", Y_LO, factor)

    def gene_side(sketch):
        part = jnp.dot(sketch, stored, preferred_element_type=F32).astype(BF16)
        return gather_sum(part, "z", Z, scale)

    sketch = cell_side(test, 1.0)
    for step in range(ITERS):
        panel = gene_side(sketch)
        sketch = cell_side(panel, scale)
    gene_panel = gene_side(sketch)

    width = sketch.shape[0]
    parts = sketch.reshape(width, Y_HI, CORE, rows)
    parts = jnp.where(lax.axis_index("y_hi") == 0, parts, parts[:, ::-1])
    parts = parts.reshape(width, BLOCKS, rows).transpose(1, 0, 2)
    send = jnp.concatenate([parts, copies(gene_panel, BLOCKS)], axis=2)
    got = lax.all_to_all(send, ("y_hi", "core"), 0, 0, tiled=True)
    got = got.reshape(Y_HI, CORE, Z, width // Z, rows + cols).transpose(0, 2, 1, 3, 4)
    got = got.reshape(BLOCKS * width, rows + cols)
    return (got[:, :rows].T, got[:, rows:].T)


def solution(mesh):
    fine = Mesh(
        np.asarray(mesh.devices).reshape(Y_HI, Z, CORE, Y_LO, X), ("y_hi", "z", "core", "y_lo", "x")
    )
    cell, gene = ("y_hi", "z", "core"), ("y_lo", "x")
    in_specs = (P(cell, gene), P(cell), P(gene), P(gene, cell))
    out_specs = (P(cell, None), P(gene, None))
    return jax.shard_map(shards, mesh=fine, in_specs=in_specs, out_specs=out_specs, check_vma=False)
```

time: 208 us -> 219 us (1.053)
  waiting for transfers between devices: 17.4 us -> 37.5 us
  blocking collectives: 158 us -> 138 us
  starting transfers between devices: 16.2 us -> 26.2 us
    all_to_all x13 -> x12, blocking collectives: 151 us -> 130 us  [the longest x11 106 us: spread(): return lax.all_to_all(copies(x, n), axis, 0, 0, tiled=True)]
    all_to_all x2 -> x3, waiting for transfers between devices: 17.4 us -> 37.5 us  [spread(): return lax.all_to_all(copies(x, n), axis, 0, 0, tiled=True)]
    all_to_all x2 -> x3, starting transfers between devices: 7.92 us -> 18 us  [spread(): return lax.all_to_all(copies(x, n), axis, 0, 0, tiled=True)]
    all_gather x1 -> x2, blocking collectives: 6.5 us -> 7.83 us  [resid(): both = lax.all_gather(block, 'core')]
  transfers between devices with their start and end apart: 3 -> 4, of which waited for: 2 -> 3; matrix products, arithmetic and copies ran while one was open for 1% -> 1% of each run, Pallas kernels for 0% -> 0%
where the time goes in v4:
time: 219 us; the launch traced here: 217 us
  blocking collectives  138 us (63%)
  waiting for transfers between devices  37.5 us (17%)
  starting transfers between devices  26.2 us (12%)
  other arithmetic  4.86 us (2%)
  local copies, waits for them, and re-layouts  4.38 us (2%)
  matrix products  4.17 us (2%)
    all_to_all x11, blocking collectives, spread(): return lax.all_to_all(copies(x, n), axis, 0, 0, tiled=True)  106 us
    all_to_all x3, waiting for transfers between devices, spread(): return lax.all_to_all(copies(x, n), axis, 0, 0, tiled=True)  37.5 us
    all_to_all x1, blocking collectives, shards(): got = lax.all_to_all(send, ('y_hi', 'core'), 0, 0, tiled=True)  24.1 us
    all_to_all x3, starting transfers between devices, spread(): return lax.all_to_all(copies(x, n), axis, 0, 0, tiled=True)  18 us
    ppermute x1, starting transfers between devices, shards(): other = lax.ppermute(mine, 'y_hi', [(0, 1), (1, 0)])  8.28 us
    all_gather x2, blocking collectives, resid(): both = lax.all_gather(block, 'core')  7.83 us
  transfers between devices with their start and end apart: 4, of which 3 were waited for; matrix products, arithmetic and copies ran while one was open for 1% of the time, Pallas kernels for 0%

profile of v4, /device:TPU:1, one launch (start us, length us, event | category | flops | bytes accessed | tf_op | source)
XLA Modules:
  0.0 217.0 jit_solution(5151873564835804115)
XLA Ops:
  0.6 0.0 copy-start
  0.6 0.7 and_convert_fusion.2
  1.3 0.0 copy-start.1
  1.4 1.3 convert_element_type.403
  2.7 8.3 %collective-permute-start = (s16[264,1024]{1,0:T(8,128)(2,1)S(1)}, s16[264,1024]{1,0:T(8,128)(2,1)S(1)}, u32[]{:S(2)}, u32[]{:S(2)}) collective-permute-start(s16[264,1024]{1,0:T(8,128)(2,1)S(1)} %pad_add_fusion), channel_id=1, source_target_pairs={{0,256},{256,0},{1,257},{257,1},{2,258},{258,2},{3,259},{259,3},{4... | collective-permute-start | bytes 1622024 | tf_op jit(solution)/shard_map/ppermute | solution.py:43
  11.0 0.0 copy-done
  11.0 0.7 broadcast_in_dim.40
  11.7 4.5 %all-to-all-start = ((s32[16,1,1024]{2,1,0:T(1,128)}), s32[16,1,1024]{2,1,0:T(1,128)S(1)}, u32[]{:S(2)}, u32[]{:S(2)}) async-start(s32[16,1,1024]{2,1,0:T(1,128)} %broadcast_in_dim.40), calls=%async_computation | async-start | bytes 131072 | tf_op jit(solution)/shard_map/all_to_all | solution.py:21
  16.2 3.4 %all-gather.5 = s16[528,1024]{1,0:T(8,128)(2,1)S(1)} all-gather(s16[264,1024]{1,0:T(8,128)(2,1)S(1)} %pad_add_fusion), channel_id=2, replica_groups=mesh['y_hi'=2,'z'=8,'core'=2,'y_lo'=4,'x'=4] {'core'}, dimensions={0}, use_global_device_ids=true | all-gather | bytes 1622016 | tf_op jit(solution)/shard_map/all_gather | solution.py:51
  19.6 19.7 %all-to-all-done = s32[16,1,1024]{2,1,0:T(1,128)S(1)} async-done(((s32[16,1,1024]{2,1,0:T(1,128)}), s32[16,1,1024]{2,1,0:T(1,128)S(1)}, u32[]{:S(2)}, u32[]{:S(2)}) %all-to-all-start) | async-done | bytes 65568 | tf_op jit(solution)/shard_map/all_to_all | solution.py:21
  39.3 0.8 reduce_sum.9
  40.8 0.6 broadcast_in_dim.41
  41.4 10.0 %all-to-all-start.1 = ((bf16[8,3,1024]{2,1,0:T(4,128)(2,1)}), bf16[8,3,1024]{2,1,0:T(4,128)(2,1)S(1)}, u32[]{:S(2)}, u32[]{:S(2)}) async-start(bf16[8,3,1024]{2,1,0:T(4,128)(2,1)} %broadcast_in_dim.41), calls=%async_computation.1 | async-start | bytes 131072 | tf_op jit(solution)/shard_map/all_to_all | solution.py:21
  51.5 7.2 %all-to-all-done.1 = bf16[8,3,1024]{2,1,0:T(4,128)(2,1)S(1)} async-done(((bf16[8,3,1024]{2,1,0:T(4,128)(2,1)}), bf16[8,3,1024]{2,1,0:T(4,128)(2,1)S(1)}, u32[]{:S(2)}, u32[]{:S(2)}) %all-to-all-start.1) | async-done | bytes 49184 | tf_op jit(solution)/shard_map/all_to_all | solution.py:21
  58.7 0.0 collective-permute-done
  58.7 4.4 %all-gather.4 = s16[528,1024]{1,0:T(8,128)(2,1)S(1)} all-gather(s16[264,1024]{1,0:T(8,128)(2,1)S(1)} %collective-permute-done), channel_id=3, replica_groups=mesh['y_hi'=2,'z'=8,'core'=2,'y_lo'=4,'x'=4] {'core'}, dimensions={0}, use_global_device_ids=true | all-gather | bytes 1622016 | tf_op jit(solution)/shard_map/all_gather | solution.py:51
  63.2 1.6 fusion.1
  64.8 0.2 pad_maximum_fusion
  64.9 0.7 convolution_convert_fusion.7
  65.6 7.6 %all_to_all.76 = bf16[4,24,1024]{2,1,0:T(8,128)(2,1)S(1)} all-to-all(bf16[4,24,1024]{2,1,0:T(8,128)(2,1)S(1)} %broadcast_in_dim.42), channel_id=1, replica_groups=mesh['y_hi'=2,'z'=8,'core'=2,'y_lo'=4,'x'=4] {'x'}, dimensions={0} | all-to-all | bytes 393216 | tf_op jit(solution)/shard_map/all_to_all | solution.py:21
  73.3 9.3 %all_to_all.77 = bf16[4,24,1024]{2,1,0:T(8,128)(2,1)S(1)} all-to-all(bf16[4,24,1024]{2,1,0:T(8,128)(2,1)S(1)} %broadcast_in_dim.44), channel_id=1, replica_groups=mesh['y_hi'=2,'z'=8,'core'=2,'y_lo'=4,'x'=4] {'y_lo'}, dimensions={0} | all-to-all | bytes 393216 | tf_op jit(solution)/shard_map/all_to_all | solution.py:21
  82.6 0.4 convolution_convert_fusion.6
  83.0 13.6 %all_to_all.78 = bf16[8,24,1024]{2,1,0:T(8,128)(2,1)S(1)} all-to-all(bf16[8,24,1024]{2,1,0:T(8,128)(2,1)S(1)} %broadcast_in_dim.45), channel_id=1, replica_groups=mesh['y_hi'=2,'z'=8,'core'=2,'y_lo'=4,'x'=4] {'z'}, dimensions={0} | all-to-all | bytes 786432 | tf_op jit(solution)/shard_map/all_to_all | solution.py:21
  96.6 0.7 convolution_convert_fusion.5
  97.3 7.5 %all_to_all.79 = bf16[4,24,1024]{2,1,0:T(8,128)(2,1)S(1)} all-to-all(bf16[4,24,1024]{2,1,0:T(8,128)(2,1)S(1)} %broadcast_in_dim.46), channel_id=1, replica_groups=mesh['y_hi'=2,'z'=8,'core'=2,'y_lo'=4,'x'=4] {'x'}, dimensions={0} | all-to-all | bytes 393216 | tf_op jit(solution)/shard_map/all_to_all | solution.py:21
  104.9 9.6 %all_to_all.80 = bf16[4,24,1024]{2,1,0:T(8,128)(2,1)S(1)} all-to-all(bf16[4,24,1024]{2,1,0:T(8,128)(2,1)S(1)} %broadcast_in_dim.48), channel_id=1, replica_groups=mesh['y_hi'=2,'z'=8,'core'=2,'y_lo'=4,'x'=4] {'y_lo'}, dimensions={0} | all-to-all | bytes 393216 | tf_op jit(solution)/shard_map/all_to_all | solution.py:21
  114.5 0.4 convolution_convert_fusion.4
  115.0 14.2 %all_to_all.81 = bf16[8,24,1024]{2,1,0:T(8,128)(2,1)S(1)} all-to-all(bf16[8,24,1024]{2,1,0:T(8,128)(2,1)S(1)} %broadcast_in_dim.49), channel_id=1, replica_groups=mesh['y_hi'=2,'z'=8,'core'=2,'y_lo'=4,'x'=4] {'z'}, dimensions={0} | all-to-all | bytes 786432 | tf_op jit(solution)/shard_map/all_to_all | solution.py:21
  129.1 0.7 convolution_convert_fusion.3
  129.8 7.5 %all_to_all.82 = bf16[4,24,1024]{2,1,0:T(8,128)(2,1)S(1)} all-to-all(bf16[4,24,1024]{2,1,0:T(8,128)(2,1)S(1)} %broadcast_in_dim.50), channel_id=1, replica_groups=mesh['y_hi'=2,'z'=8,'core'=2,'y_lo'=4,'x'=4] {'x'}, dimensions={0} | all-to-all | bytes 393216 | tf_op jit(solution)/shard_map/all_to_all | solution.py:21
  137.4 8.0 %all_to_all.83 = bf16[4,24,1024]{2,1,0:T(8,128)(2,1)S(1)} all-to-all(bf16[4,24,1024]{2,1,0:T(8,128)(2,1)S(1)} %broadcast_in_dim.52), channel_id=1, replica_groups=mesh['y_hi'=2,'z'=8,'core'=2,'y_lo'=4,'x'=4] {'y_lo'}, dimensions={0} | all-to-all | bytes 393216 | tf_op jit(solution)/shard_map/all_to_all | solution.py:21
  145.4 0.4 convolution_convert_fusion.2
  145.9 13.1 %all_to_all.84 = bf16[8,24,1024]{2,1,0:T(8,128)(2,1)S(1)} all-to-all(bf16[8,24,1024]{2,1,0:T(8,128)(2,1)S(1)} %broadcast_in_dim.53), channel_id=1, replica_groups=mesh['y_hi'=2,'z'=8,'core'=2,'y_lo'=4,'x'=4] {'z'}, dimensions={0} | all-to-all | bytes 786432 | tf_op jit(solution)/shard_map/all_to_all | solution.py:21
  159.0 0.7 convolution_convert_fusion.1
  159.7 7.8 %all_to_all.85 = bf16[4,24,1024]{2,1,0:T(8,128)(2,1)S(1)} all-to-all(bf16[4,24,1024]{2,1,0:T(8,128)(2,1)S(1)} %broadcast_in_dim.54), channel_id=1, replica_groups=mesh['y_hi'=2,'z'=8,'core'=2,'y_lo'=4,'x'=4] {'x'}, dimensions={0} | all-to-all | bytes 393216 | tf_op jit(solution)/shard_map/all_to_all | solution.py:21
  167.6 8.0 %all_to_all.86 = bf16[4,24,1024]{2,1,0:T(8,128)(2,1)S(1)} all-to-all(bf16[4,24,1024]{2,1,0:T(8,128)(2,1)S(1)} %broadcast_in_dim.56), channel_id=1, replica_groups=mesh['y_hi'=2,'z'=8,'core'=2,'y_lo'=4,'x'=4] {'y_lo'}, dimensions={0} | all-to-all | bytes 393216 | tf_op jit(solution)/shard_map/all_to_all | solution.py:21
  175.6 0.4 convolution_convert_fusion
  176.0 0.8 broadcast_in_dim.57
  176.8 3.5 %all-to-all-start.13 = ((bf16[8,24,1024]{2,1,0:T(8,128)(2,1)}), bf16[8,24,1024]{2,1,0:T(8,128)(2,1)S(1)}, u32[]{:S(2)}, u32[]{:S(2)}) async-start(bf16[8,24,1024]{2,1,0:T(8,128)(2,1)} %broadcast_in_dim.57), calls=%async_computation.13 | async-start | bytes 786432 | tf_op jit(solution)/shard_map/all_to_all | solution.py:21
  180.3 10.6 %all-to-all-done.13 = bf16[8,24,1024]{2,1,0:T(8,128)(2,1)S(1)} async-done(((bf16[8,24,1024]{2,1,0:T(8,128)(2,1)}), bf16[8,24,1024]{2,1,0:T(8,128)(2,1)S(1)}, u32[]{:S(2)}, u32[]{:S(2)}) %all-to-all-start.13) | async-done | bytes 393248 | tf_op jit(solution)/shard_map/all_to_all | solution.py:21
  190.9 0.1 fusion.24
  191.0 24.1 %all_to_all.87 = bf16[4,24,1280]{2,1,0:T(8,128)(2,1)S(1)} all-to-all(bf16[4,24,1280]{2,1,0:T(8,128)(2,1)S(1)} %pad_maximum_fusion.1), channel_id=1, replica_groups=mesh['y_hi'=2,'z'=8,'core'=2,'y_lo'=4,'x'=4] {'y_hi','core'}, dimensions={0} | all-to-all | bytes 491520 | tf_op jit(solution)/shard_map/all_to_all | solution.py:83
  215.1 0.1 copy.19
  215.2 0.1 reshape.136
  215.3 0.1 copy.20
  215.5 0.2 reshape.137
  215.7 0.7 slice_bitcast_fusion
  216.4 0.6 slice_bitcast_fusion.1
  (35 shorter events, 0.7 us)
Async XLA Ops:
  0.6 10.4 %copy-start = (s32[1024]{0:T(1024)S(1)}, s32[1024]{0:T(1024)}, u32[]{:S(2)}) copy-start(s32[1024]{0:T(1024)} %param.8) | copy-start | bytes 12292
  1.3 39.4 %copy-start.1 = (bf16[1024,3]{0,1:T(4,128)(2,1)S(1)}, bf16[1024,3]{0,1:T(4,128)(2,1)}, u32[]{:S(2)}) copy-start(bf16[1024,3]{0,1:T(4,128)(2,1)} %param.9) | copy-start | bytes 18436
  2.7 56.0 %collective-permute-start = (s16[264,1024]{1,0:T(8,128)(2,1)S(1)}, s16[264,1024]{1,0:T(8,128)(2,1)S(1)}, u32[]{:S(2)}, u32[]{:S(2)}) collective-permute-start(s16[264,1024]{1,0:T(8,128)(2,1)S(1)} %pad_add_fusion), channel_id=1, source_target_pairs={{0,256},{256,0},{1,257},{257,1},{2,258},{258,2},{3,259},{259,3},{4... | collective-permute-start | bytes 1622024 | tf_op jit(solution)/shard_map/ppermute | solution.py:43
  11.7 27.6 %all-to-all-start = ((s32[16,1,1024]{2,1,0:T(1,128)}), s32[16,1,1024]{2,1,0:T(1,128)S(1)}, u32[]{:S(2)}, u32[]{:S(2)}) async-start(s32[16,1,1024]{2,1,0:T(1,128)} %broadcast_in_dim.40), calls=%async_computation | async-start | bytes 131072 | tf_op jit(solution)/shard_map/all_to_all | solution.py:21
  41.4 17.3 %all-to-all-start.1 = ((bf16[8,3,1024]{2,1,0:T(4,128)(2,1)}), bf16[8,3,1024]{2,1,0:T(4,128)(2,1)S(1)}, u32[]{:S(2)}, u32[]{:S(2)}) async-start(bf16[8,3,1024]{2,1,0:T(4,128)(2,1)} %broadcast_in_dim.41), calls=%async_computation.1 | async-start | bytes 131072 | tf_op jit(solution)/shard_map/all_to_all | solution.py:21
  176.8 14.1 %all-to-all-start.13 = ((bf16[8,24,1024]{2,1,0:T(8,128)(2,1)}), bf16[8,24,1024]{2,1,0:T(8,128)(2,1)S(1)}, u32[]{:S(2)}, u32[]{:S(2)}) async-start(bf16[8,24,1024]{2,1,0:T(8,128)(2,1)} %broadcast_in_dim.57), calls=%async_computation.13 | async-start | bytes 786432 | tf_op jit(solution)/shard_map/all_to_all | solution.py:21

commit v5 on v4

--- a/solution.py
+++ b/solution.py
@@ -45,7 +45,8 @@
     total = jnp.sum(everyone).astype(F32)
     fraction = gene_totals.astype(F32) / total
     test, fraction = lax.optimization_barrier((test_matrix.T, fraction))
-    test = spread(test, "z", Z).reshape(Z * test_matrix.shape[1], cols)
+    ready, held = lax.optimization_barrier((copies(test, Z), mine))
+    test = lax.all_to_all(ready, "z", 0, 0, tiled=True).reshape(Z * test_matrix.shape[1], cols)
 
     def resid(block):
         both = lax.all_gather(block, "core")
@@ -57,7 +58,7 @@
             / jnp.sqrt(expected + expected * expected / 100.0)
         ).astype(BF16)
 
-    stored = jnp.concatenate([resid(mine), resid(other)]).reshape(BLOCKS * rows, cols)
+    stored = jnp.concatenate([resid(held), resid(other)]).reshape(BLOCKS * rows, cols)
 
     def cell_side(panel, factor):
         part = lax.dot_general(

time: 219 us -> 213 us (0.973)
  waiting for transfers between devices: 37.5 us -> 13.6 us
  blocking collectives: 138 us -> 155 us
    all_to_all x3 -> x2, waiting for transfers between devices: 37.5 us -> 11 us  [spread(): return lax.all_to_all(copies(x, n), axis, 0, 0, tiled=True)]
    all_to_all x11, blocking collectives: 106 us -> 118 us  [spread(): return lax.all_to_all(copies(x, n), axis, 0, 0, tiled=True)]
    all_to_all x0 -> x1, starting transfers between devices: none -> 10 us  [shards(): lax.all_to_all(ready, 'z', 0, 0, tiled=True)]
    all_to_all x3 -> x2, starting transfers between devices: 18 us -> 11.4 us  [spread(): return lax.all_to_all(copies(x, n), axis, 0, 0, tiled=True)]
    ppermute x1, starting transfers between devices: 8.28 us -> 4.76 us  [shards(): other = lax.ppermute(mine, 'y_hi', [(0, 1), (1, 0)])]
    all_to_all x1, blocking collectives: 24.1 us -> 27.3 us  [shards(): got = lax.all_to_all(send, ('y_hi', 'core'), 0, 0, tiled=True)]
    all_to_all x0 -> x1, waiting for transfers between devices: none -> 2.62 us  [shards(): lax.all_to_all(ready, 'z', 0, 0, tiled=True)]
    all_gather x2, blocking collectives: 7.83 us -> 10.3 us  [resid(): both = lax.all_gather(block, 'core')]
  transfers between devices with their start and end apart: 4 -> 4, of which waited for: 3 -> 3; matrix products, arithmetic and copies ran while one was open for 1% -> 2% of each run, Pallas kernels for 0% -> 0%
where the time goes in v5:
time: 213 us; the launch traced here: 211 us
  blocking collectives  155 us (73%)
  starting transfers between devices  26.2 us (12%)
  waiting for transfers between devices  13.6 us (6%)
  local copies, waits for them, and re-layouts  5.12 us (2%)
  other arithmetic  4.85 us (2%)
  matrix products  4.17 us (2%)
    all_to_all x11, blocking collectives, spread(): return lax.all_to_all(copies(x, n), axis, 0, 0, tiled=True)  118 us
    all_to_all x1, blocking collectives, shards(): got = lax.all_to_all(send, ('y_hi', 'core'), 0, 0, tiled=True)  27.3 us
    all_to_all x2, starting transfers between devices, spread(): return lax.all_to_all(copies(x, n), axis, 0, 0, tiled=True)  11.4 us
    all_to_all x2, waiting for transfers between devices, spread(): return lax.all_to_all(copies(x, n), axis, 0, 0, tiled=True)  11 us
    all_gather x2, blocking collectives, resid(): both = lax.all_gather(block, 'core')  10.3 us
    all_to_all x1, starting transfers between devices, shards(): lax.all_to_all(ready, 'z', 0, 0, tiled=True)  10 us
    ppermute x1, starting transfers between devices, shards(): other = lax.ppermute(mine, 'y_hi', [(0, 1), (1, 0)])  4.76 us
  transfers between devices with their start and end apart: 4, of which 3 were waited for; matrix products, arithmetic and copies ran while one was open for 2% of the time, Pallas kernels for 0%

profile of v5, /device:TPU:1, one launch (start us, length us, event | category | flops | bytes accessed | tf_op | source)
XLA Modules:
  0.0 210.9 jit_solution(9138275798707611114)
XLA Ops:
  0.6 0.0 copy-start
  0.6 0.0 copy-start.1
  0.6 1.4 broadcast_in_dim.40
  2.1 8.0 %all-to-all-start = ((s32[16,1,1024]{2,1,0:T(1,128)}), s32[16,1,1024]{2,1,0:T(1,128)S(1)}, u32[]{:S(2)}, u32[]{:S(2)}) async-start(s32[16,1,1024]{2,1,0:T(1,128)} %broadcast_in_dim.40), calls=%async_computation | async-start | bytes 131072 | tf_op jit(solution)/shard_map/all_to_all | solution.py:21
  10.1 0.7 and_convert_fusion.2
  10.8 1.3 convert_element_type.403
  12.1 4.8 %collective-permute-start = (s16[264,1024]{1,0:T(8,128)(2,1)S(1)}, s16[264,1024]{1,0:T(8,128)(2,1)S(1)}, u32[]{:S(2)}, u32[]{:S(2)}) collective-permute-start(s16[264,1024]{1,0:T(8,128)(2,1)S(1)} %pad_add_fusion), channel_id=1, source_target_pairs={{0,256},{256,0},{1,257},{257,1},{2,258},{258,2},{3,259},{259,3},{4... | collective-permute-start | bytes 1622024 | tf_op jit(solution)/shard_map/ppermute | solution.py:43
  16.9 0.4 all-to-all-done
  17.3 0.8 reduce_sum.9
  18.7 0.0 copy-done
  18.8 0.6 broadcast_in_dim.41
  19.4 10.0 %all-to-all-start.1 = ((bf16[8,3,1024]{2,1,0:T(4,128)(2,1)}), bf16[8,3,1024]{2,1,0:T(4,128)(2,1)S(1)}, u32[]{:S(2)}, u32[]{:S(2)}) async-start(bf16[8,3,1024]{2,1,0:T(4,128)(2,1)} %broadcast_in_dim.41), calls=%async_computation.1 | async-start | bytes 131072 | tf_op jit(solution)/shard_map/all_to_all | solution.py:49
  29.4 4.6 %all-gather.5 = s16[528,1024]{1,0:T(8,128)(2,1)S(1)} all-gather(s16[264,1024]{1,0:T(8,128)(2,1)S(1)} %pad_add_fusion), channel_id=2, replica_groups=mesh['y_hi'=2,'z'=8,'core'=2,'y_lo'=4,'x'=4] {'core'}, dimensions={0}, use_global_device_ids=true | all-gather | bytes 1622016 | tf_op jit(solution)/shard_map/all_gather | solution.py:52
  34.0 2.6 %all-to-all-done.1 = bf16[8,3,1024]{2,1,0:T(4,128)(2,1)S(1)} async-done(((bf16[8,3,1024]{2,1,0:T(4,128)(2,1)}), bf16[8,3,1024]{2,1,0:T(4,128)(2,1)S(1)}, u32[]{:S(2)}, u32[]{:S(2)}) %all-to-all-start.1) | async-done | bytes 49184 | tf_op jit(solution)/shard_map/all_to_all | solution.py:49
  36.7 0.0 collective-permute-done
  36.7 5.7 %all-gather.4 = s16[528,1024]{1,0:T(8,128)(2,1)S(1)} all-gather(s16[264,1024]{1,0:T(8,128)(2,1)S(1)} %collective-permute-done), channel_id=3, replica_groups=mesh['y_hi'=2,'z'=8,'core'=2,'y_lo'=4,'x'=4] {'core'}, dimensions={0}, use_global_device_ids=true | all-gather | bytes 1622016 | tf_op jit(solution)/shard_map/all_gather | solution.py:52
  42.5 1.6 fusion.1
  44.1 0.2 pad_maximum_fusion
  44.3 0.7 convolution_convert_fusion.7
  45.0 8.2 %all_to_all.76 = bf16[4,24,1024]{2,1,0:T(8,128)(2,1)S(1)} all-to-all(bf16[4,24,1024]{2,1,0:T(8,128)(2,1)S(1)} %broadcast_in_dim.42), channel_id=1, replica_groups=mesh['y_hi'=2,'z'=8,'core'=2,'y_lo'=4,'x'=4] {'x'}, dimensions={0} | all-to-all | bytes 393216 | tf_op jit(solution)/shard_map/all_to_all | solution.py:21
  53.3 14.7 %all_to_all.77 = bf16[4,24,1024]{2,1,0:T(8,128)(2,1)S(1)} all-to-all(bf16[4,24,1024]{2,1,0:T(8,128)(2,1)S(1)} %broadcast_in_dim.44), channel_id=1, replica_groups=mesh['y_hi'=2,'z'=8,'core'=2,'y_lo'=4,'x'=4] {'y_lo'}, dimensions={0} | all-to-all | bytes 393216 | tf_op jit(solution)/shard_map/all_to_all | solution.py:21
  68.0 0.4 convolution_convert_fusion.6
  68.4 20.9 %all_to_all.78 = bf16[8,24,1024]{2,1,0:T(8,128)(2,1)S(1)} all-to-all(bf16[8,24,1024]{2,1,0:T(8,128)(2,1)S(1)} %broadcast_in_dim.45), channel_id=1, replica_groups=mesh['y_hi'=2,'z'=8,'core'=2,'y_lo'=4,'x'=4] {'z'}, dimensions={0} | all-to-all | bytes 786432 | tf_op jit(solution)/shard_map/all_to_all | solution.py:21
  89.4 0.7 convolution_convert_fusion.5
  90.1 7.5 %all_to_all.79 = bf16[4,24,1024]{2,1,0:T(8,128)(2,1)S(1)} all-to-all(bf16[4,24,1024]{2,1,0:T(8,128)(2,1)S(1)} %broadcast_in_dim.46), channel_id=1, replica_groups=mesh['y_hi'=2,'z'=8,'core'=2,'y_lo'=4,'x'=4] {'x'}, dimensions={0} | all-to-all | bytes 393216 | tf_op jit(solution)/shard_map/all_to_all | solution.py:21
  97.7 8.0 %all_to_all.80 = bf16[4,24,1024]{2,1,0:T(8,128)(2,1)S(1)} all-to-all(bf16[4,24,1024]{2,1,0:T(8,128)(2,1)S(1)} %broadcast_in_dim.48), channel_id=1, replica_groups=mesh['y_hi'=2,'z'=8,'core'=2,'y_lo'=4,'x'=4] {'y_lo'}, dimensions={0} | all-to-all | bytes 393216 | tf_op jit(solution)/shard_map/all_to_all | solution.py:21
  105.7 0.4 convolution_convert_fusion.4
  106.1 13.5 %all_to_all.81 = bf16[8,24,1024]{2,1,0:T(8,128)(2,1)S(1)} all-to-all(bf16[8,24,1024]{2,1,0:T(8,128)(2,1)S(1)} %broadcast_in_dim.49), channel_id=1, replica_groups=mesh['y_hi'=2,'z'=8,'core'=2,'y_lo'=4,'x'=4] {'z'}, dimensions={0} | all-to-all | bytes 786432 | tf_op jit(solution)/shard_map/all_to_all | solution.py:21
  119.6 0.7 convolution_convert_fusion.3
  120.3 7.5 %all_to_all.82 = bf16[4,24,1024]{2,1,0:T(8,128)(2,1)S(1)} all-to-all(bf16[4,24,1024]{2,1,0:T(8,128)(2,1)S(1)} %broadcast_in_dim.50), channel_id=1, replica_groups=mesh['y_hi'=2,'z'=8,'core'=2,'y_lo'=4,'x'=4] {'x'}, dimensions={0} | all-to-all | bytes 393216 | tf_op jit(solution)/shard_map/all_to_all | solution.py:21
  127.9 8.2 %all_to_all.83 = bf16[4,24,1024]{2,1,0:T(8,128)(2,1)S(1)} all-to-all(bf16[4,24,1024]{2,1,0:T(8,128)(2,1)S(1)} %broadcast_in_dim.52), channel_id=1, replica_groups=mesh['y_hi'=2,'z'=8,'core'=2,'y_lo'=4,'x'=4] {'y_lo'}, dimensions={0} | all-to-all | bytes 393216 | tf_op jit(solution)/shard_map/all_to_all | solution.py:21
  136.1 0.4 convolution_convert_fusion.2
  136.5 13.1 %all_to_all.84 = bf16[8,24,1024]{2,1,0:T(8,128)(2,1)S(1)} all-to-all(bf16[8,24,1024]{2,1,0:T(8,128)(2,1)S(1)} %broadcast_in_dim.53), channel_id=1, replica_groups=mesh['y_hi'=2,'z'=8,'core'=2,'y_lo'=4,'x'=4] {'z'}, dimensions={0} | all-to-all | bytes 786432 | tf_op jit(solution)/shard_map/all_to_all | solution.py:21
  149.7 0.7 convolution_convert_fusion.1
  150.3 7.8 %all_to_all.85 = bf16[4,24,1024]{2,1,0:T(8,128)(2,1)S(1)} all-to-all(bf16[4,24,1024]{2,1,0:T(8,128)(2,1)S(1)} %broadcast_in_dim.54), channel_id=1, replica_groups=mesh['y_hi'=2,'z'=8,'core'=2,'y_lo'=4,'x'=4] {'x'}, dimensions={0} | all-to-all | bytes 393216 | tf_op jit(solution)/shard_map/all_to_all | solution.py:21
  158.2 8.0 %all_to_all.86 = bf16[4,24,1024]{2,1,0:T(8,128)(2,1)S(1)} all-to-all(bf16[4,24,1024]{2,1,0:T(8,128)(2,1)S(1)} %broadcast_in_dim.56), channel_id=1, replica_groups=mesh['y_hi'=2,'z'=8,'core'=2,'y_lo'=4,'x'=4] {'y_lo'}, dimensions={0} | all-to-all | bytes 393216 | tf_op jit(solution)/shard_map/all_to_all | solution.py:21
  166.3 0.4 convolution_convert_fusion
  166.7 0.8 broadcast_in_dim.57
  167.5 3.5 %all-to-all-start.13 = ((bf16[8,24,1024]{2,1,0:T(8,128)(2,1)}), bf16[8,24,1024]{2,1,0:T(8,128)(2,1)S(1)}, u32[]{:S(2)}, u32[]{:S(2)}) async-start(bf16[8,24,1024]{2,1,0:T(8,128)(2,1)} %broadcast_in_dim.57), calls=%async_computation.13 | async-start | bytes 786432 | tf_op jit(solution)/shard_map/all_to_all | solution.py:21
  171.0 10.6 %all-to-all-done.13 = bf16[8,24,1024]{2,1,0:T(8,128)(2,1)S(1)} async-done(((bf16[8,24,1024]{2,1,0:T(8,128)(2,1)}), bf16[8,24,1024]{2,1,0:T(8,128)(2,1)S(1)}, u32[]{:S(2)}, u32[]{:S(2)}) %all-to-all-start.13) | async-done | bytes 393248 | tf_op jit(solution)/shard_map/all_to_all | solution.py:21
  181.6 0.1 fusion.24
  181.7 27.3 %all_to_all.87 = bf16[4,24,1280]{2,1,0:T(8,128)(2,1)S(1)} all-to-all(bf16[4,24,1280]{2,1,0:T(8,128)(2,1)S(1)} %pad_maximum_fusion.1), channel_id=1, replica_groups=mesh['y_hi'=2,'z'=8,'core'=2,'y_lo'=4,'x'=4] {'y_hi','core'}, dimensions={0} | all-to-all | bytes 491520 | tf_op jit(solution)/shard_map/all_to_all | solution.py:84
  209.0 0.1 copy.19
  209.1 0.1 reshape.136
  209.2 0.1 copy.20
  209.4 0.2 reshape.137
  209.6 0.6 slice_bitcast_fusion.1
  210.2 0.7 slice_bitcast_fusion
  (35 shorter events, 0.7 us)
Async XLA Ops:
  0.6 18.1 %copy-start = (s32[1024]{0:T(1024)S(1)}, s32[1024]{0:T(1024)}, u32[]{:S(2)}) copy-start(s32[1024]{0:T(1024)} %param.8) | copy-start | bytes 12292
  0.6 18.1 %copy-start.1 = (bf16[1024,3]{0,1:T(4,128)(2,1)S(1)}, bf16[1024,3]{0,1:T(4,128)(2,1)}, u32[]{:S(2)}) copy-start(bf16[1024,3]{0,1:T(4,128)(2,1)} %param.9) | copy-start | bytes 18436
  2.1 15.3 %all-to-all-start = ((s32[16,1,1024]{2,1,0:T(1,128)}), s32[16,1,1024]{2,1,0:T(1,128)S(1)}, u32[]{:S(2)}, u32[]{:S(2)}) async-start(s32[16,1,1024]{2,1,0:T(1,128)} %broadcast_in_dim.40), calls=%async_computation | async-start | bytes 131072 | tf_op jit(solution)/shard_map/all_to_all | solution.py:21
  12.1 24.6 %collective-permute-start = (s16[264,1024]{1,0:T(8,128)(2,1)S(1)}, s16[264,1024]{1,0:T(8,128)(2,1)S(1)}, u32[]{:S(2)}, u32[]{:S(2)}) collective-permute-start(s16[264,1024]{1,0:T(8,128)(2,1)S(1)} %pad_add_fusion), channel_id=1, source_target_pairs={{0,256},{256,0},{1,257},{257,1},{2,258},{258,2},{3,259},{259,3},{4... | collective-permute-start | bytes 1622024 | tf_op jit(solution)/shard_map/ppermute | solution.py:43
  19.4 17.3 %all-to-all-start.1 = ((bf16[8,3,1024]{2,1,0:T(4,128)(2,1)}), bf16[8,3,1024]{2,1,0:T(4,128)(2,1)S(1)}, u32[]{:S(2)}, u32[]{:S(2)}) async-start(bf16[8,3,1024]{2,1,0:T(4,128)(2,1)} %broadcast_in_dim.41), calls=%async_computation.1 | async-start | bytes 131072 | tf_op jit(solution)/shard_map/all_to_all | solution.py:49
  167.5 14.1 %all-to-all-start.13 = ((bf16[8,24,1024]{2,1,0:T(8,128)(2,1)}), bf16[8,24,1024]{2,1,0:T(8,128)(2,1)S(1)}, u32[]{:S(2)}, u32[]{:S(2)}) async-start(bf16[8,24,1024]{2,1,0:T(8,128)(2,1)} %broadcast_in_dim.57), calls=%async_computation.13 | async-start | bytes 786432 | tf_op jit(solution)/shard_map/all_to_all | solution.py:21

commit v6 on v3

--- a/solution.py
+++ b/solution.py
@@ -21,14 +21,19 @@
     return lax.all_to_all(copies(x, n), axis, 0, 0, tiled=True)
 
 
-def gather_sum(x, axis, n, factor=None):
-    got = spread(x, axis, n)
+def total_of(got, factor=None):
     total = got[0].astype(F32)
-    for i in range(1, n):
+    for i in range(1, got.shape[0]):
         total = total + got[i].astype(F32)
     if factor is not None:
         total = total * factor
     return total.astype(BF16)
+
+
+def gather_sum(x, axis, n, factor=None):
+    shape = x.shape
+    got = spread(x.reshape(-1, 4, shape[1]) if shape[0] % 8 else x, axis, n)
+    return total_of(got, factor).reshape(shape)
 
 
 def shards(counts, cell_totals, gene_totals, test_matrix):
@@ -36,15 +41,12 @@
     scale = 1.0 / math.sqrt(rows * Y_HI * Z * CORE + cols * Y_LO * X)
     x_hi = lax.axis_index("x_hi")
 
-    totals = spread(gene_totals, ("y_lo", "x_hi", "x_lo"), Y_LO * X)
-    total = jnp.sum(totals).astype(F32)
-    fraction = gene_totals.astype(F32) / total
-    place = lax.axis_index(("y_lo", "x_hi", "x_lo"))
-    beside = lax.dynamic_index_in_dim(totals, place ^ 3, 0, keepdims=False).astype(F32) / total
-
     pieces = jnp.stack([cell_totals >> shift & 2047 for shift in (0, 11, 22)])
     extra = jnp.zeros((EXTRA, cols), I16).at[:3, :rows].set(pieces.astype(I16))
     mine = jnp.concatenate([counts.astype(I16), extra])
+
+    def both(block):
+        return lax.all_gather(block, "core")
 
     def over_y(block):
         return lax.ppermute(block, "y_hi", [(0, 1), (1, 0)])
@@ -52,8 +54,7 @@
     def over_x(block):
         return lax.ppermute(block, ("x_hi", "x_lo"), [(i, 3 - i) for i in range(X)])
 
-    def resid(block, fraction):
-        both = lax.all_gather(block, "core")
+    def resid(both, fraction):
         pieces = both[:, rows : rows + 3, :rows].astype(jnp.int32)
         owned = (pieces[:, 0] + (pieces[:, 1] << 11) + (pieces[:, 2] << 22)).astype(F32)
         expected = owned[:, :, None] * fraction[None, None, :]
@@ -62,33 +63,49 @@
             / jnp.sqrt(expected + expected * expected / 100.0)
         ).astype(BF16)
 
-    other = over_y(mine)
+    cut = rows // 2
+    other = [over_y(mine[:cut]), over_y(mine[cut:])]
     near = over_x(mine)
-    test = spread(test_matrix.T, "z", Z).reshape(Z * test_matrix.shape[1], cols)
-    far = over_x(other)
+    ready, first = lax.optimization_barrier((copies(gene_totals, Y_LO * X), other[0]))
+    totals = lax.all_to_all(ready, ("y_lo", "x_hi", "x_lo"), 0, 0, tiled=True)
+    total = jnp.sum(totals).astype(F32)
+    fraction = gene_totals.astype(F32) / total
+    place = lax.axis_index(("y_lo", "x_hi", "x_lo"))
+    beside = lax.dynamic_index_in_dim(totals, place ^ 3, 0, keepdims=False).astype(F32) / total
+    ready, held = lax.optimization_barrier((copies(test_matrix.T, Z), mine))
+    test = lax.all_to_all(ready, "z", 0, 0, tiled=True).reshape(Z * test_matrix.shape[1], cols)
+    near = both(near)
+    near, last = lax.optimization_barrier((near, other[1]))
+    other = [first, last]
+    far = [over_x(chunk) for chunk in other]
 
     cells = BLOCKS * rows
-    own = jnp.concatenate([resid(mine, fraction), resid(other, fraction)]).reshape(cells, cols)
+    own = [resid(both(held), fraction), resid(both(jnp.concatenate(other)), fraction)]
+    own = jnp.concatenate(own).reshape(cells, cols)
 
     def cell_part(panel, stored):
         return lax.dot_general(
             panel, stored, (((1,), (1,)), ((), ())), preferred_element_type=F32
-        ).astype(BF16)
+        )
 
-    part = gather_sum(cell_part(test, own), ("x_hi", "x_lo"), X)
+    ready, far = lax.optimization_barrier((copies(cell_part(test, own).astype(BF16), X), far))
+    part = total_of(lax.all_to_all(ready, ("x_hi", "x_lo"), 0, 0, tiled=True))
     width = part.shape[0] // 2
     part = jnp.where(x_hi == 0, part[:width], part[width:])
     sketch = gather_sum(part, "y_lo", Y_LO)
 
-    paired = jnp.concatenate([resid(near, beside), resid(far, beside)]).reshape(cells, cols)
-    stored = jnp.concatenate([own, paired], axis=1)
+    paired = [resid(near, beside), resid(both(jnp.concatenate(far)), beside)]
+    paired = jnp.concatenate(paired).reshape(cells, cols)
 
     def gene_side(sketch):
-        part = jnp.dot(sketch, stored, preferred_element_type=F32).astype(BF16)
-        return gather_sum(part, "z", Z, scale)
+        part = jnp.concatenate(
+            [jnp.dot(sketch, stored, preferred_element_type=F32) for stored in (own, paired)], axis=1
+        )
+        return gather_sum(part.astype(BF16), "z", Z, scale)
 
     def cell_side(panel):
-        return gather_sum(cell_part(panel, stored), ("y_lo", "x_lo"), Y_LO * X_LO, scale)
+        part = cell_part(panel[:, :cols], own) + cell_part(panel[:, cols:], paired)
+        return gather_sum(part.astype(BF16), ("y_lo", "x_lo"), Y_LO * X_LO, scale)
 
     for step in range(ITERS):
         sketch = cell_side(gene_side(sketch))

time: 227 us -> 225 us (level)
  waiting for transfers between devices: 31.4 us -> 18.4 us
  blocking collectives: 127 us -> 120 us
  local copies, waits for them, and re-layouts: 6.28 us -> 11.7 us
  starting transfers between devices: 40.9 us -> 46.3 us
  other arithmetic: 8.04 us -> 12.8 us
  matrix products: 8.58 us -> 12.6 us
    all_to_all x0 -> x3, starting transfers between devices: none -> 17.6 us  [the longest x1 10 us: shards(): lax.all_to_all(ready, 'z', 0, 0, tiled=True)]
    all_to_all x5 -> x2, starting transfers between devices: 23.7 us -> 6.76 us  [spread(): return lax.all_to_all(copies(x, n), axis, 0, 0, tiled=True)]
    all_to_all x6, blocking collectives: 89.9 us -> 76.5 us  [spread(): return lax.all_to_all(copies(x, n), axis, 0, 0, tiled=True)]
    all_to_all x5 -> x2, waiting for transfers between devices: 23 us -> 12.3 us  [spread(): return lax.all_to_all(copies(x, n), axis, 0, 0, tiled=True)]
    all_to_all x1, blocking collectives: 21.3 us -> 27.5 us  [shards(): lax.all_to_all(send, ('y_hi', 'core', 'x_hi', 'x_lo'), 0, 0, axis_index_g...]
    ppermute x2 -> x3, waiting for transfers between devices: 8.4 us -> 2.69 us  [over_x(): return lax.ppermute(block, ('x_hi', 'x_lo'), [(i, 3 - i) for i in range(X)])]
    unnamed x10 -> x20, local copies, waits for them, and re-layouts: 0.03 us -> 4.76 us
    concatenate x2 -> x8, other arithmetic: 1.7 us -> 5.4 us  [the longest x1 3.05 us: shards(): paired = jnp.concatenate(paired).reshape(cells, cols)]
  transfers between devices with their start and end apart: 8 -> 10, of which waited for: 5 -> 5; matrix products, arithmetic and copies ran while one was open for 3% -> 5% of each run, Pallas kernels for 0% -> 0%
where the time goes in v6:
time: 225 us; the launch traced here: 223 us
  blocking collectives  120 us (53%)
  starting transfers between devices  46.3 us (21%)
  waiting for transfers between devices  18.4 us (8%)
  other arithmetic  12.8 us (6%)
  matrix products  12.6 us (6%)
  local copies, waits for them, and re-layouts  11.7 us (5%)
    all_to_all x6, blocking collectives, spread(): return lax.all_to_all(copies(x, n), axis, 0, 0, tiled=True)  76.5 us
    all_to_all x1, blocking collectives, shards(): lax.all_to_all(send, ('y_hi', 'core', 'x_hi', 'x_lo'), 0, 0, axis_index_g...  27.5 us
    all_gather x4, blocking collectives, both(): return lax.all_gather(block, 'core')  15.6 us
    all_to_all x2, waiting for transfers between devices, spread(): return lax.all_to_all(copies(x, n), axis, 0, 0, tiled=True)  12.3 us
    ppermute x3, starting transfers between devices, over_x(): return lax.ppermute(block, ('x_hi', 'x_lo'), [(i, 3 - i) for i in range(X)])  11.8 us
    ppermute x2, starting transfers between devices, over_y(): return lax.ppermute(block, 'y_hi', [(0, 1), (1, 0)])  10.2 us
    all_to_all x1, starting transfers between devices, shards(): lax.all_to_all(ready, 'z', 0, 0, tiled=True)  10 us
    dot_general x8, matrix products, gene_side(): jnp.dot(sketch, stored, preferred_element_type=F32)  8.06 us
  transfers between devices with their start and end apart: 10, of which 5 were waited for; matrix products, arithmetic and copies ran while one was open for 5% of the time, Pallas kernels for 0%

profile of v6, /device:TPU:1, one launch (start us, length us, event | category | flops | bytes accessed | tf_op | source)
XLA Modules:
  0.0 223.2 jit_solution(17331403947421895714)
XLA Ops:
  0.6 1.3 convert_element_type.574
  2.0 8.3 %collective-permute-start = (s16[128,1024]{1,0:T(8,128)(2,1)S(1)}, s16[128,1024]{1,0:T(8,128)(2,1)}, u32[]{:S(2)}, u32[]{:S(2)}) collective-permute-start(s16[128,1024]{1,0:T(8,128)(2,1)S(1)} %slice.417), channel_id=1, source_target_pairs={{0,256},{256,0},{1,257},{257,1},{2,258},{258,2},{3,259},{259,3},{4... | collective-permute-start | bytes 786440 | tf_op jit(solution)/shard_map/ppermute | solution.py:52
  10.4 4.4 %collective-permute-start.1 = (s16[264,1024]{1,0:T(8,128)(2,1)S(1)}, s16[264,1024]{1,0:T(8,128)(2,1)}, u32[]{:S(2)}, u32[]{:S(2)}) collective-permute-start(s16[264,1024]{1,0:T(8,128)(2,1)S(1)} %pad_add_fusion), channel_id=1, source_target_pairs={{0,3},{1,2},{2,1},{3,0},{4,7},{5,6},{6,5},{7,4},{8,11},{9,10},{10,... | collective-permute-start | bytes 1622024 | tf_op jit(solution)/shard_map/ppermute | solution.py:55
  15.5 10.0 %all-to-all-start = ((bf16[8,3,1024]{2,1,0:T(4,128)(2,1)}), bf16[8,3,1024]{2,1,0:T(4,128)(2,1)S(1)}, u32[]{:S(2)}, u32[]{:S(2)}) async-start(bf16[8,3,1024]{2,1,0:T(4,128)(2,1)} %broadcast_in_dim.34), calls=%async_computation | async-start | bytes 131072 | tf_op jit(solution)/shard_map/all_to_all | solution.py:76
  25.5 1.9 collective-permute-start.2
  27.5 3.8 %all-gather.10 = s16[528,1024]{1,0:T(8,128)(2,1)S(1)} all-gather(s16[264,1024]{1,0:T(8,128)(2,1)S(1)} %pad_add_fusion), channel_id=2, replica_groups=mesh['y_hi'=2,'z'=8,'core'=2,'y_lo'=4,'x_hi'=2,'x_lo'=2] {'core'}, dimensions={0}, use_global_device_ids=true | all-gather | bytes 1622016 | tf_op jit(solution)/shard_map/all_gather | solution.py:49
  31.3 0.7 all_to_all.40
  32.0 0.7 all-to-all-done
  32.7 4.2 %all-to-all-start.1 = ((s32[16,1,1024]{2,1,0:T(1,128)}), s32[16,1,1024]{2,1,0:T(1,128)S(1)}, u32[]{:S(2)}, u32[]{:S(2)}) async-start(s32[16,1,1024]{2,1,0:T(1,128)} %all_to_all.40), calls=%async_computation.1 | async-start | bytes 131072 | tf_op jit(solution)/shard_map/all_to_all | solution.py:70
  37.0 4.5 %collective-permute-start.3 = (s16[128,1024]{1,0:T(8,128)(2,1)}, s16[128,1024]{1,0:T(8,128)(2,1)}, u32[]{:S(2)}, u32[]{:S(2)}) collective-permute-start(s16[128,1024]{1,0:T(8,128)(2,1)} %collective-permute-done), channel_id=1, source_target_pairs={{0,3},{1,2},{2,1},{3,0},{4,7},{5,6},{6,5},{7,4},{8,11},{9,10},{10,... | collective-permute-start | bytes 786440 | tf_op jit(solution)/shard_map/ppermute | solution.py:55
  41.5 2.7 %all-to-all-done.1 = s32[16,1,1024]{2,1,0:T(1,128)S(1)} async-done(((s32[16,1,1024]{2,1,0:T(1,128)}), s32[16,1,1024]{2,1,0:T(1,128)S(1)}, u32[]{:S(2)}, u32[]{:S(2)}) %all-to-all-start.1) | async-done | bytes 65568 | tf_op jit(solution)/shard_map/all_to_all | solution.py:70
  44.2 0.8 reduce_sum.9
  45.7 5.5 %all-gather.8 = s16[528,1024]{1,0:T(8,128)(2,1)S(1)} all-gather(s16[264,1024]{1,0:T(8,128)(2,1)} %collective-permute-done.1), channel_id=3, replica_groups=mesh['y_hi'=2,'z'=8,'core'=2,'y_lo'=4,'x_hi'=2,'x_lo'=2] {'core'}, dimensions={0}, use_global_device_ids=true | all-gather | bytes 1622016 | tf_op jit(solution)/shard_map/all_gather | solution.py:49
  51.2 1.0 pad_add_fusion.1
  52.1 2.9 %collective-permute-start.4 = (s16[136,1024]{1,0:T(8,128)(2,1)S(1)}, s16[136,1024]{1,0:T(8,128)(2,1)S(1)}, u32[]{:S(2)}, u32[]{:S(2)}) collective-permute-start(s16[136,1024]{1,0:T(8,128)(2,1)S(1)} %collective-permute-done.2), channel_id=1, source_target_pairs={{0,3},{1,2},{2,1},{3,0},{4,7},{5,6},{6,5},{7,4},{8,11},{9,10},{10,... | collective-permute-start | bytes 835592 | tf_op jit(solution)/shard_map/ppermute | solution.py:55
  55.1 2.9 %all-gather.9 = s16[528,1024]{1,0:T(8,128)(2,1)S(1)} all-gather(s16[264,1024]{1,0:T(8,128)(2,1)S(1)} %pad_add_fusion.1), channel_id=4, replica_groups=mesh['y_hi'=2,'z'=8,'core'=2,'y_lo'=4,'x_hi'=2,'x_lo'=2] {'core'}, dimensions={0}, use_global_device_ids=true | all-gather | bytes 1622016 | tf_op jit(solution)/shard_map/all_gather | solution.py:49
  58.0 1.6 fusion.1
  59.8 0.7 convolution_convert_fusion
  60.4 2.7 %collective-permute-done.4 = s16[136,1024]{1,0:T(8,128)(2,1)S(1)} collective-permute-done((s16[136,1024]{1,0:T(8,128)(2,1)S(1)}, s16[136,1024]{1,0:T(8,128)(2,1)S(1)}, u32[]{:S(2)}, u32[]{:S(2)}) %collective-permute-start.4) | collective-permute-done | bytes 278560 | tf_op jit(solution)/shard_map/ppermute | solution.py:55
  63.1 0.7 copy-done.4
  63.8 0.7 broadcast_in_dim.36
  64.5 3.4 %all-to-all-start.2 = ((bf16[4,24,1024]{2,1,0:T(8,128)(2,1)}), bf16[4,24,1024]{2,1,0:T(8,128)(2,1)S(1)}, u32[]{:S(2)}, u32[]{:S(2)}) async-start(bf16[4,24,1024]{2,1,0:T(8,128)(2,1)} %broadcast_in_dim.36), calls=%async_computation.2 | async-start | bytes 393216 | tf_op jit(solution)/shard_map/all_to_all | solution.py:92
  67.9 1.1 pad_add_fusion.2
  69.0 3.4 %all-gather.11 = s16[528,1024]{1,0:T(8,128)(2,1)S(1)} all-gather(s16[264,1024]{1,0:T(8,128)(2,1)S(1)} %pad_add_fusion.2), channel_id=5, replica_groups=mesh['y_hi'=2,'z'=8,'core'=2,'y_lo'=4,'x_hi'=2,'x_lo'=2] {'core'}, dimensions={0}, use_global_device_ids=true | all-gather | bytes 1622016 | tf_op jit(solution)/shard_map/all_gather | solution.py:49
  72.4 2.9 %fusion.9 = (bf16[2,256,1024]{2,1,0:T(8,128)(2,1)}, bf16[2,256,1024]{2,1,0:T(8,128)(2,1)}) fusion(f32[1024]{0:T(1024)S(1)} %bitcast.96, f32[2,256]{1,0:T(2,128)S(1)} %bitcast.98, s16[2,264,1024]{2,1,0:T(8,128)(2,1)S(1)} %bitcast.89, f32[2,256]{1,0:T(2,128)S(1)} %bitcast.100, s16[2,264,1024]{2,1,0:T(8,128)(2,1)S(1)} %bitcast.93), kind=kLoop, calls=%fused_computation.21 | loop fusion | flops 8388608 | bytes 4202496 | tf_op jit(solution)/shard_map/convert_element_type | solution.py:64
  75.4 0.7 broadcast_in_dim.38
  76.1 3.3 %all-to-all-start.3 = ((bf16[4,3,4,1024]{3,2,1,0:T(4,128)(2,1)}), bf16[4,3,4,1024]{3,2,1,0:T(4,128)(2,1)S(1)}, u32[]{:S(2)}, u32[]{:S(2)}) async-start(bf16[4,3,4,1024]{3,2,1,0:T(4,128)(2,1)} %broadcast_in_dim.38), calls=%async_computation.3 | async-start | bytes 196608 | tf_op jit(solution)/shard_map/all_to_all | solution.py:21
  79.4 3.0 %pad_maximum_fusion.1 = bf16[4,256,1024]{2,1,0:T(8,128)(2,1)} fusion(bf16[2,256,1024]{2,1,0:T(8,128)(2,1)} %get-tuple-element.33, bf16[2,256,1024]{2,1,0:T(8,128)(2,1)} %get-tuple-element.32), kind=kLoop, calls=%fused_computation.29 | loop fusion | flops 1048576 | bytes 4194304 | tf_op jit(solution)/shard_map/concatenate | solution.py:98
  82.4 1.7 all-to-all-done.3
  84.5 1.2 copy-done
  86.3 18.3 %all_to_all.64 = bf16[8,3,4,2048]{3,2,1,0:T(4,128)(2,1)S(1)} all-to-all(bf16[8,3,4,2048]{3,2,1,0:T(4,128)(2,1)S(1)} %broadcast_in_dim.39), channel_id=1, replica_groups=mesh['y_hi'=2,'z'=8,'core'=2,'y_lo'=4,'x_hi'=2,'x_lo'=2] {'z'}, dimensions={0} | all-to-all | bytes 786432 | tf_op jit(solution)/shard_map/all_to_all | solution.py:21
  105.4 0.9 copy-done.1
  106.4 0.6 fusion.16
  107.1 12.0 %all_to_all.65 = bf16[8,3,4,1024]{3,2,1,0:T(4,128)(2,1)S(1)} all-to-all(bf16[8,3,4,1024]{3,2,1,0:T(4,128)(2,1)S(1)} %broadcast_in_dim.41), channel_id=1, replica_groups=mesh['y_hi'=2,'z'=8,'core'=2,'y_lo'=4,'x_hi'=2,'x_lo'=2] {'y_lo','x_lo'}, dimensions={0} | all-to-all | bytes 393216 | tf_op jit(solution)/shard_map/all_to_all | solution.py:21
  119.1 2.0 convolution_convert_fusion.5
  121.7 13.0 %all_to_all.66 = bf16[8,3,4,2048]{3,2,1,0:T(4,128)(2,1)S(1)} all-to-all(bf16[8,3,4,2048]{3,2,1,0:T(4,128)(2,1)S(1)} %broadcast_in_dim.42), channel_id=1, replica_groups=mesh['y_hi'=2,'z'=8,'core'=2,'y_lo'=4,'x_hi'=2,'x_lo'=2] {'z'}, dimensions={0} | all-to-all | bytes 786432 | tf_op jit(solution)/shard_map/all_to_all | solution.py:21
  135.5 0.9 copy-done.2
  137.2 10.3 %all_to_all.67 = bf16[8,3,4,1024]{3,2,1,0:T(4,128)(2,1)S(1)} all-to-all(bf16[8,3,4,1024]{3,2,1,0:T(4,128)(2,1)S(1)} %broadcast_in_dim.44), channel_id=1, replica_groups=mesh['y_hi'=2,'z'=8,'core'=2,'y_lo'=4,'x_hi'=2,'x_lo'=2] {'y_lo','x_lo'}, dimensions={0} | all-to-all | bytes 393216 | tf_op jit(solution)/shard_map/all_to_all | solution.py:21
  147.6 2.0 convolution_convert_fusion.3
  150.2 13.8 %all_to_all.68 = bf16[8,3,4,2048]{3,2,1,0:T(4,128)(2,1)S(1)} all-to-all(bf16[8,3,4,2048]{3,2,1,0:T(4,128)(2,1)S(1)} %broadcast_in_dim.45), channel_id=1, replica_groups=mesh['y_hi'=2,'z'=8,'core'=2,'y_lo'=4,'x_hi'=2,'x_lo'=2] {'z'}, dimensions={0} | all-to-all | bytes 786432 | tf_op jit(solution)/shard_map/all_to_all | solution.py:21
  164.8 0.9 copy-done.3
  166.5 9.0 %all_to_all.69 = bf16[8,3,4,1024]{3,2,1,0:T(4,128)(2,1)S(1)} all-to-all(bf16[8,3,4,1024]{3,2,1,0:T(4,128)(2,1)S(1)} %broadcast_in_dim.47), channel_id=1, replica_groups=mesh['y_hi'=2,'z'=8,'core'=2,'y_lo'=4,'x_hi'=2,'x_lo'=2] {'y_lo','x_lo'}, dimensions={0} | all-to-all | bytes 393216 | tf_op jit(solution)/shard_map/all_to_all | solution.py:21
  175.6 2.0 convolution_convert_fusion.1
  178.0 0.9 broadcast_in_dim.49
  179.0 3.5 %all-to-all-start.10 = ((bf16[8,3,4,2048]{3,2,1,0:T(4,128)(2,1)}), bf16[8,3,4,2048]{3,2,1,0:T(4,128)(2,1)S(1)}, u32[]{:S(2)}, u32[]{:S(2)}) async-start(bf16[8,3,4,2048]{3,2,1,0:T(4,128)(2,1)} %broadcast_in_dim.49), calls=%async_computation.10 | async-start | bytes 786432 | tf_op jit(solution)/shard_map/all_to_all | solution.py:21
  182.5 10.6 %all-to-all-done.10 = bf16[8,3,4,2048]{3,2,1,0:T(4,128)(2,1)S(1)} async-done(((bf16[8,3,4,2048]{3,2,1,0:T(4,128)(2,1)}), bf16[8,3,4,2048]{3,2,1,0:T(4,128)(2,1)S(1)}, u32[]{:S(2)}, u32[]{:S(2)}) %all-to-all-start.10) | async-done | bytes 393248 | tf_op jit(solution)/shard_map/all_to_all | solution.py:21
  193.8 27.5 %all_to_all.70 = bf16[8,12,1280]{2,1,0:T(8,128)(2,1)S(1)} all-to-all(bf16[8,12,1280]{2,1,0:T(8,128)(2,1)S(1)} %bitcast.94), channel_id=1, replica_groups={{0,3,16,19,256,259,272,275},{1,2,17,18,257,258,273,274},{4,7,20,23,260,..., dimensions={0} | all-to-all | bytes 491520 | tf_op jit(solution)/shard_map/all_to_all | solution.py:126
  222.5 0.7 slice_bitcast_fusion
  (91 shorter events, 9.7 us)
Async XLA Ops:
  0.6 9.7 %copy-start.7 = (s32[256]{0:T(256)S(1)}, s32[256]{0:T(256)}, u32[]{:S(2)}) copy-start(s32[256]{0:T(256)} %param.7) | copy-start | bytes 3076
  0.6 14.2 %copy-start.6 = (bf16[1024,3]{0,1:T(4,128)(2,1)S(1)}, bf16[1024,3]{0,1:T(4,128)(2,1)}, u32[]{:S(2)}) copy-start(bf16[1024,3]{0,1:T(4,128)(2,1)} %param.9) | copy-start | bytes 18436
  2.0 29.3 %copy-start.5 = (s32[1024]{0:T(1024)S(1)}, s32[1024]{0:T(1024)}, u32[]{:S(2)}) copy-start(s32[1024]{0:T(1024)} %param.8) | copy-start | bytes 12292
  2.0 29.3 %collective-permute-start = (s16[128,1024]{1,0:T(8,128)(2,1)S(1)}, s16[128,1024]{1,0:T(8,128)(2,1)}, u32[]{:S(2)}, u32[]{:S(2)}) collective-permute-start(s16[128,1024]{1,0:T(8,128)(2,1)S(1)} %slice.417), channel_id=1, source_target_pairs={{0,256},{256,0},{1,257},{257,1},{2,258},{258,2},{3,259},{259,3},{4... | collective-permute-start | bytes 786440 | tf_op jit(solution)/shard_map/ppermute | solution.py:52
  10.4 35.2 %collective-permute-start.1 = (s16[264,1024]{1,0:T(8,128)(2,1)S(1)}, s16[264,1024]{1,0:T(8,128)(2,1)}, u32[]{:S(2)}, u32[]{:S(2)}) collective-permute-start(s16[264,1024]{1,0:T(8,128)(2,1)S(1)} %pad_add_fusion), channel_id=1, source_target_pairs={{0,3},{1,2},{2,1},{3,0},{4,7},{5,6},{6,5},{7,4},{8,11},{9,10},{10,... | collective-permute-start | bytes 1622024 | tf_op jit(solution)/shard_map/ppermute | solution.py:55
  15.5 17.3 %all-to-all-start = ((bf16[8,3,1024]{2,1,0:T(4,128)(2,1)}), bf16[8,3,1024]{2,1,0:T(4,128)(2,1)S(1)}, u32[]{:S(2)}, u32[]{:S(2)}) async-start(bf16[8,3,1024]{2,1,0:T(4,128)(2,1)} %broadcast_in_dim.34), calls=%async_computation | async-start | bytes 131072 | tf_op jit(solution)/shard_map/all_to_all | solution.py:76
  25.5 25.6 %collective-permute-start.2 = (s16[136,1024]{1,0:T(8,128)(2,1)S(1)}, s16[136,1024]{1,0:T(8,128)(2,1)S(1)}, u32[]{:S(2)}, u32[]{:S(2)}) collective-permute-start(s16[136,1024]{1,0:T(8,128)(2,1)S(1)} %fusion.19), channel_id=1, source_target_pairs={{0,256},{256,0},{1,257},{257,1},{2,258},{258,2},{3,259},{259,3},{4... | collective-permute-start | bytes 835592 | tf_op jit(solution)/shard_map/ppermute | solution.py:52
  32.7 11.5 %all-to-all-start.1 = ((s32[16,1,1024]{2,1,0:T(1,128)}), s32[16,1,1024]{2,1,0:T(1,128)S(1)}, u32[]{:S(2)}, u32[]{:S(2)}) async-start(s32[16,1,1024]{2,1,0:T(1,128)} %all_to_all.40), calls=%async_computation.1 | async-start | bytes 131072 | tf_op jit(solution)/shard_map/all_to_all | solution.py:70
  37.0 23.4 %collective-permute-start.3 = (s16[128,1024]{1,0:T(8,128)(2,1)}, s16[128,1024]{1,0:T(8,128)(2,1)}, u32[]{:S(2)}, u32[]{:S(2)}) collective-permute-start(s16[128,1024]{1,0:T(8,128)(2,1)} %collective-permute-done), channel_id=1, source_target_pairs={{0,3},{1,2},{2,1},{3,0},{4,7},{5,6},{6,5},{7,4},{8,11},{9,10},{10,... | collective-permute-start | bytes 786440 | tf_op jit(solution)/shard_map/ppermute | solution.py:55
  52.1 11.0 %collective-permute-start.4 = (s16[136,1024]{1,0:T(8,128)(2,1)S(1)}, s16[136,1024]{1,0:T(8,128)(2,1)S(1)}, u32[]{:S(2)}, u32[]{:S(2)}) collective-permute-start(s16[136,1024]{1,0:T(8,128)(2,1)S(1)} %collective-permute-done.2), channel_id=1, source_target_pairs={{0,3},{1,2},{2,1},{3,0},{4,7},{5,6},{6,5},{7,4},{8,11},{9,10},{10,... | collective-permute-start | bytes 835592 | tf_op jit(solution)/shard_map/ppermute | solution.py:55
  63.1 0.7 copy-start.4
  64.5 10.8 %all-to-all-start.2 = ((bf16[4,24,1024]{2,1,0:T(8,128)(2,1)}), bf16[4,24,1024]{2,1,0:T(8,128)(2,1)S(1)}, u32[]{:S(2)}, u32[]{:S(2)}) async-start(bf16[4,24,1024]{2,1,0:T(8,128)(2,1)} %broadcast_in_dim.36), calls=%async_computation.2 | async-start | bytes 393216 | tf_op jit(solution)/shard_map/all_to_all | solution.py:92
  76.1 8.1 %all-to-all-start.3 = ((bf16[4,3,4,1024]{3,2,1,0:T(4,128)(2,1)}), bf16[4,3,4,1024]{3,2,1,0:T(4,128)(2,1)S(1)}, u32[]{:S(2)}, u32[]{:S(2)}) async-start(bf16[4,3,4,1024]{3,2,1,0:T(4,128)(2,1)} %broadcast_in_dim.38), calls=%async_computation.3 | async-start | bytes 196608 | tf_op jit(solution)/shard_map/all_to_all | solution.py:21
  84.1 1.6 copy-start
  104.8 1.6 copy-start.1
  134.9 1.6 copy-start.2
  164.2 1.6 copy-start.3
  179.0 14.1 %all-to-all-start.10 = ((bf16[8,3,4,2048]{3,2,1,0:T(4,128)(2,1)}), bf16[8,3,4,2048]{3,2,1,0:T(4,128)(2,1)S(1)}, u32[]{:S(2)}, u32[]{:S(2)}) async-start(bf16[8,3,4,2048]{3,2,1,0:T(4,128)(2,1)} %broadcast_in_dim.49), calls=%async_computation.10 | async-start | bytes 786432 | tf_op jit(solution)/shard_map/all_to_all | solution.py:21

commit v7 on v4

--- a/solution.py
+++ b/solution.py
@@ -35,20 +35,25 @@
     rows, cols = counts.shape
     scale = 1.0 / math.sqrt(rows * Y_HI * Z * CORE + cols * Y_LO * X)
 
-    everyone = spread(gene_totals, ("y_lo", "x"), Y_LO * X)
+    def over_y(block):
+        return lax.ppermute(block, "y_hi", [(0, 1), (1, 0)])
 
+    mine = counts.astype(I16)
+    other = over_y(mine)
+    held, cell_totals = lax.optimization_barrier((mine, cell_totals))
     pieces = jnp.stack([cell_totals >> shift & 2047 for shift in (0, 11, 22)])
-    extra = jnp.zeros((EXTRA, cols), I16).at[:3, :rows].set(pieces.astype(I16))
-    mine = jnp.concatenate([counts.astype(I16), extra])
-    other = lax.ppermute(mine, "y_hi", [(0, 1), (1, 0)])
+    pieces = jnp.zeros((EXTRA, cols), I16).at[:3, :rows].set(pieces.astype(I16))
+    beyond = over_y(pieces)
 
+    ready, held, pieces = lax.optimization_barrier((copies(test_matrix.T, Z), held, pieces))
+    test = lax.all_to_all(ready, "z", 0, 0, tiled=True).reshape(Z * test_matrix.shape[1], cols)
+    ready, test = lax.optimization_barrier((copies(gene_totals, Y_LO * X), test))
+    everyone = lax.all_to_all(ready, ("y_lo", "x"), 0, 0, tiled=True)
     total = jnp.sum(everyone).astype(F32)
     fraction = gene_totals.astype(F32) / total
-    test, fraction = lax.optimization_barrier((test_matrix.T, fraction))
-    test = spread(test, "z", Z).reshape(Z * test_matrix.shape[1], cols)
 
-    def resid(block):
-        both = lax.all_gather(block, "core")
+    def resid(block, pieces):
+        both = lax.all_gather(jnp.concatenate([block, pieces]), "core")
         pieces = both[:, rows : rows + 3, :rows].astype(jnp.int32)
         owned = (pieces[:, 0] + (pieces[:, 1] << 11) + (pieces[:, 2] << 22)).astype(F32)
         expected = owned[:, :, None] * fraction[None, None, :]
@@ -57,7 +62,8 @@
             / jnp.sqrt(expected + expected * expected / 100.0)
         ).astype(BF16)
 
-    stored = jnp.concatenate([resid(mine), resid(other)]).reshape(BLOCKS * rows, cols)
+    stored = jnp.concatenate([resid(held, pieces), resid(other, beyond)])
+    stored = stored.reshape(BLOCKS * rows, cols)
 
     def cell_side(panel, factor):
         part = lax.dot_general(
@@ -75,15 +81,27 @@
         sketch = cell_side(panel, scale)
     gene_panel = gene_side(sketch)
 
-    width = sketch.shape[0]
-    parts = sketch.reshape(width, Y_HI, CORE, rows)
-    parts = jnp.where(lax.axis_index("y_hi") == 0, parts, parts[:, ::-1])
-    parts = parts.reshape(width, BLOCKS, rows).transpose(1, 0, 2)
-    send = jnp.concatenate([parts, copies(gene_panel, BLOCKS)], axis=2)
+    sketch, gene_panel = lax.optimization_barrier((sketch, gene_panel))
+    half = CORE * rows
+    near, far = sketch[:, :half], sketch[:, half:]
+    low = lax.axis_index("y_hi") == 0
+    parts = jnp.concatenate([jnp.where(low, near, far), jnp.where(low, far, near)], axis=1)
+    send = jnp.stack(
+        [
+            jnp.concatenate([parts[:, i * rows : (i + 1) * rows], gene_panel], axis=1)
+            for i in range(BLOCKS)
+        ]
+    )
     got = lax.all_to_all(send, ("y_hi", "core"), 0, 0, tiled=True)
-    got = got.reshape(Y_HI, CORE, Z, width // Z, rows + cols).transpose(0, 2, 1, 3, 4)
-    got = got.reshape(BLOCKS * width, rows + cols)
-    return (got[:, :rows].T, got[:, rows:].T)
+    got = got.reshape(-1, rows + cols)
+    count = got.shape[0]
+    order = np.arange(count).reshape(Y_HI, CORE, Z, -1).transpose(0, 2, 1, 3).reshape(-1)
+    pick = jnp.asarray(np.eye(count)[order], BF16)
+
+    def ordered(block):
+        return jnp.dot(pick, block, preferred_element_type=F32).astype(BF16).T
+
+    return (ordered(got[:, :rows]), ordered(got[:, rows:]))
 
 
 def solution(mesh):

time: 219 us -> 212 us (0.968)
  waiting for transfers between devices: 37.5 us -> 21.5 us
  starting transfers between devices: 26.2 us -> 31 us
  blocking collectives: 138 us -> 141 us
    all_to_all x3 -> x1, waiting for transfers between devices: 37.5 us -> 10.6 us  [spread(): return lax.all_to_all(copies(x, n), axis, 0, 0, tiled=True)]
    all_to_all x0 -> x2, starting transfers between devices: none -> 17.3 us  [the longest x1 10 us: shards(): lax.all_to_all(ready, 'z', 0, 0, tiled=True)]
    all_to_all x3 -> x1, starting transfers between devices: 18 us -> 3.45 us  [spread(): return lax.all_to_all(copies(x, n), axis, 0, 0, tiled=True)]
    all_to_all x0 -> x2, waiting for transfers between devices: none -> 10.9 us  [the longest x1 7.24 us: shards(): everyone = lax.all_to_all(ready, ('y_lo', 'x'), 0, 0, tiled=True)]
    ppermute x1 -> x2, starting transfers between devices: 8.28 us -> 10.2 us  [over_y(): return lax.ppermute(block, 'y_hi', [(0, 1), (1, 0)])]
  transfers between devices with their start and end apart: 4 -> 5, of which waited for: 3 -> 3; matrix products, arithmetic and copies ran while one was open for 1% -> 1% of each run, Pallas kernels for 0% -> 0%
where the time goes in v7:
time: 212 us; the launch traced here: 209 us
  blocking collectives  141 us (67%)
  starting transfers between devices  31 us (15%)
  waiting for transfers between devices  21.5 us (10%)
  matrix products  5.8 us (3%)
  other arithmetic  4.92 us (2%)
  local copies, waits for them, and re-layouts  3.21 us (2%)
    all_to_all x11, blocking collectives, spread(): return lax.all_to_all(copies(x, n), axis, 0, 0, tiled=True)  106 us
    all_to_all x1, blocking collectives, shards(): got = lax.all_to_all(send, ('y_hi', 'core'), 0, 0, tiled=True)  25.7 us
    all_to_all x1, waiting for transfers between devices, spread(): return lax.all_to_all(copies(x, n), axis, 0, 0, tiled=True)  10.6 us
    ppermute x2, starting transfers between devices, over_y(): return lax.ppermute(block, 'y_hi', [(0, 1), (1, 0)])  10.2 us
    all_to_all x1, starting transfers between devices, shards(): lax.all_to_all(ready, 'z', 0, 0, tiled=True)  10 us
    all_gather x2, blocking collectives, resid(): both = lax.all_gather(jnp.concatenate([block, pieces]), 'core')  9.53 us
    all_to_all x1, starting transfers between devices, shards(): everyone = lax.all_to_all(ready, ('y_lo', 'x'), 0, 0, tiled=True)  7.27 us
    all_to_all x1, waiting for transfers between devices, shards(): everyone = lax.all_to_all(ready, ('y_lo', 'x'), 0, 0, tiled=True)  7.24 us
  transfers between devices with their start and end apart: 5, of which 3 were waited for; matrix products, arithmetic and copies ran while one was open for 1% of the time, Pallas kernels for 0%

profile of v7, /device:TPU:1, one launch (start us, length us, event | category | flops | bytes accessed | tf_op | source)
XLA Modules:
  0.0 209.4 jit_solution(12580507026499278519)
XLA Ops:
  0.6 0.0 copy-start.1
  0.6 1.3 convert_element_type.411
  1.9 8.3 %collective-permute-start = (s16[256,1024]{1,0:T(8,128)(2,1)S(1)}, s16[256,1024]{1,0:T(8,128)(2,1)S(1)}, u32[]{:S(2)}, u32[]{:S(2)}) collective-permute-start(s16[256,1024]{1,0:T(8,128)(2,1)S(1)} %convert_element_type.411), channel_id=1, source_target_pairs={{0,256},{256,0},{1,257},{257,1},{2,258},{258,2},{3,259},{259,3},{4... | collective-permute-start | bytes 1572872 | tf_op jit(solution)/shard_map/ppermute | solution.py:39
  10.2 0.7 and_convert_fusion.2
  11.0 1.9 collective-permute-start.1
  12.9 1.3 broadcast_in_dim.37
  14.3 10.0 %all-to-all-start = ((bf16[8,3,1024]{2,1,0:T(4,128)(2,1)}), bf16[8,3,1024]{2,1,0:T(4,128)(2,1)S(1)}, u32[]{:S(2)}, u32[]{:S(2)}) async-start(bf16[8,3,1024]{2,1,0:T(4,128)(2,1)} %broadcast_in_dim.37), calls=%async_computation | async-start | bytes 131072 | tf_op jit(solution)/shard_map/all_to_all | solution.py:49
  24.3 3.5 %all-gather.4 = s16[528,1024]{1,0:T(8,128)(2,1)S(1)} all-gather(s16[264,1024]{1,0:T(8,128)(2,1)S(1)} %pad_add_fusion), channel_id=2, replica_groups=mesh['y_hi'=2,'z'=8,'core'=2,'y_lo'=4,'x'=4] {'core'}, dimensions={0}, use_global_device_ids=true | all-gather | bytes 1622016 | tf_op jit(solution)/shard_map/all_gather | solution.py:56
  27.9 3.6 %all-to-all-done = bf16[8,3,1024]{2,1,0:T(4,128)(2,1)S(1)} async-done(((bf16[8,3,1024]{2,1,0:T(4,128)(2,1)}), bf16[8,3,1024]{2,1,0:T(4,128)(2,1)S(1)}, u32[]{:S(2)}, u32[]{:S(2)}) %all-to-all-start) | async-done | bytes 49184 | tf_op jit(solution)/shard_map/all_to_all | solution.py:49
  31.6 0.0 copy-done.1
  31.6 0.7 all_to_all.49
  32.3 7.3 %all-to-all-start.1 = ((s32[16,1,1024]{2,1,0:T(1,128)}), s32[16,1,1024]{2,1,0:T(1,128)S(1)}, u32[]{:S(2)}, u32[]{:S(2)}) async-start(s32[16,1,1024]{2,1,0:T(1,128)} %all_to_all.49), calls=%async_computation.1 | async-start | bytes 131072 | tf_op jit(solution)/shard_map/all_to_all | solution.py:51
  39.6 7.2 %all-to-all-done.1 = s32[16,1,1024]{2,1,0:T(1,128)S(1)} async-done(((s32[16,1,1024]{2,1,0:T(1,128)}), s32[16,1,1024]{2,1,0:T(1,128)S(1)}, u32[]{:S(2)}, u32[]{:S(2)}) %all-to-all-start.1) | async-done | bytes 65568 | tf_op jit(solution)/shard_map/all_to_all | solution.py:51
  46.8 0.8 reduce_sum.9
  48.2 0.0 collective-permute-done.1
  48.3 0.0 collective-permute-done
  48.3 6.0 %all-gather.5 = s16[528,1024]{1,0:T(8,128)(2,1)S(1)} all-gather(s16[264,1024]{1,0:T(8,128)(2,1)S(1)} %pad_add_fusion.1), channel_id=3, replica_groups=mesh['y_hi'=2,'z'=8,'core'=2,'y_lo'=4,'x'=4] {'core'}, dimensions={0}, use_global_device_ids=true | all-gather | bytes 1622016 | tf_op jit(solution)/shard_map/all_gather | solution.py:56
  54.3 1.6 fusion.1
  55.9 0.2 pad_maximum_fusion
  56.1 0.7 convolution_convert_fusion.9
  56.8 7.8 %all_to_all.79 = bf16[4,24,1024]{2,1,0:T(8,128)(2,1)S(1)} all-to-all(bf16[4,24,1024]{2,1,0:T(8,128)(2,1)S(1)} %broadcast_in_dim.38), channel_id=1, replica_groups=mesh['y_hi'=2,'z'=8,'core'=2,'y_lo'=4,'x'=4] {'x'}, dimensions={0} | all-to-all | bytes 393216 | tf_op jit(solution)/shard_map/all_to_all | solution.py:21
  64.7 8.0 %all_to_all.80 = bf16[4,24,1024]{2,1,0:T(8,128)(2,1)S(1)} all-to-all(bf16[4,24,1024]{2,1,0:T(8,128)(2,1)S(1)} %broadcast_in_dim.40), channel_id=1, replica_groups=mesh['y_hi'=2,'z'=8,'core'=2,'y_lo'=4,'x'=4] {'y_lo'}, dimensions={0} | all-to-all | bytes 393216 | tf_op jit(solution)/shard_map/all_to_all | solution.py:21
  72.7 0.4 convolution_convert_fusion.8
  73.1 13.7 %all_to_all.81 = bf16[8,24,1024]{2,1,0:T(8,128)(2,1)S(1)} all-to-all(bf16[8,24,1024]{2,1,0:T(8,128)(2,1)S(1)} %broadcast_in_dim.41), channel_id=1, replica_groups=mesh['y_hi'=2,'z'=8,'core'=2,'y_lo'=4,'x'=4] {'z'}, dimensions={0} | all-to-all | bytes 786432 | tf_op jit(solution)/shard_map/all_to_all | solution.py:21
  86.9 0.7 convolution_convert_fusion.7
  87.6 7.5 %all_to_all.82 = bf16[4,24,1024]{2,1,0:T(8,128)(2,1)S(1)} all-to-all(bf16[4,24,1024]{2,1,0:T(8,128)(2,1)S(1)} %broadcast_in_dim.42), channel_id=1, replica_groups=mesh['y_hi'=2,'z'=8,'core'=2,'y_lo'=4,'x'=4] {'x'}, dimensions={0} | all-to-all | bytes 393216 | tf_op jit(solution)/shard_map/all_to_all | solution.py:21
  95.2 11.2 %all_to_all.83 = bf16[4,24,1024]{2,1,0:T(8,128)(2,1)S(1)} all-to-all(bf16[4,24,1024]{2,1,0:T(8,128)(2,1)S(1)} %broadcast_in_dim.44), channel_id=1, replica_groups=mesh['y_hi'=2,'z'=8,'core'=2,'y_lo'=4,'x'=4] {'y_lo'}, dimensions={0} | all-to-all | bytes 393216 | tf_op jit(solution)/shard_map/all_to_all | solution.py:21
  106.3 0.4 convolution_convert_fusion.6
  106.8 13.3 %all_to_all.84 = bf16[8,24,1024]{2,1,0:T(8,128)(2,1)S(1)} all-to-all(bf16[8,24,1024]{2,1,0:T(8,128)(2,1)S(1)} %broadcast_in_dim.45), channel_id=1, replica_groups=mesh['y_hi'=2,'z'=8,'core'=2,'y_lo'=4,'x'=4] {'z'}, dimensions={0} | all-to-all | bytes 786432 | tf_op jit(solution)/shard_map/all_to_all | solution.py:21
  120.1 0.7 convolution_convert_fusion.5
  120.8 7.5 %all_to_all.85 = bf16[4,24,1024]{2,1,0:T(8,128)(2,1)S(1)} all-to-all(bf16[4,24,1024]{2,1,0:T(8,128)(2,1)S(1)} %broadcast_in_dim.46), channel_id=1, replica_groups=mesh['y_hi'=2,'z'=8,'core'=2,'y_lo'=4,'x'=4] {'x'}, dimensions={0} | all-to-all | bytes 393216 | tf_op jit(solution)/shard_map/all_to_all | solution.py:21
  128.4 8.0 %all_to_all.86 = bf16[4,24,1024]{2,1,0:T(8,128)(2,1)S(1)} all-to-all(bf16[4,24,1024]{2,1,0:T(8,128)(2,1)S(1)} %broadcast_in_dim.48), channel_id=1, replica_groups=mesh['y_hi'=2,'z'=8,'core'=2,'y_lo'=4,'x'=4] {'y_lo'}, dimensions={0} | all-to-all | bytes 393216 | tf_op jit(solution)/shard_map/all_to_all | solution.py:21
  136.4 0.4 convolution_convert_fusion.4
  136.9 13.1 %all_to_all.87 = bf16[8,24,1024]{2,1,0:T(8,128)(2,1)S(1)} all-to-all(bf16[8,24,1024]{2,1,0:T(8,128)(2,1)S(1)} %broadcast_in_dim.49), channel_id=1, replica_groups=mesh['y_hi'=2,'z'=8,'core'=2,'y_lo'=4,'x'=4] {'z'}, dimensions={0} | all-to-all | bytes 786432 | tf_op jit(solution)/shard_map/all_to_all | solution.py:21
  150.0 0.7 convolution_convert_fusion.3
  150.7 7.8 %all_to_all.88 = bf16[4,24,1024]{2,1,0:T(8,128)(2,1)S(1)} all-to-all(bf16[4,24,1024]{2,1,0:T(8,128)(2,1)S(1)} %broadcast_in_dim.50), channel_id=1, replica_groups=mesh['y_hi'=2,'z'=8,'core'=2,'y_lo'=4,'x'=4] {'x'}, dimensions={0} | all-to-all | bytes 393216 | tf_op jit(solution)/shard_map/all_to_all | solution.py:21
  158.6 8.0 %all_to_all.89 = bf16[4,24,1024]{2,1,0:T(8,128)(2,1)S(1)} all-to-all(bf16[4,24,1024]{2,1,0:T(8,128)(2,1)S(1)} %broadcast_in_dim.52), channel_id=1, replica_groups=mesh['y_hi'=2,'z'=8,'core'=2,'y_lo'=4,'x'=4] {'y_lo'}, dimensions={0} | all-to-all | bytes 393216 | tf_op jit(solution)/shard_map/all_to_all | solution.py:21
  166.6 0.4 convolution_convert_fusion.2
  167.0 0.0 copy-start
  167.0 0.8 broadcast_in_dim.53
  167.8 3.5 %all-to-all-start.13 = ((bf16[8,24,1024]{2,1,0:T(8,128)(2,1)}), bf16[8,24,1024]{2,1,0:T(8,128)(2,1)S(1)}, u32[]{:S(2)}, u32[]{:S(2)}) async-start(bf16[8,24,1024]{2,1,0:T(8,128)(2,1)} %broadcast_in_dim.53), calls=%async_computation.13 | async-start | bytes 786432 | tf_op jit(solution)/shard_map/all_to_all | solution.py:21
  171.3 10.6 %all-to-all-done.13 = bf16[8,24,1024]{2,1,0:T(8,128)(2,1)S(1)} async-done(((bf16[8,24,1024]{2,1,0:T(8,128)(2,1)}), bf16[8,24,1024]{2,1,0:T(8,128)(2,1)S(1)}, u32[]{:S(2)}, u32[]{:S(2)}) %all-to-all-start.13) | async-done | bytes 393248 | tf_op jit(solution)/shard_map/all_to_all | solution.py:21
  181.9 0.1 fusion.26
  182.1 25.7 %all_to_all.90 = bf16[4,24,1280]{2,1,0:T(8,128)(2,1)S(1)} all-to-all(bf16[4,24,1280]{2,1,0:T(8,128)(2,1)S(1)} %pad_maximum_fusion.1), channel_id=1, replica_groups=mesh['y_hi'=2,'z'=8,'core'=2,'y_lo'=4,'x'=4] {'y_hi','core'}, dimensions={0} | all-to-all | bytes 491520 | tf_op jit(solution)/shard_map/all_to_all | solution.py:95
  207.8 0.0 copy-done
  207.8 0.9 convolution_convert_fusion
  208.6 0.8 convolution_convert_fusion.1
  (36 shorter events, 0.7 us)
Async XLA Ops:
  0.6 30.9 %copy-start.1 = (s32[1024]{0:T(1024)S(1)}, s32[1024]{0:T(1024)}, u32[]{:S(2)}) copy-start(s32[1024]{0:T(1024)} %param.9) | copy-start | bytes 12292
  1.9 46.3 %collective-permute-start = (s16[256,1024]{1,0:T(8,128)(2,1)S(1)}, s16[256,1024]{1,0:T(8,128)(2,1)S(1)}, u32[]{:S(2)}, u32[]{:S(2)}) collective-permute-start(s16[256,1024]{1,0:T(8,128)(2,1)S(1)} %convert_element_type.411), channel_id=1, source_target_pairs={{0,256},{256,0},{1,257},{257,1},{2,258},{258,2},{3,259},{259,3},{4... | collective-permute-start | bytes 1572872 | tf_op jit(solution)/shard_map/ppermute | solution.py:39
  11.0 37.3 %collective-permute-start.1 = (s16[8,1024]{1,0:T(8,128)(2,1)S(1)}, s16[8,1024]{1,0:T(8,128)(2,1)S(1)}, u32[]{:S(2)}, u32[]{:S(2)}) collective-permute-start(s16[8,1024]{1,0:T(8,128)(2,1)S(1)} %scatter.4), channel_id=1, source_target_pairs={{0,256},{256,0},{1,257},{257,1},{2,258},{258,2},{3,259},{259,3},{4... | collective-permute-start | bytes 49160 | tf_op jit(solution)/shard_map/ppermute | solution.py:39
  14.3 17.3 %all-to-all-start = ((bf16[8,3,1024]{2,1,0:T(4,128)(2,1)}), bf16[8,3,1024]{2,1,0:T(4,128)(2,1)S(1)}, u32[]{:S(2)}, u32[]{:S(2)}) async-start(bf16[8,3,1024]{2,1,0:T(4,128)(2,1)} %broadcast_in_dim.37), calls=%async_computation | async-start | bytes 131072 | tf_op jit(solution)/shard_map/all_to_all | solution.py:49
  32.3 14.5 %all-to-all-start.1 = ((s32[16,1,1024]{2,1,0:T(1,128)}), s32[16,1,1024]{2,1,0:T(1,128)S(1)}, u32[]{:S(2)}, u32[]{:S(2)}) async-start(s32[16,1,1024]{2,1,0:T(1,128)} %all_to_all.49), calls=%async_computation.1 | async-start | bytes 131072 | tf_op jit(solution)/shard_map/all_to_all | solution.py:51
  167.0 40.8 %copy-start = (bf16[96,96]{1,0:T(8,128)(2,1)S(1)}, bf16[96,96]{1,0:T(8,128)(2,1)}, u32[]{:S(2)}) copy-start(bf16[96,96]{1,0:T(8,128)(2,1)} %constant.52.clone) | copy-start | bytes 55300
  167.8 14.1 %all-to-all-start.13 = ((bf16[8,24,1024]{2,1,0:T(8,128)(2,1)}), bf16[8,24,1024]{2,1,0:T(8,128)(2,1)S(1)}, u32[]{:S(2)}, u32[]{:S(2)}) async-start(bf16[8,24,1024]{2,1,0:T(8,128)(2,1)} %broadcast_in_dim.53), calls=%async_computation.13 | async-start | bytes 786432 | tf_op jit(solution)/shard_map/all_to_all | solution.py:21

commit v8 on v2

v8 whole, which is shorter than its diff:
```python
import math

import jax
import jax.numpy as jnp
import numpy as np
from jax import lax
from jax.sharding import Mesh, PartitionSpec as P

ITERS = 3
Y_HI, Z, CORE, Y_LO, X = 2, 8, 2, 4, 4
BLOCKS = CORE * Y_HI
EXTRA = 8
F32, BF16, I16 = jnp.float32, jnp.bfloat16, jnp.int16


def copies(x, n):
    return jnp.broadcast_to(x[None], (n,) + x.shape)


def spread(x, axis, n):
    return lax.all_to_all(copies(x, n), axis, 0, 0)


def gather_sum(x, axis, n, factor=None):
    got = spread(x, axis, n)
    total = got[0].astype(F32)
    for i in range(1, n):
        total = total + got[i].astype(F32)
    if factor is not None:
        total = total * factor
    return total.astype(BF16)


def shards(counts, cell_totals, gene_totals, test_matrix):
    rows, cols = counts.shape
    scale = 1.0 / math.sqrt(rows * Y_HI * Z * CORE + cols * Y_LO * X)

    pieces = jnp.stack([cell_totals >> shift & 2047 for shift in (0, 11, 22)])
    extra = jnp.zeros((EXTRA, cols), I16).at[:3, :rows].set(pieces.astype(I16))
    mine = jnp.concatenate([counts.astype(I16), extra])
    other = lax.ppermute(mine, "y_hi", [(0, 1), (1, 0)])

    test = spread(test_matrix.T, "z", Z)
    ready, test = lax.optimization_barrier((gene_totals.reshape(8, -1), test))
    totals = spread(ready, ("y_lo", "x"), Y_LO * X)
    test, totals = lax.optimization_barrier((test, totals))
    test = test.reshape(Z * test_matrix.shape[1], cols)
    total = jnp.sum(totals)
    fraction = gene_totals.astype(F32) / total.astype(F32)

    low = lax.axis_index("y_hi") == 0
    pair = jnp.stack([jnp.where(low, mine, other), jnp.where(low, other, mine)])
    blocks = lax.all_gather(pair, "core").reshape(BLOCKS, rows + EXTRA, cols)
    pieces = blocks[:, rows : rows + 3, :rows].astype(jnp.int32)
    owned = (pieces[:, 0] + (pieces[:, 1] << 11) + (pieces[:, 2] << 22)).astype(F32)
    expected = owned[:, :, None] * fraction[None, None, :]
    stored = (
        (blocks[:, :rows].astype(F32) - expected)
        / jnp.sqrt(expected + expected * expected / 100.0)
    ).astype(BF16)
    stored = stored.reshape(BLOCKS * rows, cols)

    def cell_side(panel, factor):
        part = lax.dot_general(
            panel, stored, (((1,), (1,)), ((), ())), preferred_element_type=F32
        ).astype(BF16)
        return gather_sum(gather_sum(part, "x", X), "y_lo", Y_LO, factor)

    def gene_side(sketch):
        part = jnp.dot(sketch, stored, preferred_element_type=F32).astype(BF16)
        return gather_sum(part, "z", Z, scale)

    sketch = cell_side(test, 1.0)
    for step in range(ITERS):
        panel = gene_side(sketch)
        sketch = cell_side(panel, scale)
    gene_panel = gene_side(sketch)

    width = sketch.shape[0]
    count = BLOCKS * width
    order = np.arange(count).reshape(CORE, Y_HI, Z, -1).transpose(1, 2, 0, 3).reshape(-1)
    pick = jnp.asarray(np.eye(count)[order], BF16)
    sketch, gene_panel = lax.optimization_barrier((sketch, gene_panel))
    send = jnp.stack(
        [
            jnp.concatenate([sketch[:, i * rows : (i + 1) * rows], gene_panel], axis=1)
            for i in range(BLOCKS)
        ]
    )
    got = lax.all_to_all(send, ("core", "y_hi"), 0, 0)
    got = got.reshape(-1, rows + cols)

    def ordered(block):
        return jnp.dot(pick, block, preferred_element_type=F32).astype(BF16).T

    return (ordered(got[:, :rows]), ordered(got[:, rows:]))


def solution(mesh):
    fine = Mesh(
        np.asarray(mesh.devices).reshape(Y_HI, Z, CORE, Y_LO, X), ("y_hi", "z", "core", "y_lo", "x")
    )
    cell, gene = ("y_hi", "z", "core"), ("y_lo", "x")
    in_specs = (P(cell, gene), P(cell), P(gene), P(gene, cell))
    out_specs = (P(cell, None), P(gene, None))
    return jax.shard_map(shards, mesh=fine, in_specs=in_specs, out_specs=out_specs, check_vma=False)
```

time: 208 us -> 206 us (level)
  blocking collectives: 158 us -> 171 us
  waiting for transfers between devices: 17.4 us -> 7.25 us
  starting transfers between devices: 16.2 us -> 12.7 us
  local copies, waits for them, and re-layouts: 4.06 us -> 1.08 us
    all_to_all x13 -> x14, blocking collectives: 151 us -> 164 us  [the longest x13 140 us: spread(): return lax.all_to_all(copies(x, n), axis, 0, 0)]
    all_to_all x2 -> x1, waiting for transfers between devices: 17.4 us -> 7.24 us  [spread(): return lax.all_to_all(copies(x, n), axis, 0, 0)]
    all_to_all x2 -> x1, starting transfers between devices: 7.92 us -> 4.47 us  [spread(): return lax.all_to_all(copies(x, n), axis, 0, 0)]
  transfers between devices with their start and end apart: 3 -> 2, of which waited for: 2 -> 1; matrix products, arithmetic and copies ran while one was open for 1% -> 1% of each run, Pallas kernels for 0% -> 0%
where the time goes in v8:
time: 206 us; the launch traced here: 204 us
  blocking collectives  171 us (83%)
  starting transfers between devices  12.7 us (6%)
  waiting for transfers between devices  7.25 us (4%)
  matrix products  5.79 us (3%)
  other arithmetic  4.9 us (2%)
    all_to_all x13, blocking collectives, spread(): return lax.all_to_all(copies(x, n), axis, 0, 0)  140 us
    all_to_all x1, blocking collectives, shards(): got = lax.all_to_all(send, ('core', 'y_hi'), 0, 0)  24.4 us
    ppermute x1, starting transfers between devices, shards(): other = lax.ppermute(mine, 'y_hi', [(0, 1), (1, 0)])  8.28 us
    all_to_all x1, waiting for transfers between devices, spread(): return lax.all_to_all(copies(x, n), axis, 0, 0)  7.24 us
    all_gather x1, blocking collectives, shards(): blocks = lax.all_gather(pair, 'core').reshape(BLOCKS, rows + EXTRA, cols)  6.5 us
    all_to_all x1, starting transfers between devices, spread(): return lax.all_to_all(copies(x, n), axis, 0, 0)  4.47 us
  transfers between devices with their start and end apart: 2, of which 1 were waited for; matrix products, arithmetic and copies ran while one was open for 1% of the time, Pallas kernels for 0%

profile of v8, /device:TPU:1, one launch (start us, length us, event | category | flops | bytes accessed | tf_op | source)
XLA Modules:
  0.0 204.1 jit_solution(17875913329501433338)
XLA Ops:
  0.6 0.0 copy-start.2
  0.6 0.0 copy-start.1
  0.7 0.7 and_convert_fusion.2
  1.4 1.3 convert_element_type.392
  2.7 8.3 %collective-permute-start = (s16[264,1024]{1,0:T(8,128)(2,1)S(1)}, s16[264,1024]{1,0:T(8,128)(2,1)S(1)}, u32[]{:S(2)}, u32[]{:S(2)}) collective-permute-start(s16[264,1024]{1,0:T(8,128)(2,1)S(1)} %pad_add_fusion.1), channel_id=1, source_target_pairs={{0,256},{256,0},{1,257},{257,1},{2,258},{258,2},{3,259},{259,3},{4... | collective-permute-start | bytes 1622024 | tf_op jit(solution)/shard_map/ppermute | solution.py:41
  11.0 0.0 copy-done.2
  11.1 17.4 %all_to_all.75 = bf16[8,3,1024]{2,1,0:T(4,128)(2,1)S(1)} all-to-all(bf16[8,3,1024]{2,1,0:T(4,128)(2,1)S(1)} %broadcast_in_dim.36), channel_id=1, replica_groups=mesh['y_hi'=2,'z'=8,'core'=2,'y_lo'=4,'x'=4] {'z'}, dimensions={0} | all-to-all | bytes 98304 | tf_op jit(solution)/shard_map/all_to_all | solution.py:21
  28.4 0.0 copy-done.1
  28.4 0.6 broadcast_in_dim.37
  29.1 4.5 %all-to-all-start.1 = ((s32[16,8,128]{2,1,0:T(8,128)}), s32[16,8,128]{2,1,0:T(8,128)S(1)}, u32[]{:S(2)}, u32[]{:S(2)}) async-start(s32[16,8,128]{2,1,0:T(8,128)} %broadcast_in_dim.37), calls=%async_computation.1 | async-start | bytes 131072 | tf_op jit(solution)/shard_map/all_to_all | solution.py:21
  33.5 7.2 %all-to-all-done.1 = s32[16,8,128]{2,1,0:T(8,128)S(1)} async-done(((s32[16,8,128]{2,1,0:T(8,128)}), s32[16,8,128]{2,1,0:T(8,128)S(1)}, u32[]{:S(2)}, u32[]{:S(2)}) %all-to-all-start.1) | async-done | bytes 65568 | tf_op jit(solution)/shard_map/all_to_all | solution.py:21
  40.8 0.6 reduce_sum.9
  42.1 0.0 collective-permute-done
  42.2 0.3 select_bitcast_fusion.1
  42.4 0.1 pad_add_fusion
  42.5 6.5 %all-gather.2 = s16[4,264,1024]{2,1,0:T(8,128)(2,1)S(1)} all-gather(s16[2,264,1024]{2,1,0:T(8,128)(2,1)S(1)} %pad_add_fusion), channel_id=2, replica_groups=mesh['y_hi'=2,'z'=8,'core'=2,'y_lo'=4,'x'=4] {'core'}, dimensions={0}, use_global_device_ids=true | all-gather | bytes 3244032 | tf_op jit(solution)/shard_map/all_gather | solution.py:53
  49.0 1.6 fusion.1
  50.6 0.7 convolution_convert_fusion.9
  51.3 7.8 %all_to_all.76 = bf16[4,24,1024]{2,1,0:T(8,128)(2,1)S(1)} all-to-all(bf16[4,24,1024]{2,1,0:T(8,128)(2,1)S(1)} %broadcast_in_dim.38), channel_id=1, replica_groups=mesh['y_hi'=2,'z'=8,'core'=2,'y_lo'=4,'x'=4] {'x'}, dimensions={0} | all-to-all | bytes 393216 | tf_op jit(solution)/shard_map/all_to_all | solution.py:21
  59.2 8.0 %all_to_all.77 = bf16[4,24,1024]{2,1,0:T(8,128)(2,1)S(1)} all-to-all(bf16[4,24,1024]{2,1,0:T(8,128)(2,1)S(1)} %broadcast_in_dim.40), channel_id=1, replica_groups=mesh['y_hi'=2,'z'=8,'core'=2,'y_lo'=4,'x'=4] {'y_lo'}, dimensions={0} | all-to-all | bytes 393216 | tf_op jit(solution)/shard_map/all_to_all | solution.py:21
  67.2 0.4 convolution_convert_fusion.8
  67.6 17.9 %all_to_all.78 = bf16[8,24,1024]{2,1,0:T(8,128)(2,1)S(1)} all-to-all(bf16[8,24,1024]{2,1,0:T(8,128)(2,1)S(1)} %broadcast_in_dim.41), channel_id=1, replica_groups=mesh['y_hi'=2,'z'=8,'core'=2,'y_lo'=4,'x'=4] {'z'}, dimensions={0} | all-to-all | bytes 786432 | tf_op jit(solution)/shard_map/all_to_all | solution.py:21
  85.5 0.7 convolution_convert_fusion.7
  86.2 7.5 %all_to_all.79 = bf16[4,24,1024]{2,1,0:T(8,128)(2,1)S(1)} all-to-all(bf16[4,24,1024]{2,1,0:T(8,128)(2,1)S(1)} %broadcast_in_dim.42), channel_id=1, replica_groups=mesh['y_hi'=2,'z'=8,'core'=2,'y_lo'=4,'x'=4] {'x'}, dimensions={0} | all-to-all | bytes 393216 | tf_op jit(solution)/shard_map/all_to_all | solution.py:21
  93.8 9.0 %all_to_all.80 = bf16[4,24,1024]{2,1,0:T(8,128)(2,1)S(1)} all-to-all(bf16[4,24,1024]{2,1,0:T(8,128)(2,1)S(1)} %broadcast_in_dim.44), channel_id=1, replica_groups=mesh['y_hi'=2,'z'=8,'core'=2,'y_lo'=4,'x'=4] {'y_lo'}, dimensions={0} | all-to-all | bytes 393216 | tf_op jit(solution)/shard_map/all_to_all | solution.py:21
  102.8 0.4 convolution_convert_fusion.6
  103.2 14.7 %all_to_all.81 = bf16[8,24,1024]{2,1,0:T(8,128)(2,1)S(1)} all-to-all(bf16[8,24,1024]{2,1,0:T(8,128)(2,1)S(1)} %broadcast_in_dim.45), channel_id=1, replica_groups=mesh['y_hi'=2,'z'=8,'core'=2,'y_lo'=4,'x'=4] {'z'}, dimensions={0} | all-to-all | bytes 786432 | tf_op jit(solution)/shard_map/all_to_all | solution.py:21
  117.9 0.7 convolution_convert_fusion.5
  118.6 7.5 %all_to_all.82 = bf16[4,24,1024]{2,1,0:T(8,128)(2,1)S(1)} all-to-all(bf16[4,24,1024]{2,1,0:T(8,128)(2,1)S(1)} %broadcast_in_dim.46), channel_id=1, replica_groups=mesh['y_hi'=2,'z'=8,'core'=2,'y_lo'=4,'x'=4] {'x'}, dimensions={0} | all-to-all | bytes 393216 | tf_op jit(solution)/shard_map/all_to_all | solution.py:21
  126.2 8.0 %all_to_all.83 = bf16[4,24,1024]{2,1,0:T(8,128)(2,1)S(1)} all-to-all(bf16[4,24,1024]{2,1,0:T(8,128)(2,1)S(1)} %broadcast_in_dim.48), channel_id=1, replica_groups=mesh['y_hi'=2,'z'=8,'core'=2,'y_lo'=4,'x'=4] {'y_lo'}, dimensions={0} | all-to-all | bytes 393216 | tf_op jit(solution)/shard_map/all_to_all | solution.py:21
  134.2 0.4 convolution_convert_fusion.4
  134.7 13.1 %all_to_all.84 = bf16[8,24,1024]{2,1,0:T(8,128)(2,1)S(1)} all-to-all(bf16[8,24,1024]{2,1,0:T(8,128)(2,1)S(1)} %broadcast_in_dim.49), channel_id=1, replica_groups=mesh['y_hi'=2,'z'=8,'core'=2,'y_lo'=4,'x'=4] {'z'}, dimensions={0} | all-to-all | bytes 786432 | tf_op jit(solution)/shard_map/all_to_all | solution.py:21
  147.8 0.7 convolution_convert_fusion.3
  148.5 7.5 %all_to_all.85 = bf16[4,24,1024]{2,1,0:T(8,128)(2,1)S(1)} all-to-all(bf16[4,24,1024]{2,1,0:T(8,128)(2,1)S(1)} %broadcast_in_dim.50), channel_id=1, replica_groups=mesh['y_hi'=2,'z'=8,'core'=2,'y_lo'=4,'x'=4] {'x'}, dimensions={0} | all-to-all | bytes 393216 | tf_op jit(solution)/shard_map/all_to_all | solution.py:21
  156.1 8.2 %all_to_all.86 = bf16[4,24,1024]{2,1,0:T(8,128)(2,1)S(1)} all-to-all(bf16[4,24,1024]{2,1,0:T(8,128)(2,1)S(1)} %broadcast_in_dim.52), channel_id=1, replica_groups=mesh['y_hi'=2,'z'=8,'core'=2,'y_lo'=4,'x'=4] {'y_lo'}, dimensions={0} | all-to-all | bytes 393216 | tf_op jit(solution)/shard_map/all_to_all | solution.py:21
  164.3 0.4 convolution_convert_fusion.2
  164.7 0.0 copy-start
  164.7 13.1 %all_to_all.87 = bf16[8,24,1024]{2,1,0:T(8,128)(2,1)S(1)} all-to-all(bf16[8,24,1024]{2,1,0:T(8,128)(2,1)S(1)} %broadcast_in_dim.53), channel_id=1, replica_groups=mesh['y_hi'=2,'z'=8,'core'=2,'y_lo'=4,'x'=4] {'z'}, dimensions={0} | all-to-all | bytes 786432 | tf_op jit(solution)/shard_map/all_to_all | solution.py:21
  177.8 0.1 fusion.22
  178.0 24.4 %all_to_all.88 = bf16[4,24,1280]{2,1,0:T(8,128)(2,1)S(1)} all-to-all(bf16[4,24,1280]{2,1,0:T(8,128)(2,1)S(1)} %pad_maximum_fusion), channel_id=1, replica_groups=mesh['y_hi'=2,'z'=8,'core'=2,'y_lo'=4,'x'=4] {'core','y_hi'}, dimensions={0} | all-to-all | bytes 491520 | tf_op jit(solution)/shard_map/all_to_all | solution.py:90
  202.4 0.0 copy-done
  202.4 0.8 convolution_convert_fusion.1
  203.2 0.9 convolution_convert_fusion
  (31 shorter events, 0.7 us)
Async XLA Ops:
  0.6 10.4 %copy-start.2 = (bf16[1024,3]{0,1:T(4,128)(2,1)S(1)}, bf16[1024,3]{0,1:T(4,128)(2,1)}, u32[]{:S(2)}) copy-start(bf16[1024,3]{0,1:T(4,128)(2,1)} %param.10) | copy-start | bytes 18436
  0.6 27.8 %copy-start.1 = (s32[1024]{0:T(1024)S(1)}, s32[1024]{0:T(1024)}, u32[]{:S(2)}) copy-start(s32[1024]{0:T(1024)} %param.9) | copy-start | bytes 12292
  2.7 39.4 %collective-permute-start = (s16[264,1024]{1,0:T(8,128)(2,1)S(1)}, s16[264,1024]{1,0:T(8,128)(2,1)S(1)}, u32[]{:S(2)}, u32[]{:S(2)}) collective-permute-start(s16[264,1024]{1,0:T(8,128)(2,1)S(1)} %pad_add_fusion.1), channel_id=1, source_target_pairs={{0,256},{256,0},{1,257},{257,1},{2,258},{258,2},{3,259},{259,3},{4... | collective-permute-start | bytes 1622024 | tf_op jit(solution)/shard_map/ppermute | solution.py:41
  29.1 11.7 %all-to-all-start.1 = ((s32[16,8,128]{2,1,0:T(8,128)}), s32[16,8,128]{2,1,0:T(8,128)S(1)}, u32[]{:S(2)}, u32[]{:S(2)}) async-start(s32[16,8,128]{2,1,0:T(8,128)} %broadcast_in_dim.37), calls=%async_computation.1 | async-start | bytes 131072 | tf_op jit(solution)/shard_map/all_to_all | solution.py:21
  164.7 37.8 %copy-start = (bf16[96,96]{1,0:T(8,128)(2,1)S(1)}, bf16[96,96]{1,0:T(8,128)(2,1)}, u32[]{:S(2)}) copy-start(bf16[96,96]{1,0:T(8,128)(2,1)} %constant.51.clone) | copy-start | bytes 55300

commit v9 on v8

--- a/solution.py
+++ b/solution.py
@@ -35,22 +35,35 @@
     rows, cols = counts.shape
     scale = 1.0 / math.sqrt(rows * Y_HI * Z * CORE + cols * Y_LO * X)
 
-    pieces = jnp.stack([cell_totals >> shift & 2047 for shift in (0, 11, 22)])
-    extra = jnp.zeros((EXTRA, cols), I16).at[:3, :rows].set(pieces.astype(I16))
-    mine = jnp.concatenate([counts.astype(I16), extra])
-    other = lax.ppermute(mine, "y_hi", [(0, 1), (1, 0)])
+    def over_y(block):
+        return lax.ppermute(block, "y_hi", [(0, 1), (1, 0)])
 
-    test = spread(test_matrix.T, "z", Z)
-    ready, test = lax.optimization_barrier((gene_totals.reshape(8, -1), test))
+    def over_core(block):
+        return lax.all_gather(block, "core")
+
+    mine = counts.astype(I16)
+    other = over_y(mine)
+    ready, held = lax.optimization_barrier((gene_totals.reshape(8, -1), mine))
     totals = spread(ready, ("y_lo", "x"), Y_LO * X)
+
+    test, held = lax.optimization_barrier((test_matrix.T, held))
+    for axis in ("z_lo", "z_mid", "z_hi"):
+        test = lax.all_gather(test, axis)
+        if axis == "z_lo":
+            test, cell_totals = lax.optimization_barrier((test, cell_totals))
+            pieces = jnp.stack([cell_totals >> shift & 2047 for shift in (0, 11, 22)])
+            pieces = jnp.zeros((EXTRA, cols), I16).at[:3, :rows].set(pieces.astype(I16))
+            beyond = over_y(pieces)
+    test = test.reshape(Z * test_matrix.shape[1], cols)
+    own = over_core(jnp.concatenate([held, pieces]))
+
     test, totals = lax.optimization_barrier((test, totals))
-    test = test.reshape(Z * test_matrix.shape[1], cols)
-    total = jnp.sum(totals)
-    fraction = gene_totals.astype(F32) / total.astype(F32)
+    fraction = gene_totals.astype(F32) / jnp.sum(totals).astype(F32)
+    other = over_core(jnp.concatenate([other, beyond]))
 
     low = lax.axis_index("y_hi") == 0
-    pair = jnp.stack([jnp.where(low, mine, other), jnp.where(low, other, mine)])
-    blocks = lax.all_gather(pair, "core").reshape(BLOCKS, rows + EXTRA, cols)
+    blocks = jnp.stack([jnp.where(low, own, other), jnp.where(low, other, own)], axis=1)
+    blocks = blocks.reshape(BLOCKS, rows + EXTRA, cols)
     pieces = blocks[:, rows : rows + 3, :rows].astype(jnp.int32)
     owned = (pieces[:, 0] + (pieces[:, 1] << 11) + (pieces[:, 2] << 22)).astype(F32)
     expected = owned[:, :, None] * fraction[None, None, :]
@@ -68,7 +81,7 @@
 
     def gene_side(sketch):
         part = jnp.dot(sketch, stored, preferred_element_type=F32).astype(BF16)
-        return gather_sum(part, "z", Z, scale)
+        return gather_sum(part, ("z_hi", "z_mid", "z_lo"), Z, scale)
 
     sketch = cell_side(test, 1.0)
     for step in range(ITERS):
@@ -98,9 +111,10 @@
 
 def solution(mesh):
     fine = Mesh(
-        np.asarray(mesh.devices).reshape(Y_HI, Z, CORE, Y_LO, X), ("y_hi", "z", "core", "y_lo", "x")
+        np.asarray(mesh.devices).reshape(Y_HI, 2, 2, 2, CORE, Y_LO, X),
+        ("y_hi", "z_hi", "z_mid", "z_lo", "core", "y_lo", "x"),
     )
-    cell, gene = ("y_hi", "z", "core"), ("y_lo", "x")
+    cell, gene = ("y_hi", "z_hi", "z_mid", "z_lo", "core"), ("y_lo", "x")
     in_specs = (P(cell, gene), P(cell), P(gene), P(gene, cell))
     out_specs = (P(cell, None), P(gene, None))
     return jax.shard_map(shards, mesh=fine, in_specs=in_specs, out_specs=out_specs, check_vma=False)

time: 206 us -> 213 us (1.034)
  blocking collectives: 171 us -> 179 us
  waiting for transfers between devices: 7.25 us -> 0.01 us
  starting transfers between devices: 12.7 us -> 17.2 us
    all_gather x1 -> x5, blocking collectives: 6.5 us -> 27.7 us  [the longest x3 17.4 us: shards(): test = lax.all_gather(test, axis)]
    all_to_all x13 -> x12, blocking collectives: 140 us -> 124 us  [spread(): return lax.all_to_all(copies(x, n), axis, 0, 0)]
    all_to_all x1, waiting for transfers between devices: 7.24 us -> 0.01 us  [spread(): return lax.all_to_all(copies(x, n), axis, 0, 0)]
    all_to_all x1, blocking collectives: 24.4 us -> 27.3 us  [shards(): got = lax.all_to_all(send, ('core', 'y_hi'), 0, 0)]
    all_to_all x1, starting transfers between devices: 4.47 us -> 6.98 us  [spread(): return lax.all_to_all(copies(x, n), axis, 0, 0)]
    ppermute x1 -> x2, starting transfers between devices: 8.28 us -> 10.2 us  [over_y(): return lax.ppermute(block, 'y_hi', [(0, 1), (1, 0)])]
  transfers between devices with their start and end apart: 2 -> 3, of which waited for: 1 -> 0; matrix products, arithmetic and copies ran while one was open for 1% -> 1% of each run, Pallas kernels for 0% -> 0%
where the time goes in v9:
time: 213 us; the launch traced here: 211 us
  blocking collectives  179 us (84%)
  starting transfers between devices  17.2 us (8%)
  matrix products  5.8 us (3%)
  other arithmetic  5.37 us (3%)
    all_to_all x12, blocking collectives, spread(): return lax.all_to_all(copies(x, n), axis, 0, 0)  124 us
    all_to_all x1, blocking collectives, shards(): got = lax.all_to_all(send, ('core', 'y_hi'), 0, 0)  27.3 us
    all_gather x3, blocking collectives, shards(): test = lax.all_gather(test, axis)  17.4 us
    all_gather x2, blocking collectives, over_core(): return lax.all_gather(block, 'core')  10.2 us
    ppermute x2, starting transfers between devices, over_y(): return lax.ppermute(block, 'y_hi', [(0, 1), (1, 0)])  10.2 us
    all_to_all x1, starting transfers between devices, spread(): return lax.all_to_all(copies(x, n), axis, 0, 0)  6.98 us
  transfers between devices with their start and end apart: 3, of which 0 were waited for; matrix products, arithmetic and copies ran while one was open for 1% of the time, Pallas kernels for 0%

profile of v9, /device:TPU:1, one launch (start us, length us, event | category | flops | bytes accessed | tf_op | source)
XLA Modules:
  0.0 211.1 jit_solution(6539582270810448544)
XLA Ops:
  0.6 1.3 convert_element_type.392
  1.9 0.0 copy-start.1
  1.9 8.3 %collective-permute-start = (s16[256,1024]{1,0:T(8,128)(2,1)S(1)}, s16[256,1024]{1,0:T(8,128)(2,1)S(1)}, u32[]{:S(2)}, u32[]{:S(2)}) collective-permute-start(s16[256,1024]{1,0:T(8,128)(2,1)S(1)} %convert_element_type.392), channel_id=1, source_target_pairs={{0,256},{256,0},{1,257},{257,1},{2,258},{258,2},{3,259},{259,3},{4... | collective-permute-start | bytes 1572872 | tf_op jit(solution)/shard_map/ppermute | solution.py:39
  10.2 4.1 %all-gather.5 = bf16[2,3,1024]{2,1,0:T(4,128)(2,1)S(1)} all-gather(bf16[1,3,1024]{2,1,0:T(4,128)(2,1)} %bitcast.79), channel_id=2, replica_groups=mesh['y_hi'=2,'z_hi'=2,'z_mid'=2,'z_lo'=2,'core'=2,'y_lo'=4,'x'=4] {'z_lo'}, dimensions={0}, use_global_device_ids=true | all-gather | bytes 18432 | tf_op jit(solution)/shard_map/all_gather | solution.py:51
  14.3 0.7 and_convert_fusion.2
  15.1 1.9 collective-permute-start.1
  17.0 1.3 broadcast_in_dim.34
  18.3 7.0 %all-to-all-start = ((s32[16,8,128]{2,1,0:T(8,128)}), s32[16,8,128]{2,1,0:T(8,128)S(1)}, u32[]{:S(2)}, u32[]{:S(2)}) async-start(s32[16,8,128]{2,1,0:T(8,128)} %broadcast_in_dim.34), calls=%async_computation | async-start | bytes 131072 | tf_op jit(solution)/shard_map/all_to_all | solution.py:21
  25.4 5.6 %all-gather.8 = s16[528,1024]{1,0:T(8,128)(2,1)S(1)} all-gather(s16[264,1024]{1,0:T(8,128)(2,1)S(1)} %pad_add_fusion.1), channel_id=5, replica_groups=mesh['y_hi'=2,'z_hi'=2,'z_mid'=2,'z_lo'=2,'core'=2,'y_lo'=4,'x'=4] {'core'}, dimensions={0}, use_global_device_ids=true | all-gather | bytes 1622016 | tf_op jit(solution)/shard_map/all_gather | solution.py:42
  31.0 4.9 %all-gather.1 = bf16[4,3,1024]{2,1,0:T(4,128)(2,1)S(1)} all-gather(bf16[2,3,1024]{2,1,0:T(4,128)(2,1)S(1)} %all-gather.5), channel_id=3, replica_groups=mesh['y_hi'=2,'z_hi'=2,'z_mid'=2,'z_lo'=2,'core'=2,'y_lo'=4,'x'=4] {'z_m..., dimensions={0}, use_global_device_ids=true | all-gather | bytes 36864 | tf_op jit(solution)/shard_map/all_gather | solution.py:51
  35.9 8.4 %all-gather.2 = bf16[4,2,3,1024]{3,1,2,0:T(2,128)(2,1)S(1)} all-gather(bf16[2,2,3,1024]{3,1,2,0:T(2,128)(2,1)S(1)} %copy.7), channel_id=4, replica_groups=mesh['y_hi'=2,'z_hi'=2,'z_mid'=2,'z_lo'=2,'core'=2,'y_lo'=4,'x'=4] {'z_hi'}, dimensions={0}, use_global_device_ids=true | all-gather | bytes 73728 | tf_op jit(solution)/shard_map/all_gather | solution.py:51
  44.4 0.0 all-to-all-done
  44.4 0.6 reduce_sum.9
  45.7 0.0 copy-done.1
  45.8 0.0 collective-permute-done.1
  45.8 0.0 collective-permute-done
  45.8 4.6 %all-gather.9 = s16[528,1024]{1,0:T(8,128)(2,1)S(1)} all-gather(s16[264,1024]{1,0:T(8,128)(2,1)S(1)} %pad_add_fusion.2), channel_id=6, replica_groups=mesh['y_hi'=2,'z_hi'=2,'z_mid'=2,'z_lo'=2,'core'=2,'y_lo'=4,'x'=4] {'core'}, dimensions={0}, use_global_device_ids=true | all-gather | bytes 1622016 | tf_op jit(solution)/shard_map/all_gather | solution.py:42
  50.4 0.6 broadcast_select_fusion.1
  51.0 0.2 pad_add_fusion
  51.3 1.6 fusion.1
  52.9 0.7 convolution_convert_fusion.9
  53.6 9.5 %all_to_all.70 = bf16[4,24,1024]{2,1,0:T(8,128)(2,1)S(1)} all-to-all(bf16[4,24,1024]{2,1,0:T(8,128)(2,1)S(1)} %broadcast_in_dim.35), channel_id=1, replica_groups=mesh['y_hi'=2,'z_hi'=2,'z_mid'=2,'z_lo'=2,'core'=2,'y_lo'=4,'x'=4] {'x'}, dimensions={0} | all-to-all | bytes 393216 | tf_op jit(solution)/shard_map/all_to_all | solution.py:21
  63.1 9.8 %all_to_all.71 = bf16[4,24,1024]{2,1,0:T(8,128)(2,1)S(1)} all-to-all(bf16[4,24,1024]{2,1,0:T(8,128)(2,1)S(1)} %broadcast_in_dim.37), channel_id=1, replica_groups=mesh['y_hi'=2,'z_hi'=2,'z_mid'=2,'z_lo'=2,'core'=2,'y_lo'=4,'x'=4] {'y_lo'}, dimensions={0} | all-to-all | bytes 393216 | tf_op jit(solution)/shard_map/all_to_all | solution.py:21
  72.9 0.4 convolution_convert_fusion.8
  73.4 18.1 %all_to_all.72 = bf16[8,24,1024]{2,1,0:T(8,128)(2,1)S(1)} all-to-all(bf16[8,24,1024]{2,1,0:T(8,128)(2,1)S(1)} %broadcast_in_dim.38), channel_id=1, replica_groups=mesh['y_hi'=2,'z_hi'=2,'z_mid'=2,'z_lo'=2,'core'=2,'y_lo'=4,'x'=4] {'z_h..., dimensions={0} | all-to-all | bytes 786432 | tf_op jit(solution)/shard_map/all_to_all | solution.py:21
  91.5 0.7 convolution_convert_fusion.7
  92.2 7.5 %all_to_all.73 = bf16[4,24,1024]{2,1,0:T(8,128)(2,1)S(1)} all-to-all(bf16[4,24,1024]{2,1,0:T(8,128)(2,1)S(1)} %broadcast_in_dim.39), channel_id=1, replica_groups=mesh['y_hi'=2,'z_hi'=2,'z_mid'=2,'z_lo'=2,'core'=2,'y_lo'=4,'x'=4] {'x'}, dimensions={0} | all-to-all | bytes 393216 | tf_op jit(solution)/shard_map/all_to_all | solution.py:21
  99.8 8.0 %all_to_all.74 = bf16[4,24,1024]{2,1,0:T(8,128)(2,1)S(1)} all-to-all(bf16[4,24,1024]{2,1,0:T(8,128)(2,1)S(1)} %broadcast_in_dim.41), channel_id=1, replica_groups=mesh['y_hi'=2,'z_hi'=2,'z_mid'=2,'z_lo'=2,'core'=2,'y_lo'=4,'x'=4] {'y_lo'}, dimensions={0} | all-to-all | bytes 393216 | tf_op jit(solution)/shard_map/all_to_all | solution.py:21
  107.8 0.4 convolution_convert_fusion.6
  108.2 13.5 %all_to_all.75 = bf16[8,24,1024]{2,1,0:T(8,128)(2,1)S(1)} all-to-all(bf16[8,24,1024]{2,1,0:T(8,128)(2,1)S(1)} %broadcast_in_dim.42), channel_id=1, replica_groups=mesh['y_hi'=2,'z_hi'=2,'z_mid'=2,'z_lo'=2,'core'=2,'y_lo'=4,'x'=4] {'z_h..., dimensions={0} | all-to-all | bytes 786432 | tf_op jit(solution)/shard_map/all_to_all | solution.py:21
  121.7 0.7 convolution_convert_fusion.5
  122.4 7.5 %all_to_all.76 = bf16[4,24,1024]{2,1,0:T(8,128)(2,1)S(1)} all-to-all(bf16[4,24,1024]{2,1,0:T(8,128)(2,1)S(1)} %broadcast_in_dim.43), channel_id=1, replica_groups=mesh['y_hi'=2,'z_hi'=2,'z_mid'=2,'z_lo'=2,'core'=2,'y_lo'=4,'x'=4] {'x'}, dimensions={0} | all-to-all | bytes 393216 | tf_op jit(solution)/shard_map/all_to_all | solution.py:21
  130.0 8.2 %all_to_all.77 = bf16[4,24,1024]{2,1,0:T(8,128)(2,1)S(1)} all-to-all(bf16[4,24,1024]{2,1,0:T(8,128)(2,1)S(1)} %broadcast_in_dim.45), channel_id=1, replica_groups=mesh['y_hi'=2,'z_hi'=2,'z_mid'=2,'z_lo'=2,'core'=2,'y_lo'=4,'x'=4] {'y_lo'}, dimensions={0} | all-to-all | bytes 393216 | tf_op jit(solution)/shard_map/all_to_all | solution.py:21
  138.2 0.4 convolution_convert_fusion.4
  138.6 13.1 %all_to_all.78 = bf16[8,24,1024]{2,1,0:T(8,128)(2,1)S(1)} all-to-all(bf16[8,24,1024]{2,1,0:T(8,128)(2,1)S(1)} %broadcast_in_dim.46), channel_id=1, replica_groups=mesh['y_hi'=2,'z_hi'=2,'z_mid'=2,'z_lo'=2,'core'=2,'y_lo'=4,'x'=4] {'z_h..., dimensions={0} | all-to-all | bytes 786432 | tf_op jit(solution)/shard_map/all_to_all | solution.py:21
  151.8 0.7 convolution_convert_fusion.3
  152.4 7.8 %all_to_all.79 = bf16[4,24,1024]{2,1,0:T(8,128)(2,1)S(1)} all-to-all(bf16[4,24,1024]{2,1,0:T(8,128)(2,1)S(1)} %broadcast_in_dim.47), channel_id=1, replica_groups=mesh['y_hi'=2,'z_hi'=2,'z_mid'=2,'z_lo'=2,'core'=2,'y_lo'=4,'x'=4] {'x'}, dimensions={0} | all-to-all | bytes 393216 | tf_op jit(solution)/shard_map/all_to_all | solution.py:21
  160.3 8.0 %all_to_all.80 = bf16[4,24,1024]{2,1,0:T(8,128)(2,1)S(1)} all-to-all(bf16[4,24,1024]{2,1,0:T(8,128)(2,1)S(1)} %broadcast_in_dim.49), channel_id=1, replica_groups=mesh['y_hi'=2,'z_hi'=2,'z_mid'=2,'z_lo'=2,'core'=2,'y_lo'=4,'x'=4] {'y_lo'}, dimensions={0} | all-to-all | bytes 393216 | tf_op jit(solution)/shard_map/all_to_all | solution.py:21
  168.4 0.4 convolution_convert_fusion.2
  168.8 0.0 copy-start
  168.8 13.1 %all_to_all.81 = bf16[8,24,1024]{2,1,0:T(8,128)(2,1)S(1)} all-to-all(bf16[8,24,1024]{2,1,0:T(8,128)(2,1)S(1)} %broadcast_in_dim.50), channel_id=1, replica_groups=mesh['y_hi'=2,'z_hi'=2,'z_mid'=2,'z_lo'=2,'core'=2,'y_lo'=4,'x'=4] {'z_h..., dimensions={0} | all-to-all | bytes 786432 | tf_op jit(solution)/shard_map/all_to_all | solution.py:21
  182.0 0.1 fusion.22
  182.1 27.3 %all_to_all.82 = bf16[4,24,1280]{2,1,0:T(8,128)(2,1)S(1)} all-to-all(bf16[4,24,1280]{2,1,0:T(8,128)(2,1)S(1)} %pad_maximum_fusion), channel_id=1, replica_groups=mesh['y_hi'=2,'z_hi'=2,'z_mid'=2,'z_lo'=2,'core'=2,'y_lo'=4,'x'=4] {'cor..., dimensions={0} | all-to-all | bytes 491520 | tf_op jit(solution)/shard_map/all_to_all | solution.py:103
  209.4 0.0 copy-done
  209.4 0.9 convolution_convert_fusion
  210.3 0.8 convolution_convert_fusion.1
  (34 shorter events, 0.8 us)
Async XLA Ops:
  1.9 43.8 %copy-start.1 = (s32[1024]{0:T(1024)S(1)}, s32[1024]{0:T(1024)}, u32[]{:S(2)}) copy-start(s32[1024]{0:T(1024)} %param.9) | copy-start | bytes 12292
  1.9 43.8 %collective-permute-start = (s16[256,1024]{1,0:T(8,128)(2,1)S(1)}, s16[256,1024]{1,0:T(8,128)(2,1)S(1)}, u32[]{:S(2)}, u32[]{:S(2)}) collective-permute-start(s16[256,1024]{1,0:T(8,128)(2,1)S(1)} %convert_element_type.392), channel_id=1, source_target_pairs={{0,256},{256,0},{1,257},{257,1},{2,258},{258,2},{3,259},{259,3},{4... | collective-permute-start | bytes 1572872 | tf_op jit(solution)/shard_map/ppermute | solution.py:39
  15.1 30.7 %collective-permute-start.1 = (s16[8,1024]{1,0:T(8,128)(2,1)S(1)}, s16[8,1024]{1,0:T(8,128)(2,1)S(1)}, u32[]{:S(2)}, u32[]{:S(2)}) collective-permute-start(s16[8,1024]{1,0:T(8,128)(2,1)S(1)} %scatter.4), channel_id=1, source_target_pairs={{0,256},{256,0},{1,257},{257,1},{2,258},{258,2},{3,259},{259,3},{4... | collective-permute-start | bytes 49160 | tf_op jit(solution)/shard_map/ppermute | solution.py:39
  18.3 26.1 %all-to-all-start = ((s32[16,8,128]{2,1,0:T(8,128)}), s32[16,8,128]{2,1,0:T(8,128)S(1)}, u32[]{:S(2)}, u32[]{:S(2)}) async-start(s32[16,8,128]{2,1,0:T(8,128)} %broadcast_in_dim.34), calls=%async_computation | async-start | bytes 131072 | tf_op jit(solution)/shard_map/all_to_all | solution.py:21
  168.8 40.7 %copy-start = (bf16[96,96]{1,0:T(8,128)(2,1)S(1)}, bf16[96,96]{1,0:T(8,128)(2,1)}, u32[]{:S(2)}) copy-start(bf16[96,96]{1,0:T(8,128)(2,1)} %constant.51.clone) | copy-start | bytes 55300

commit v10 on v8

--- a/solution.py
+++ b/solution.py
@@ -35,22 +35,24 @@
     rows, cols = counts.shape
     scale = 1.0 / math.sqrt(rows * Y_HI * Z * CORE + cols * Y_LO * X)
 
+    low = lax.axis_index("y_hi") == 0
     pieces = jnp.stack([cell_totals >> shift & 2047 for shift in (0, 11, 22)])
     extra = jnp.zeros((EXTRA, cols), I16).at[:3, :rows].set(pieces.astype(I16))
+    extra = extra.at[3].set(low.astype(I16))
     mine = jnp.concatenate([counts.astype(I16), extra])
     other = lax.ppermute(mine, "y_hi", [(0, 1), (1, 0)])
 
     test = spread(test_matrix.T, "z", Z)
     ready, test = lax.optimization_barrier((gene_totals.reshape(8, -1), test))
     totals = spread(ready, ("y_lo", "x"), Y_LO * X)
-    test, totals = lax.optimization_barrier((test, totals))
+
+    pair = jnp.stack([jnp.where(low, mine, other), jnp.where(low, other, mine)])
+    blocks = lax.all_gather(pair, "core").reshape(BLOCKS, rows + EXTRA, cols)
+    test, totals, blocks = lax.optimization_barrier((test, totals, blocks))
     test = test.reshape(Z * test_matrix.shape[1], cols)
     total = jnp.sum(totals)
     fraction = gene_totals.astype(F32) / total.astype(F32)
 
-    low = lax.axis_index("y_hi") == 0
-    pair = jnp.stack([jnp.where(low, mine, other), jnp.where(low, other, mine)])
-    blocks = lax.all_gather(pair, "core").reshape(BLOCKS, rows + EXTRA, cols)
     pieces = blocks[:, rows : rows + 3, :rows].astype(jnp.int32)
     owned = (pieces[:, 0] + (pieces[:, 1] << 11) + (pieces[:, 2] << 22)).astype(F32)
     expected = owned[:, :, None] * fraction[None, None, :]

time: 206 us -> 208 us (level)
  blocking collectives: 171 us -> 178 us
  waiting for transfers between devices: 7.25 us -> 1.54 us
    all_to_all x1, waiting for transfers between devices: 7.24 us -> 1.53 us  [spread(): return lax.all_to_all(copies(x, n), axis, 0, 0)]
    all_to_all x1, blocking collectives: 24.4 us -> 29.9 us  [shards(): got = lax.all_to_all(send, ('core', 'y_hi'), 0, 0)]
    all_to_all x13, blocking collectives: 140 us -> 142 us  [spread(): return lax.all_to_all(copies(x, n), axis, 0, 0)]
  transfers between devices with their start and end apart: 2 -> 2, of which waited for: 1 -> 1; matrix products, arithmetic and copies ran while one was open for 1% -> 0% of each run, Pallas kernels for 0% -> 0%
where the time goes in v10:
time: 208 us; the launch traced here: 205 us
  blocking collectives  178 us (86%)
  starting transfers between devices  12.7 us (6%)
  matrix products  5.79 us (3%)
  other arithmetic  4.89 us (2%)
    all_to_all x13, blocking collectives, spread(): return lax.all_to_all(copies(x, n), axis, 0, 0)  142 us
    all_to_all x1, blocking collectives, shards(): got = lax.all_to_all(send, ('core', 'y_hi'), 0, 0)  29.9 us
    ppermute x1, starting transfers between devices, shards(): other = lax.ppermute(mine, 'y_hi', [(0, 1), (1, 0)])  8.28 us
    all_gather x1, blocking collectives, shards(): blocks = lax.all_gather(pair, 'core').reshape(BLOCKS, rows + EXTRA, cols)  5.35 us
    all_to_all x1, starting transfers between devices, spread(): return lax.all_to_all(copies(x, n), axis, 0, 0)  4.47 us
  transfers between devices with their start and end apart: 2, of which 1 were waited for; matrix products, arithmetic and copies ran while one was open for 0% of the time, Pallas kernels for 0%

profile of v10, /device:TPU:1, one launch (start us, length us, event | category | flops | bytes accessed | tf_op | source)
XLA Modules:
  0.0 205.3 jit_solution(498648463760636244)
XLA Ops:
  0.6 0.0 copy-start.2
  0.6 0.0 copy-start.1
  0.7 0.7 and_convert_fusion.2
  1.4 1.3 convert_element_type.395
  2.7 0.1 scatter.9
  2.8 8.3 %collective-permute-start = (s16[264,1024]{1,0:T(8,128)(2,1)S(1)}, s16[264,1024]{1,0:T(8,128)(2,1)S(1)}, u32[]{:S(2)}, u32[]{:S(2)}) collective-permute-start(s16[264,1024]{1,0:T(8,128)(2,1)S(1)} %pad_add_fusion.1), channel_id=1, source_target_pairs={{0,256},{256,0},{1,257},{257,1},{2,258},{258,2},{3,259},{259,3},{4... | collective-permute-start | bytes 1622024 | tf_op jit(solution)/shard_map/ppermute | solution.py:43
  11.1 0.0 copy-done.2
  11.2 17.4 %all_to_all.75 = bf16[8,3,1024]{2,1,0:T(4,128)(2,1)S(1)} all-to-all(bf16[8,3,1024]{2,1,0:T(4,128)(2,1)S(1)} %broadcast_in_dim.36), channel_id=1, replica_groups=mesh['y_hi'=2,'z'=8,'core'=2,'y_lo'=4,'x'=4] {'z'}, dimensions={0} | all-to-all | bytes 98304 | tf_op jit(solution)/shard_map/all_to_all | solution.py:21
  28.5 0.0 copy-done.1
  28.5 0.6 broadcast_in_dim.37
  29.2 4.5 %all-to-all-start.1 = ((s32[16,8,128]{2,1,0:T(8,128)}), s32[16,8,128]{2,1,0:T(8,128)S(1)}, u32[]{:S(2)}, u32[]{:S(2)}) async-start(s32[16,8,128]{2,1,0:T(8,128)} %broadcast_in_dim.37), calls=%async_computation.1 | async-start | bytes 131072 | tf_op jit(solution)/shard_map/all_to_all | solution.py:21
  33.6 0.0 collective-permute-done
  33.6 0.3 select_bitcast_fusion.1
  33.9 0.1 pad_add_fusion
  34.0 5.3 %all-gather.2 = s16[4,264,1024]{2,1,0:T(8,128)(2,1)S(1)} all-gather(s16[2,264,1024]{2,1,0:T(8,128)(2,1)S(1)} %pad_add_fusion), channel_id=2, replica_groups=mesh['y_hi'=2,'z'=8,'core'=2,'y_lo'=4,'x'=4] {'core'}, dimensions={0}, use_global_device_ids=true | all-gather | bytes 3244032 | tf_op jit(solution)/shard_map/all_gather | solution.py:50
  39.3 1.5 all-to-all-done.1
  40.9 0.6 reduce_sum.9
  42.3 1.6 fusion.1
  43.9 0.7 convolution_convert_fusion.9
  44.6 7.9 %all_to_all.76 = bf16[4,24,1024]{2,1,0:T(8,128)(2,1)S(1)} all-to-all(bf16[4,24,1024]{2,1,0:T(8,128)(2,1)S(1)} %broadcast_in_dim.38), channel_id=1, replica_groups=mesh['y_hi'=2,'z'=8,'core'=2,'y_lo'=4,'x'=4] {'x'}, dimensions={0} | all-to-all | bytes 393216 | tf_op jit(solution)/shard_map/all_to_all | solution.py:21
  52.5 9.8 %all_to_all.77 = bf16[4,24,1024]{2,1,0:T(8,128)(2,1)S(1)} all-to-all(bf16[4,24,1024]{2,1,0:T(8,128)(2,1)S(1)} %broadcast_in_dim.40), channel_id=1, replica_groups=mesh['y_hi'=2,'z'=8,'core'=2,'y_lo'=4,'x'=4] {'y_lo'}, dimensions={0} | all-to-all | bytes 393216 | tf_op jit(solution)/shard_map/all_to_all | solution.py:21
  62.3 0.4 convolution_convert_fusion.8
  62.7 20.4 %all_to_all.78 = bf16[8,24,1024]{2,1,0:T(8,128)(2,1)S(1)} all-to-all(bf16[8,24,1024]{2,1,0:T(8,128)(2,1)S(1)} %broadcast_in_dim.41), channel_id=1, replica_groups=mesh['y_hi'=2,'z'=8,'core'=2,'y_lo'=4,'x'=4] {'z'}, dimensions={0} | all-to-all | bytes 786432 | tf_op jit(solution)/shard_map/all_to_all | solution.py:21
  83.2 0.7 convolution_convert_fusion.7
  83.9 7.5 %all_to_all.79 = bf16[4,24,1024]{2,1,0:T(8,128)(2,1)S(1)} all-to-all(bf16[4,24,1024]{2,1,0:T(8,128)(2,1)S(1)} %broadcast_in_dim.42), channel_id=1, replica_groups=mesh['y_hi'=2,'z'=8,'core'=2,'y_lo'=4,'x'=4] {'x'}, dimensions={0} | all-to-all | bytes 393216 | tf_op jit(solution)/shard_map/all_to_all | solution.py:21
  91.5 8.0 %all_to_all.80 = bf16[4,24,1024]{2,1,0:T(8,128)(2,1)S(1)} all-to-all(bf16[4,24,1024]{2,1,0:T(8,128)(2,1)S(1)} %broadcast_in_dim.44), channel_id=1, replica_groups=mesh['y_hi'=2,'z'=8,'core'=2,'y_lo'=4,'x'=4] {'y_lo'}, dimensions={0} | all-to-all | bytes 393216 | tf_op jit(solution)/shard_map/all_to_all | solution.py:21
  99.5 0.4 convolution_convert_fusion.6
  99.9 13.5 %all_to_all.81 = bf16[8,24,1024]{2,1,0:T(8,128)(2,1)S(1)} all-to-all(bf16[8,24,1024]{2,1,0:T(8,128)(2,1)S(1)} %broadcast_in_dim.45), channel_id=1, replica_groups=mesh['y_hi'=2,'z'=8,'core'=2,'y_lo'=4,'x'=4] {'z'}, dimensions={0} | all-to-all | bytes 786432 | tf_op jit(solution)/shard_map/all_to_all | solution.py:21
  113.4 0.7 convolution_convert_fusion.5
  114.1 7.5 %all_to_all.82 = bf16[4,24,1024]{2,1,0:T(8,128)(2,1)S(1)} all-to-all(bf16[4,24,1024]{2,1,0:T(8,128)(2,1)S(1)} %broadcast_in_dim.46), channel_id=1, replica_groups=mesh['y_hi'=2,'z'=8,'core'=2,'y_lo'=4,'x'=4] {'x'}, dimensions={0} | all-to-all | bytes 393216 | tf_op jit(solution)/shard_map/all_to_all | solution.py:21
  121.7 8.2 %all_to_all.83 = bf16[4,24,1024]{2,1,0:T(8,128)(2,1)S(1)} all-to-all(bf16[4,24,1024]{2,1,0:T(8,128)(2,1)S(1)} %broadcast_in_dim.48), channel_id=1, replica_groups=mesh['y_hi'=2,'z'=8,'core'=2,'y_lo'=4,'x'=4] {'y_lo'}, dimensions={0} | all-to-all | bytes 393216 | tf_op jit(solution)/shard_map/all_to_all | solution.py:21
  129.9 0.4 convolution_convert_fusion.4
  130.4 13.1 %all_to_all.84 = bf16[8,24,1024]{2,1,0:T(8,128)(2,1)S(1)} all-to-all(bf16[8,24,1024]{2,1,0:T(8,128)(2,1)S(1)} %broadcast_in_dim.49), channel_id=1, replica_groups=mesh['y_hi'=2,'z'=8,'core'=2,'y_lo'=4,'x'=4] {'z'}, dimensions={0} | all-to-all | bytes 786432 | tf_op jit(solution)/shard_map/all_to_all | solution.py:21
  143.5 0.7 convolution_convert_fusion.3
  144.2 7.8 %all_to_all.85 = bf16[4,24,1024]{2,1,0:T(8,128)(2,1)S(1)} all-to-all(bf16[4,24,1024]{2,1,0:T(8,128)(2,1)S(1)} %broadcast_in_dim.50), channel_id=1, replica_groups=mesh['y_hi'=2,'z'=8,'core'=2,'y_lo'=4,'x'=4] {'x'}, dimensions={0} | all-to-all | bytes 393216 | tf_op jit(solution)/shard_map/all_to_all | solution.py:21
  152.1 8.0 %all_to_all.86 = bf16[4,24,1024]{2,1,0:T(8,128)(2,1)S(1)} all-to-all(bf16[4,24,1024]{2,1,0:T(8,128)(2,1)S(1)} %broadcast_in_dim.52), channel_id=1, replica_groups=mesh['y_hi'=2,'z'=8,'core'=2,'y_lo'=4,'x'=4] {'y_lo'}, dimensions={0} | all-to-all | bytes 393216 | tf_op jit(solution)/shard_map/all_to_all | solution.py:21
  160.1 0.4 convolution_convert_fusion.2
  160.5 0.0 copy-start
  160.6 13.1 %all_to_all.87 = bf16[8,24,1024]{2,1,0:T(8,128)(2,1)S(1)} all-to-all(bf16[8,24,1024]{2,1,0:T(8,128)(2,1)S(1)} %broadcast_in_dim.53), channel_id=1, replica_groups=mesh['y_hi'=2,'z'=8,'core'=2,'y_lo'=4,'x'=4] {'z'}, dimensions={0} | all-to-all | bytes 786432 | tf_op jit(solution)/shard_map/all_to_all | solution.py:21
  173.7 0.1 fusion.22
  173.8 29.9 %all_to_all.88 = bf16[4,24,1280]{2,1,0:T(8,128)(2,1)S(1)} all-to-all(bf16[4,24,1280]{2,1,0:T(8,128)(2,1)S(1)} %pad_maximum_fusion), channel_id=1, replica_groups=mesh['y_hi'=2,'z'=8,'core'=2,'y_lo'=4,'x'=4] {'core','y_hi'}, dimensions={0} | all-to-all | bytes 491520 | tf_op jit(solution)/shard_map/all_to_all | solution.py:92
  203.7 0.0 copy-done
  203.7 0.8 convolution_convert_fusion.1
  204.5 0.9 convolution_convert_fusion
  (33 shorter events, 0.7 us)
Async XLA Ops:
  0.6 10.5 %copy-start.2 = (bf16[1024,3]{0,1:T(4,128)(2,1)S(1)}, bf16[1024,3]{0,1:T(4,128)(2,1)}, u32[]{:S(2)}) copy-start(bf16[1024,3]{0,1:T(4,128)(2,1)} %param.12) | copy-start | bytes 18436
  0.6 27.9 %copy-start.1 = (s32[1024]{0:T(1024)S(1)}, s32[1024]{0:T(1024)}, u32[]{:S(2)}) copy-start(s32[1024]{0:T(1024)} %param.11) | copy-start | bytes 12292
  2.8 30.8 %collective-permute-start = (s16[264,1024]{1,0:T(8,128)(2,1)S(1)}, s16[264,1024]{1,0:T(8,128)(2,1)S(1)}, u32[]{:S(2)}, u32[]{:S(2)}) collective-permute-start(s16[264,1024]{1,0:T(8,128)(2,1)S(1)} %pad_add_fusion.1), channel_id=1, source_target_pairs={{0,256},{256,0},{1,257},{257,1},{2,258},{258,2},{3,259},{259,3},{4... | collective-permute-start | bytes 1622024 | tf_op jit(solution)/shard_map/ppermute | solution.py:43
  29.2 11.7 %all-to-all-start.1 = ((s32[16,8,128]{2,1,0:T(8,128)}), s32[16,8,128]{2,1,0:T(8,128)S(1)}, u32[]{:S(2)}, u32[]{:S(2)}) async-start(s32[16,8,128]{2,1,0:T(8,128)} %broadcast_in_dim.37), calls=%async_computation.1 | async-start | bytes 131072 | tf_op jit(solution)/shard_map/all_to_all | solution.py:21
  160.5 43.2 %copy-start = (bf16[96,96]{1,0:T(8,128)(2,1)S(1)}, bf16[96,96]{1,0:T(8,128)(2,1)}, u32[]{:S(2)}) copy-start(bf16[96,96]{1,0:T(8,128)(2,1)} %constant.79.clone) | copy-start | bytes 55300

commit v11 on v8

--- a/solution.py
+++ b/solution.py
@@ -42,7 +42,7 @@
 
     test = spread(test_matrix.T, "z", Z)
     ready, test = lax.optimization_barrier((gene_totals.reshape(8, -1), test))
-    totals = spread(ready, ("y_lo", "x"), Y_LO * X)
+    totals = spread(jnp.sum(ready, axis=0, keepdims=True), ("y_lo", "x"), Y_LO * X)
     test, totals = lax.optimization_barrier((test, totals))
     test = test.reshape(Z * test_matrix.shape[1], cols)
     total = jnp.sum(totals)

time: 206 us -> 206 us (level)
  no operation moved by 1% of the time
where the time goes in v11:
time: 206 us; the launch traced here: 203 us
  blocking collectives  171 us (83%)
  starting transfers between devices  12.7 us (6%)
  waiting for transfers between devices  6.68 us (3%)
  matrix products  5.79 us (3%)
  other arithmetic  4.92 us (2%)
    all_to_all x13, blocking collectives, spread(): return lax.all_to_all(copies(x, n), axis, 0, 0)  140 us
    all_to_all x1, blocking collectives, shards(): got = lax.all_to_all(send, ('core', 'y_hi'), 0, 0)  24.2 us
    ppermute x1, starting transfers between devices, shards(): other = lax.ppermute(mine, 'y_hi', [(0, 1), (1, 0)])  8.28 us
    all_to_all x1, waiting for transfers between devices, spread(): return lax.all_to_all(copies(x, n), axis, 0, 0)  6.68 us
    all_gather x1, blocking collectives, shards(): blocks = lax.all_gather(pair, 'core').reshape(BLOCKS, rows + EXTRA, cols)  6.5 us
    all_to_all x1, starting transfers between devices, spread(): return lax.all_to_all(copies(x, n), axis, 0, 0)  4.47 us
  transfers between devices with their start and end apart: 2, of which 1 were waited for; matrix products, arithmetic and copies ran while one was open for 1% of the time, Pallas kernels for 0%

profile of v11, /device:TPU:1, one launch (start us, length us, event | category | flops | bytes accessed | tf_op | source)
XLA Modules:
  0.0 203.4 jit_solution(7711735981865422517)
XLA Ops:
  0.6 0.0 copy-start.2
  0.6 0.0 copy-start.1
  0.7 0.7 and_convert_fusion.2
  1.4 1.3 convert_element_type.392
  2.7 8.3 %collective-permute-start = (s16[264,1024]{1,0:T(8,128)(2,1)S(1)}, s16[264,1024]{1,0:T(8,128)(2,1)S(1)}, u32[]{:S(2)}, u32[]{:S(2)}) collective-permute-start(s16[264,1024]{1,0:T(8,128)(2,1)S(1)} %pad_add_fusion.1), channel_id=1, source_target_pairs={{0,256},{256,0},{1,257},{257,1},{2,258},{258,2},{3,259},{259,3},{4... | collective-permute-start | bytes 1622024 | tf_op jit(solution)/shard_map/ppermute | solution.py:41
  11.0 0.0 copy-done.2
  11.1 17.4 %all_to_all.75 = bf16[8,3,1024]{2,1,0:T(4,128)(2,1)S(1)} all-to-all(bf16[8,3,1024]{2,1,0:T(4,128)(2,1)S(1)} %broadcast_in_dim.36), channel_id=1, replica_groups=mesh['y_hi'=2,'z'=8,'core'=2,'y_lo'=4,'x'=4] {'z'}, dimensions={0} | all-to-all | bytes 98304 | tf_op jit(solution)/shard_map/all_to_all | solution.py:21
  28.4 0.0 copy-done.1
  28.4 0.6 broadcast_in_dim.37
  29.0 4.5 %all-to-all-start.1 = ((s32[16,1,128]{2,1,0:T(1,128)}), s32[16,1,128]{2,1,0:T(1,128)S(1)}, u32[]{:S(2)}, u32[]{:S(2)}) async-start(s32[16,1,128]{2,1,0:T(1,128)} %broadcast_in_dim.37), calls=%async_computation.1 | async-start | bytes 16384 | tf_op jit(solution)/shard_map/all_to_all | solution.py:21
  33.5 6.7 %all-to-all-done.1 = s32[16,1,128]{2,1,0:T(1,128)S(1)} async-done(((s32[16,1,128]{2,1,0:T(1,128)}), s32[16,1,128]{2,1,0:T(1,128)S(1)}, u32[]{:S(2)}, u32[]{:S(2)}) %all-to-all-start.1) | async-done | bytes 8224 | tf_op jit(solution)/shard_map/all_to_all | solution.py:21
  40.2 0.6 reduce_sum.19
  41.6 0.0 collective-permute-done
  41.6 0.3 select_bitcast_fusion.1
  41.8 0.1 pad_add_fusion
  41.9 6.5 %all-gather.2 = s16[4,264,1024]{2,1,0:T(8,128)(2,1)S(1)} all-gather(s16[2,264,1024]{2,1,0:T(8,128)(2,1)S(1)} %pad_add_fusion), channel_id=2, replica_groups=mesh['y_hi'=2,'z'=8,'core'=2,'y_lo'=4,'x'=4] {'core'}, dimensions={0}, use_global_device_ids=true | all-gather | bytes 3244032 | tf_op jit(solution)/shard_map/all_gather | solution.py:53
  48.5 1.6 fusion.1
  50.1 0.7 convolution_convert_fusion.9
  50.7 7.8 %all_to_all.76 = bf16[4,24,1024]{2,1,0:T(8,128)(2,1)S(1)} all-to-all(bf16[4,24,1024]{2,1,0:T(8,128)(2,1)S(1)} %broadcast_in_dim.38), channel_id=1, replica_groups=mesh['y_hi'=2,'z'=8,'core'=2,'y_lo'=4,'x'=4] {'x'}, dimensions={0} | all-to-all | bytes 393216 | tf_op jit(solution)/shard_map/all_to_all | solution.py:21
  58.6 8.0 %all_to_all.77 = bf16[4,24,1024]{2,1,0:T(8,128)(2,1)S(1)} all-to-all(bf16[4,24,1024]{2,1,0:T(8,128)(2,1)S(1)} %broadcast_in_dim.40), channel_id=1, replica_groups=mesh['y_hi'=2,'z'=8,'core'=2,'y_lo'=4,'x'=4] {'y_lo'}, dimensions={0} | all-to-all | bytes 393216 | tf_op jit(solution)/shard_map/all_to_all | solution.py:21
  66.6 0.4 convolution_convert_fusion.8
  67.1 17.7 %all_to_all.78 = bf16[8,24,1024]{2,1,0:T(8,128)(2,1)S(1)} all-to-all(bf16[8,24,1024]{2,1,0:T(8,128)(2,1)S(1)} %broadcast_in_dim.41), channel_id=1, replica_groups=mesh['y_hi'=2,'z'=8,'core'=2,'y_lo'=4,'x'=4] {'z'}, dimensions={0} | all-to-all | bytes 786432 | tf_op jit(solution)/shard_map/all_to_all | solution.py:21
  84.8 0.7 convolution_convert_fusion.7
  85.5 7.5 %all_to_all.79 = bf16[4,24,1024]{2,1,0:T(8,128)(2,1)S(1)} all-to-all(bf16[4,24,1024]{2,1,0:T(8,128)(2,1)S(1)} %broadcast_in_dim.42), channel_id=1, replica_groups=mesh['y_hi'=2,'z'=8,'core'=2,'y_lo'=4,'x'=4] {'x'}, dimensions={0} | all-to-all | bytes 393216 | tf_op jit(solution)/shard_map/all_to_all | solution.py:21
  93.1 9.5 %all_to_all.80 = bf16[4,24,1024]{2,1,0:T(8,128)(2,1)S(1)} all-to-all(bf16[4,24,1024]{2,1,0:T(8,128)(2,1)S(1)} %broadcast_in_dim.44), channel_id=1, replica_groups=mesh['y_hi'=2,'z'=8,'core'=2,'y_lo'=4,'x'=4] {'y_lo'}, dimensions={0} | all-to-all | bytes 393216 | tf_op jit(solution)/shard_map/all_to_all | solution.py:21
  102.6 0.4 convolution_convert_fusion.6
  103.0 14.4 %all_to_all.81 = bf16[8,24,1024]{2,1,0:T(8,128)(2,1)S(1)} all-to-all(bf16[8,24,1024]{2,1,0:T(8,128)(2,1)S(1)} %broadcast_in_dim.45), channel_id=1, replica_groups=mesh['y_hi'=2,'z'=8,'core'=2,'y_lo'=4,'x'=4] {'z'}, dimensions={0} | all-to-all | bytes 786432 | tf_op jit(solution)/shard_map/all_to_all | solution.py:21
  117.4 0.7 convolution_convert_fusion.5
  118.1 7.5 %all_to_all.82 = bf16[4,24,1024]{2,1,0:T(8,128)(2,1)S(1)} all-to-all(bf16[4,24,1024]{2,1,0:T(8,128)(2,1)S(1)} %broadcast_in_dim.46), channel_id=1, replica_groups=mesh['y_hi'=2,'z'=8,'core'=2,'y_lo'=4,'x'=4] {'x'}, dimensions={0} | all-to-all | bytes 393216 | tf_op jit(solution)/shard_map/all_to_all | solution.py:21
  125.7 8.0 %all_to_all.83 = bf16[4,24,1024]{2,1,0:T(8,128)(2,1)S(1)} all-to-all(bf16[4,24,1024]{2,1,0:T(8,128)(2,1)S(1)} %broadcast_in_dim.48), channel_id=1, replica_groups=mesh['y_hi'=2,'z'=8,'core'=2,'y_lo'=4,'x'=4] {'y_lo'}, dimensions={0} | all-to-all | bytes 393216 | tf_op jit(solution)/shard_map/all_to_all | solution.py:21
  133.7 0.4 convolution_convert_fusion.4
  134.2 13.1 %all_to_all.84 = bf16[8,24,1024]{2,1,0:T(8,128)(2,1)S(1)} all-to-all(bf16[8,24,1024]{2,1,0:T(8,128)(2,1)S(1)} %broadcast_in_dim.49), channel_id=1, replica_groups=mesh['y_hi'=2,'z'=8,'core'=2,'y_lo'=4,'x'=4] {'z'}, dimensions={0} | all-to-all | bytes 786432 | tf_op jit(solution)/shard_map/all_to_all | solution.py:21
  147.3 0.7 convolution_convert_fusion.3
  148.0 7.8 %all_to_all.85 = bf16[4,24,1024]{2,1,0:T(8,128)(2,1)S(1)} all-to-all(bf16[4,24,1024]{2,1,0:T(8,128)(2,1)S(1)} %broadcast_in_dim.50), channel_id=1, replica_groups=mesh['y_hi'=2,'z'=8,'core'=2,'y_lo'=4,'x'=4] {'x'}, dimensions={0} | all-to-all | bytes 393216 | tf_op jit(solution)/shard_map/all_to_all | solution.py:21
  155.9 8.0 %all_to_all.86 = bf16[4,24,1024]{2,1,0:T(8,128)(2,1)S(1)} all-to-all(bf16[4,24,1024]{2,1,0:T(8,128)(2,1)S(1)} %broadcast_in_dim.52), channel_id=1, replica_groups=mesh['y_hi'=2,'z'=8,'core'=2,'y_lo'=4,'x'=4] {'y_lo'}, dimensions={0} | all-to-all | bytes 393216 | tf_op jit(solution)/shard_map/all_to_all | solution.py:21
  163.9 0.4 convolution_convert_fusion.2
  164.3 0.0 copy-start
  164.4 13.1 %all_to_all.87 = bf16[8,24,1024]{2,1,0:T(8,128)(2,1)S(1)} all-to-all(bf16[8,24,1024]{2,1,0:T(8,128)(2,1)S(1)} %broadcast_in_dim.53), channel_id=1, replica_groups=mesh['y_hi'=2,'z'=8,'core'=2,'y_lo'=4,'x'=4] {'z'}, dimensions={0} | all-to-all | bytes 786432 | tf_op jit(solution)/shard_map/all_to_all | solution.py:21
  177.5 0.1 fusion.22
  177.6 24.2 %all_to_all.88 = bf16[4,24,1280]{2,1,0:T(8,128)(2,1)S(1)} all-to-all(bf16[4,24,1280]{2,1,0:T(8,128)(2,1)S(1)} %pad_maximum_fusion), channel_id=1, replica_groups=mesh['y_hi'=2,'z'=8,'core'=2,'y_lo'=4,'x'=4] {'core','y_hi'}, dimensions={0} | all-to-all | bytes 491520 | tf_op jit(solution)/shard_map/all_to_all | solution.py:90
  201.8 0.0 copy-done
  201.8 0.8 convolution_convert_fusion.1
  202.6 0.9 convolution_convert_fusion
  (32 shorter events, 0.7 us)
Async XLA Ops:
  0.6 10.4 %copy-start.2 = (bf16[1024,3]{0,1:T(4,128)(2,1)S(1)}, bf16[1024,3]{0,1:T(4,128)(2,1)}, u32[]{:S(2)}) copy-start(bf16[1024,3]{0,1:T(4,128)(2,1)} %param.10) | copy-start | bytes 18436
  0.6 27.8 %copy-start.1 = (s32[1024]{0:T(1024)S(1)}, s32[1024]{0:T(1024)}, u32[]{:S(2)}) copy-start(s32[1024]{0:T(1024)} %param.9) | copy-start | bytes 12292
  2.7 38.8 %collective-permute-start = (s16[264,1024]{1,0:T(8,128)(2,1)S(1)}, s16[264,1024]{1,0:T(8,128)(2,1)S(1)}, u32[]{:S(2)}, u32[]{:S(2)}) collective-permute-start(s16[264,1024]{1,0:T(8,128)(2,1)S(1)} %pad_add_fusion.1), channel_id=1, source_target_pairs={{0,256},{256,0},{1,257},{257,1},{2,258},{258,2},{3,259},{259,3},{4... | collective-permute-start | bytes 1622024 | tf_op jit(solution)/shard_map/ppermute | solution.py:41
  29.0 11.2 %all-to-all-start.1 = ((s32[16,1,128]{2,1,0:T(1,128)}), s32[16,1,128]{2,1,0:T(1,128)S(1)}, u32[]{:S(2)}, u32[]{:S(2)}) async-start(s32[16,1,128]{2,1,0:T(1,128)} %broadcast_in_dim.37), calls=%async_computation.1 | async-start | bytes 16384 | tf_op jit(solution)/shard_map/all_to_all | solution.py:21
  164.3 37.5 %copy-start = (bf16[96,96]{1,0:T(8,128)(2,1)S(1)}, bf16[96,96]{1,0:T(8,128)(2,1)}, u32[]{:S(2)}) copy-start(bf16[96,96]{1,0:T(8,128)(2,1)} %constant.51.clone) | copy-start | bytes 55300

commit v12 on v11

--- a/solution.py
+++ b/solution.py
@@ -35,8 +35,10 @@
     rows, cols = counts.shape
     scale = 1.0 / math.sqrt(rows * Y_HI * Z * CORE + cols * Y_LO * X)
 
+    low = lax.axis_index("y_hi") == 0
     pieces = jnp.stack([cell_totals >> shift & 2047 for shift in (0, 11, 22)])
     extra = jnp.zeros((EXTRA, cols), I16).at[:3, :rows].set(pieces.astype(I16))
+    extra = extra.at[3].set(low.astype(I16))
     mine = jnp.concatenate([counts.astype(I16), extra])
     other = lax.ppermute(mine, "y_hi", [(0, 1), (1, 0)])
 
@@ -48,7 +50,6 @@
     total = jnp.sum(totals)
     fraction = gene_totals.astype(F32) / total.astype(F32)
 
-    low = lax.axis_index("y_hi") == 0
     pair = jnp.stack([jnp.where(low, mine, other), jnp.where(low, other, mine)])
     blocks = lax.all_gather(pair, "core").reshape(BLOCKS, rows + EXTRA, cols)
     pieces = blocks[:, rows : rows + 3, :rows].astype(jnp.int32)

time: 206 us -> 206 us (level)
  blocking collectives: 171 us -> 182 us
  waiting for transfers between devices: 6.68 us -> 0.01 us
  starting transfers between devices: 12.7 us -> 8.28 us
    all_to_all x13 -> x14, blocking collectives: 140 us -> 152 us  [spread(): return lax.all_to_all(copies(x, n), axis, 0, 0)]
    all_to_all x1 -> x0, waiting for transfers between devices: 6.68 us -> none  [spread(): return lax.all_to_all(copies(x, n), axis, 0, 0)]
    all_to_all x1 -> x0, starting transfers between devices: 4.47 us -> none  [spread(): return lax.all_to_all(copies(x, n), axis, 0, 0)]
  transfers between devices with their start and end apart: 2 -> 1, of which waited for: 1 -> 0; matrix products, arithmetic and copies ran while one was open for 1% -> 0% of each run, Pallas kernels for 0% -> 0%
where the time goes in v12:
time: 206 us; the launch traced here: 204 us
  blocking collectives  182 us (88%)
  starting transfers between devices  8.28 us (4%)
  matrix products  5.79 us (3%)
  other arithmetic  4.92 us (2%)
    all_to_all x14, blocking collectives, spread(): return lax.all_to_all(copies(x, n), axis, 0, 0)  152 us
    all_to_all x1, blocking collectives, shards(): got = lax.all_to_all(send, ('core', 'y_hi'), 0, 0)  24.2 us
    ppermute x1, starting transfers between devices, shards(): other = lax.ppermute(mine, 'y_hi', [(0, 1), (1, 0)])  8.28 us
    all_gather x1, blocking collectives, shards(): blocks = lax.all_gather(pair, 'core').reshape(BLOCKS, rows + EXTRA, cols)  6.5 us
  transfers between devices with their start and end apart: 1, of which 0 were waited for; matrix products, arithmetic and copies ran while one was open for 0% of the time, Pallas kernels for 0%

profile of v12, /device:TPU:1, one launch (start us, length us, event | category | flops | bytes accessed | tf_op | source)
XLA Modules:
  0.0 203.5 jit_solution(18087939648483424271)
XLA Ops:
  0.6 0.0 copy-start.2
  0.6 0.0 copy-start.1
  0.7 0.7 and_convert_fusion.2
  1.4 1.3 convert_element_type.395
  2.7 0.1 scatter.9
  2.8 8.3 %collective-permute-start = (s16[264,1024]{1,0:T(8,128)(2,1)S(1)}, s16[264,1024]{1,0:T(8,128)(2,1)S(1)}, u32[]{:S(2)}, u32[]{:S(2)}) collective-permute-start(s16[264,1024]{1,0:T(8,128)(2,1)S(1)} %pad_add_fusion.1), channel_id=1, source_target_pairs={{0,256},{256,0},{1,257},{257,1},{2,258},{258,2},{3,259},{259,3},{4... | collective-permute-start | bytes 1622024 | tf_op jit(solution)/shard_map/ppermute | solution.py:43
  11.1 0.0 copy-done.2
  11.2 17.4 %all_to_all.75 = bf16[8,3,1024]{2,1,0:T(4,128)(2,1)S(1)} all-to-all(bf16[8,3,1024]{2,1,0:T(4,128)(2,1)S(1)} %broadcast_in_dim.36), channel_id=1, replica_groups=mesh['y_hi'=2,'z'=8,'core'=2,'y_lo'=4,'x'=4] {'z'}, dimensions={0} | all-to-all | bytes 98304 | tf_op jit(solution)/shard_map/all_to_all | solution.py:21
  28.5 0.0 copy-done.1
  28.5 11.0 %all_to_all.76 = s32[16,1,128]{2,1,0:T(1,128)S(1)} all-to-all(s32[16,1,128]{2,1,0:T(1,128)S(1)} %broadcast_in_dim.37), channel_id=1, replica_groups=mesh['y_hi'=2,'z'=8,'core'=2,'y_lo'=4,'x'=4] {'y_lo','x'}, dimensions={0} | all-to-all | bytes 16384 | tf_op jit(solution)/shard_map/all_to_all | solution.py:21
  39.6 0.6 reduce_sum.19
  40.9 0.0 collective-permute-done
  41.0 0.3 select_bitcast_fusion.1
  41.2 0.1 pad_add_fusion
  41.3 6.5 %all-gather.2 = s16[4,264,1024]{2,1,0:T(8,128)(2,1)S(1)} all-gather(s16[2,264,1024]{2,1,0:T(8,128)(2,1)S(1)} %pad_add_fusion), channel_id=2, replica_groups=mesh['y_hi'=2,'z'=8,'core'=2,'y_lo'=4,'x'=4] {'core'}, dimensions={0}, use_global_device_ids=true | all-gather | bytes 3244032 | tf_op jit(solution)/shard_map/all_gather | solution.py:54
  47.8 1.6 fusion.1
  49.4 0.7 convolution_convert_fusion.9
  50.1 7.8 %all_to_all.77 = bf16[4,24,1024]{2,1,0:T(8,128)(2,1)S(1)} all-to-all(bf16[4,24,1024]{2,1,0:T(8,128)(2,1)S(1)} %broadcast_in_dim.38), channel_id=1, replica_groups=mesh['y_hi'=2,'z'=8,'core'=2,'y_lo'=4,'x'=4] {'x'}, dimensions={0} | all-to-all | bytes 393216 | tf_op jit(solution)/shard_map/all_to_all | solution.py:21
  58.0 8.0 %all_to_all.78 = bf16[4,24,1024]{2,1,0:T(8,128)(2,1)S(1)} all-to-all(bf16[4,24,1024]{2,1,0:T(8,128)(2,1)S(1)} %broadcast_in_dim.40), channel_id=1, replica_groups=mesh['y_hi'=2,'z'=8,'core'=2,'y_lo'=4,'x'=4] {'y_lo'}, dimensions={0} | all-to-all | bytes 393216 | tf_op jit(solution)/shard_map/all_to_all | solution.py:21
  66.0 0.4 convolution_convert_fusion.8
  66.5 18.4 %all_to_all.79 = bf16[8,24,1024]{2,1,0:T(8,128)(2,1)S(1)} all-to-all(bf16[8,24,1024]{2,1,0:T(8,128)(2,1)S(1)} %broadcast_in_dim.41), channel_id=1, replica_groups=mesh['y_hi'=2,'z'=8,'core'=2,'y_lo'=4,'x'=4] {'z'}, dimensions={0} | all-to-all | bytes 786432 | tf_op jit(solution)/shard_map/all_to_all | solution.py:21
  84.9 0.7 convolution_convert_fusion.7
  85.6 7.5 %all_to_all.80 = bf16[4,24,1024]{2,1,0:T(8,128)(2,1)S(1)} all-to-all(bf16[4,24,1024]{2,1,0:T(8,128)(2,1)S(1)} %broadcast_in_dim.42), channel_id=1, replica_groups=mesh['y_hi'=2,'z'=8,'core'=2,'y_lo'=4,'x'=4] {'x'}, dimensions={0} | all-to-all | bytes 393216 | tf_op jit(solution)/shard_map/all_to_all | solution.py:21
  93.2 9.5 %all_to_all.81 = bf16[4,24,1024]{2,1,0:T(8,128)(2,1)S(1)} all-to-all(bf16[4,24,1024]{2,1,0:T(8,128)(2,1)S(1)} %broadcast_in_dim.44), channel_id=1, replica_groups=mesh['y_hi'=2,'z'=8,'core'=2,'y_lo'=4,'x'=4] {'y_lo'}, dimensions={0} | all-to-all | bytes 393216 | tf_op jit(solution)/shard_map/all_to_all | solution.py:21
  102.7 0.4 convolution_convert_fusion.6
  103.1 14.4 %all_to_all.82 = bf16[8,24,1024]{2,1,0:T(8,128)(2,1)S(1)} all-to-all(bf16[8,24,1024]{2,1,0:T(8,128)(2,1)S(1)} %broadcast_in_dim.45), channel_id=1, replica_groups=mesh['y_hi'=2,'z'=8,'core'=2,'y_lo'=4,'x'=4] {'z'}, dimensions={0} | all-to-all | bytes 786432 | tf_op jit(solution)/shard_map/all_to_all | solution.py:21
  117.5 0.7 convolution_convert_fusion.5
  118.2 7.5 %all_to_all.83 = bf16[4,24,1024]{2,1,0:T(8,128)(2,1)S(1)} all-to-all(bf16[4,24,1024]{2,1,0:T(8,128)(2,1)S(1)} %broadcast_in_dim.46), channel_id=1, replica_groups=mesh['y_hi'=2,'z'=8,'core'=2,'y_lo'=4,'x'=4] {'x'}, dimensions={0} | all-to-all | bytes 393216 | tf_op jit(solution)/shard_map/all_to_all | solution.py:21
  125.8 8.0 %all_to_all.84 = bf16[4,24,1024]{2,1,0:T(8,128)(2,1)S(1)} all-to-all(bf16[4,24,1024]{2,1,0:T(8,128)(2,1)S(1)} %broadcast_in_dim.48), channel_id=1, replica_groups=mesh['y_hi'=2,'z'=8,'core'=2,'y_lo'=4,'x'=4] {'y_lo'}, dimensions={0} | all-to-all | bytes 393216 | tf_op jit(solution)/shard_map/all_to_all | solution.py:21
  133.8 0.4 convolution_convert_fusion.4
  134.3 13.1 %all_to_all.85 = bf16[8,24,1024]{2,1,0:T(8,128)(2,1)S(1)} all-to-all(bf16[8,24,1024]{2,1,0:T(8,128)(2,1)S(1)} %broadcast_in_dim.49), channel_id=1, replica_groups=mesh['y_hi'=2,'z'=8,'core'=2,'y_lo'=4,'x'=4] {'z'}, dimensions={0} | all-to-all | bytes 786432 | tf_op jit(solution)/shard_map/all_to_all | solution.py:21
  147.4 0.7 convolution_convert_fusion.3
  148.1 7.8 %all_to_all.86 = bf16[4,24,1024]{2,1,0:T(8,128)(2,1)S(1)} all-to-all(bf16[4,24,1024]{2,1,0:T(8,128)(2,1)S(1)} %broadcast_in_dim.50), channel_id=1, replica_groups=mesh['y_hi'=2,'z'=8,'core'=2,'y_lo'=4,'x'=4] {'x'}, dimensions={0} | all-to-all | bytes 393216 | tf_op jit(solution)/shard_map/all_to_all | solution.py:21
  156.0 8.0 %all_to_all.87 = bf16[4,24,1024]{2,1,0:T(8,128)(2,1)S(1)} all-to-all(bf16[4,24,1024]{2,1,0:T(8,128)(2,1)S(1)} %broadcast_in_dim.52), channel_id=1, replica_groups=mesh['y_hi'=2,'z'=8,'core'=2,'y_lo'=4,'x'=4] {'y_lo'}, dimensions={0} | all-to-all | bytes 393216 | tf_op jit(solution)/shard_map/all_to_all | solution.py:21
  164.0 0.4 convolution_convert_fusion.2
  164.4 0.0 copy-start
  164.5 13.1 %all_to_all.88 = bf16[8,24,1024]{2,1,0:T(8,128)(2,1)S(1)} all-to-all(bf16[8,24,1024]{2,1,0:T(8,128)(2,1)S(1)} %broadcast_in_dim.53), channel_id=1, replica_groups=mesh['y_hi'=2,'z'=8,'core'=2,'y_lo'=4,'x'=4] {'z'}, dimensions={0} | all-to-all | bytes 786432 | tf_op jit(solution)/shard_map/all_to_all | solution.py:21
  177.6 0.1 fusion.22
  177.7 24.2 %all_to_all.89 = bf16[4,24,1280]{2,1,0:T(8,128)(2,1)S(1)} all-to-all(bf16[4,24,1280]{2,1,0:T(8,128)(2,1)S(1)} %pad_maximum_fusion), channel_id=1, replica_groups=mesh['y_hi'=2,'z'=8,'core'=2,'y_lo'=4,'x'=4] {'core','y_hi'}, dimensions={0} | all-to-all | bytes 491520 | tf_op jit(solution)/shard_map/all_to_all | solution.py:91
  201.9 0.0 copy-done
  201.9 0.8 convolution_convert_fusion.1
  202.7 0.9 convolution_convert_fusion
  (35 shorter events, 0.7 us)
Async XLA Ops:
  0.6 10.5 %copy-start.2 = (bf16[1024,3]{0,1:T(4,128)(2,1)S(1)}, bf16[1024,3]{0,1:T(4,128)(2,1)}, u32[]{:S(2)}) copy-start(bf16[1024,3]{0,1:T(4,128)(2,1)} %param.12) | copy-start | bytes 18436
  0.6 27.9 %copy-start.1 = (s32[1024]{0:T(1024)S(1)}, s32[1024]{0:T(1024)}, u32[]{:S(2)}) copy-start(s32[1024]{0:T(1024)} %param.11) | copy-start | bytes 12292
  2.8 38.1 %collective-permute-start = (s16[264,1024]{1,0:T(8,128)(2,1)S(1)}, s16[264,1024]{1,0:T(8,128)(2,1)S(1)}, u32[]{:S(2)}, u32[]{:S(2)}) collective-permute-start(s16[264,1024]{1,0:T(8,128)(2,1)S(1)} %pad_add_fusion.1), channel_id=1, source_target_pairs={{0,256},{256,0},{1,257},{257,1},{2,258},{258,2},{3,259},{259,3},{4... | collective-permute-start | bytes 1622024 | tf_op jit(solution)/shard_map/ppermute | solution.py:43
  164.4 37.5 %copy-start = (bf16[96,96]{1,0:T(8,128)(2,1)S(1)}, bf16[96,96]{1,0:T(8,128)(2,1)}, u32[]{:S(2)}) copy-start(bf16[96,96]{1,0:T(8,128)(2,1)} %constant.79.clone) | copy-start | bytes 55300

commit v13 on v12

--- a/solution.py
+++ b/solution.py
@@ -57,7 +57,7 @@
     expected = owned[:, :, None] * fraction[None, None, :]
     stored = (
         (blocks[:, :rows].astype(F32) - expected)
-        / jnp.sqrt(expected + expected * expected / 100.0)
+        * lax.rsqrt(expected * (1.0 + expected * 0.01))
     ).astype(BF16)
     stored = stored.reshape(BLOCKS * rows, cols)
 

time: 206 us -> 206 us (level)
  no operation moved by 1% of the time
where the time goes in v13:
time: 206 us; the launch traced here: 204 us
  blocking collectives  182 us (88%)
  starting transfers between devices  8.28 us (4%)
  matrix products  5.79 us (3%)
  other arithmetic  4.92 us (2%)
    all_to_all x14, blocking collectives, spread(): return lax.all_to_all(copies(x, n), axis, 0, 0)  152 us
    all_to_all x1, blocking collectives, shards(): got = lax.all_to_all(send, ('core', 'y_hi'), 0, 0)  24.2 us
    ppermute x1, starting transfers between devices, shards(): other = lax.ppermute(mine, 'y_hi', [(0, 1), (1, 0)])  8.28 us
    all_gather x1, blocking collectives, shards(): blocks = lax.all_gather(pair, 'core').reshape(BLOCKS, rows + EXTRA, cols)  6.5 us
  transfers between devices with their start and end apart: 1, of which 0 were waited for; matrix products, arithmetic and copies ran while one was open for 0% of the time, Pallas kernels for 0%

profile of v13, /device:TPU:1, one launch (start us, length us, event | category | flops | bytes accessed | tf_op | source)
XLA Modules:
  0.0 203.5 jit_solution(14391138617816969345)
XLA Ops:
  0.6 0.0 copy-start.2
  0.6 0.0 copy-start.1
  0.7 0.7 and_convert_fusion.2
  1.4 1.3 convert_element_type.395
  2.7 0.1 scatter.9
  2.8 8.3 %collective-permute-start = (s16[264,1024]{1,0:T(8,128)(2,1)S(1)}, s16[264,1024]{1,0:T(8,128)(2,1)S(1)}, u32[]{:S(2)}, u32[]{:S(2)}) collective-permute-start(s16[264,1024]{1,0:T(8,128)(2,1)S(1)} %pad_add_fusion.1), channel_id=1, source_target_pairs={{0,256},{256,0},{1,257},{257,1},{2,258},{258,2},{3,259},{259,3},{4... | collective-permute-start | bytes 1622024 | tf_op jit(solution)/shard_map/ppermute | solution.py:43
  11.1 0.0 copy-done.2
  11.2 17.4 %all_to_all.75 = bf16[8,3,1024]{2,1,0:T(4,128)(2,1)S(1)} all-to-all(bf16[8,3,1024]{2,1,0:T(4,128)(2,1)S(1)} %broadcast_in_dim.36), channel_id=1, replica_groups=mesh['y_hi'=2,'z'=8,'core'=2,'y_lo'=4,'x'=4] {'z'}, dimensions={0} | all-to-all | bytes 98304 | tf_op jit(solution)/shard_map/all_to_all | solution.py:21
  28.5 0.0 copy-done.1
  28.5 11.0 %all_to_all.76 = s32[16,1,128]{2,1,0:T(1,128)S(1)} all-to-all(s32[16,1,128]{2,1,0:T(1,128)S(1)} %broadcast_in_dim.37), channel_id=1, replica_groups=mesh['y_hi'=2,'z'=8,'core'=2,'y_lo'=4,'x'=4] {'y_lo','x'}, dimensions={0} | all-to-all | bytes 16384 | tf_op jit(solution)/shard_map/all_to_all | solution.py:21
  39.6 0.6 reduce_sum.19
  40.9 0.0 collective-permute-done
  41.0 0.3 select_bitcast_fusion.1
  41.2 0.1 pad_add_fusion
  41.3 6.5 %all-gather.2 = s16[4,264,1024]{2,1,0:T(8,128)(2,1)S(1)} all-gather(s16[2,264,1024]{2,1,0:T(8,128)(2,1)S(1)} %pad_add_fusion), channel_id=2, replica_groups=mesh['y_hi'=2,'z'=8,'core'=2,'y_lo'=4,'x'=4] {'core'}, dimensions={0}, use_global_device_ids=true | all-gather | bytes 3244032 | tf_op jit(solution)/shard_map/all_gather | solution.py:54
  47.8 1.6 fusion.1
  49.4 0.7 convolution_convert_fusion.9
  50.1 7.8 %all_to_all.77 = bf16[4,24,1024]{2,1,0:T(8,128)(2,1)S(1)} all-to-all(bf16[4,24,1024]{2,1,0:T(8,128)(2,1)S(1)} %broadcast_in_dim.38), channel_id=1, replica_groups=mesh['y_hi'=2,'z'=8,'core'=2,'y_lo'=4,'x'=4] {'x'}, dimensions={0} | all-to-all | bytes 393216 | tf_op jit(solution)/shard_map/all_to_all | solution.py:21
  58.0 8.0 %all_to_all.78 = bf16[4,24,1024]{2,1,0:T(8,128)(2,1)S(1)} all-to-all(bf16[4,24,1024]{2,1,0:T(8,128)(2,1)S(1)} %broadcast_in_dim.40), channel_id=1, replica_groups=mesh['y_hi'=2,'z'=8,'core'=2,'y_lo'=4,'x'=4] {'y_lo'}, dimensions={0} | all-to-all | bytes 393216 | tf_op jit(solution)/shard_map/all_to_all | solution.py:21
  66.0 0.4 convolution_convert_fusion.8
  66.5 18.4 %all_to_all.79 = bf16[8,24,1024]{2,1,0:T(8,128)(2,1)S(1)} all-to-all(bf16[8,24,1024]{2,1,0:T(8,128)(2,1)S(1)} %broadcast_in_dim.41), channel_id=1, replica_groups=mesh['y_hi'=2,'z'=8,'core'=2,'y_lo'=4,'x'=4] {'z'}, dimensions={0} | all-to-all | bytes 786432 | tf_op jit(solution)/shard_map/all_to_all | solution.py:21
  84.9 0.7 convolution_convert_fusion.7
  85.6 7.5 %all_to_all.80 = bf16[4,24,1024]{2,1,0:T(8,128)(2,1)S(1)} all-to-all(bf16[4,24,1024]{2,1,0:T(8,128)(2,1)S(1)} %broadcast_in_dim.42), channel_id=1, replica_groups=mesh['y_hi'=2,'z'=8,'core'=2,'y_lo'=4,'x'=4] {'x'}, dimensions={0} | all-to-all | bytes 393216 | tf_op jit(solution)/shard_map/all_to_all | solution.py:21
  93.2 9.5 %all_to_all.81 = bf16[4,24,1024]{2,1,0:T(8,128)(2,1)S(1)} all-to-all(bf16[4,24,1024]{2,1,0:T(8,128)(2,1)S(1)} %broadcast_in_dim.44), channel_id=1, replica_groups=mesh['y_hi'=2,'z'=8,'core'=2,'y_lo'=4,'x'=4] {'y_lo'}, dimensions={0} | all-to-all | bytes 393216 | tf_op jit(solution)/shard_map/all_to_all | solution.py:21
  102.7 0.4 convolution_convert_fusion.6
  103.1 14.4 %all_to_all.82 = bf16[8,24,1024]{2,1,0:T(8,128)(2,1)S(1)} all-to-all(bf16[8,24,1024]{2,1,0:T(8,128)(2,1)S(1)} %broadcast_in_dim.45), channel_id=1, replica_groups=mesh['y_hi'=2,'z'=8,'core'=2,'y_lo'=4,'x'=4] {'z'}, dimensions={0} | all-to-all | bytes 786432 | tf_op jit(solution)/shard_map/all_to_all | solution.py:21
  117.5 0.7 convolution_convert_fusion.5
  118.2 7.5 %all_to_all.83 = bf16[4,24,1024]{2,1,0:T(8,128)(2,1)S(1)} all-to-all(bf16[4,24,1024]{2,1,0:T(8,128)(2,1)S(1)} %broadcast_in_dim.46), channel_id=1, replica_groups=mesh['y_hi'=2,'z'=8,'core'=2,'y_lo'=4,'x'=4] {'x'}, dimensions={0} | all-to-all | bytes 393216 | tf_op jit(solution)/shard_map/all_to_all | solution.py:21
  125.8 8.0 %all_to_all.84 = bf16[4,24,1024]{2,1,0:T(8,128)(2,1)S(1)} all-to-all(bf16[4,24,1024]{2,1,0:T(8,128)(2,1)S(1)} %broadcast_in_dim.48), channel_id=1, replica_groups=mesh['y_hi'=2,'z'=8,'core'=2,'y_lo'=4,'x'=4] {'y_lo'}, dimensions={0} | all-to-all | bytes 393216 | tf_op jit(solution)/shard_map/all_to_all | solution.py:21
  133.8 0.4 convolution_convert_fusion.4
  134.3 13.1 %all_to_all.85 = bf16[8,24,1024]{2,1,0:T(8,128)(2,1)S(1)} all-to-all(bf16[8,24,1024]{2,1,0:T(8,128)(2,1)S(1)} %broadcast_in_dim.49), channel_id=1, replica_groups=mesh['y_hi'=2,'z'=8,'core'=2,'y_lo'=4,'x'=4] {'z'}, dimensions={0} | all-to-all | bytes 786432 | tf_op jit(solution)/shard_map/all_to_all | solution.py:21
  147.4 0.7 convolution_convert_fusion.3
  148.1 7.8 %all_to_all.86 = bf16[4,24,1024]{2,1,0:T(8,128)(2,1)S(1)} all-to-all(bf16[4,24,1024]{2,1,0:T(8,128)(2,1)S(1)} %broadcast_in_dim.50), channel_id=1, replica_groups=mesh['y_hi'=2,'z'=8,'core'=2,'y_lo'=4,'x'=4] {'x'}, dimensions={0} | all-to-all | bytes 393216 | tf_op jit(solution)/shard_map/all_to_all | solution.py:21
  156.0 8.0 %all_to_all.87 = bf16[4,24,1024]{2,1,0:T(8,128)(2,1)S(1)} all-to-all(bf16[4,24,1024]{2,1,0:T(8,128)(2,1)S(1)} %broadcast_in_dim.52), channel_id=1, replica_groups=mesh['y_hi'=2,'z'=8,'core'=2,'y_lo'=4,'x'=4] {'y_lo'}, dimensions={0} | all-to-all | bytes 393216 | tf_op jit(solution)/shard_map/all_to_all | solution.py:21
  164.0 0.4 convolution_convert_fusion.2
  164.4 0.0 copy-start
  164.5 13.1 %all_to_all.88 = bf16[8,24,1024]{2,1,0:T(8,128)(2,1)S(1)} all-to-all(bf16[8,24,1024]{2,1,0:T(8,128)(2,1)S(1)} %broadcast_in_dim.53), channel_id=1, replica_groups=mesh['y_hi'=2,'z'=8,'core'=2,'y_lo'=4,'x'=4] {'z'}, dimensions={0} | all-to-all | bytes 786432 | tf_op jit(solution)/shard_map/all_to_all | solution.py:21
  177.6 0.1 fusion.22
  177.7 24.2 %all_to_all.89 = bf16[4,24,1280]{2,1,0:T(8,128)(2,1)S(1)} all-to-all(bf16[4,24,1280]{2,1,0:T(8,128)(2,1)S(1)} %pad_maximum_fusion), channel_id=1, replica_groups=mesh['y_hi'=2,'z'=8,'core'=2,'y_lo'=4,'x'=4] {'core','y_hi'}, dimensions={0} | all-to-all | bytes 491520 | tf_op jit(solution)/shard_map/all_to_all | solution.py:91
  201.9 0.0 copy-done
  201.9 0.8 convolution_convert_fusion.1
  202.7 0.9 convolution_convert_fusion
  (35 shorter events, 0.7 us)
Async XLA Ops:
  0.6 10.5 %copy-start.2 = (bf16[1024,3]{0,1:T(4,128)(2,1)S(1)}, bf16[1024,3]{0,1:T(4,128)(2,1)}, u32[]{:S(2)}) copy-start(bf16[1024,3]{0,1:T(4,128)(2,1)} %param.12) | copy-start | bytes 18436
  0.6 27.9 %copy-start.1 = (s32[1024]{0:T(1024)S(1)}, s32[1024]{0:T(1024)}, u32[]{:S(2)}) copy-start(s32[1024]{0:T(1024)} %param.11) | copy-start | bytes 12292
  2.8 38.1 %collective-permute-start = (s16[264,1024]{1,0:T(8,128)(2,1)S(1)}, s16[264,1024]{1,0:T(8,128)(2,1)S(1)}, u32[]{:S(2)}, u32[]{:S(2)}) collective-permute-start(s16[264,1024]{1,0:T(8,128)(2,1)S(1)} %pad_add_fusion.1), channel_id=1, source_target_pairs={{0,256},{256,0},{1,257},{257,1},{2,258},{258,2},{3,259},{259,3},{4... | collective-permute-start | bytes 1622024 | tf_op jit(solution)/shard_map/ppermute | solution.py:43
  164.4 37.5 %copy-start = (bf16[96,96]{1,0:T(8,128)(2,1)S(1)}, bf16[96,96]{1,0:T(8,128)(2,1)}, u32[]{:S(2)}) copy-start(bf16[96,96]{1,0:T(8,128)(2,1)} %constant.80.clone) | copy-start | bytes 55300

commit v14 on v11

--- a/solution.py
+++ b/solution.py
@@ -64,7 +64,7 @@
         part = lax.dot_general(
             panel, stored, (((1,), (1,)), ((), ())), preferred_element_type=F32
         ).astype(BF16)
-        return gather_sum(gather_sum(part, "x", X), "y_lo", Y_LO, factor)
+        return gather_sum(gather_sum(part, "y_lo", Y_LO), "x", X, factor)
 
     def gene_side(sketch):
         part = jnp.dot(sketch, stored, preferred_element_type=F32).astype(BF16)

time: 206 us -> 206 us (level)
  no operation moved by 1% of the time
where the time goes in v14:
time: 206 us; the launch traced here: 204 us
  blocking collectives  171 us (83%)
  starting transfers between devices  12.7 us (6%)
  waiting for transfers between devices  6.68 us (3%)
  matrix products  5.79 us (3%)
  other arithmetic  4.92 us (2%)
    all_to_all x13, blocking collectives, spread(): return lax.all_to_all(copies(x, n), axis, 0, 0)  141 us
    all_to_all x1, blocking collectives, shards(): got = lax.all_to_all(send, ('core', 'y_hi'), 0, 0)  23.6 us
    ppermute x1, starting transfers between devices, shards(): other = lax.ppermute(mine, 'y_hi', [(0, 1), (1, 0)])  8.28 us
    all_to_all x1, waiting for transfers between devices, spread(): return lax.all_to_all(copies(x, n), axis, 0, 0)  6.68 us
    all_gather x1, blocking collectives, shards(): blocks = lax.all_gather(pair, 'core').reshape(BLOCKS, rows + EXTRA, cols)  6.5 us
    all_to_all x1, starting transfers between devices, spread(): return lax.all_to_all(copies(x, n), axis, 0, 0)  4.47 us
  transfers between devices with their start and end apart: 2, of which 1 were waited for; matrix products, arithmetic and copies ran while one was open for 1% of the time, Pallas kernels for 0%

profile of v14, /device:TPU:1, one launch (start us, length us, event | category | flops | bytes accessed | tf_op | source)
XLA Modules:
  0.0 204.2 jit_solution(7212813369649241076)
XLA Ops:
  0.6 0.0 copy-start.2
  0.6 0.0 copy-start.1
  0.7 0.7 and_convert_fusion.2
  1.4 1.3 convert_element_type.392
  2.7 8.3 %collective-permute-start = (s16[264,1024]{1,0:T(8,128)(2,1)S(1)}, s16[264,1024]{1,0:T(8,128)(2,1)S(1)}, u32[]{:S(2)}, u32[]{:S(2)}) collective-permute-start(s16[264,1024]{1,0:T(8,128)(2,1)S(1)} %pad_add_fusion.1), channel_id=1, source_target_pairs={{0,256},{256,0},{1,257},{257,1},{2,258},{258,2},{3,259},{259,3},{4... | collective-permute-start | bytes 1622024 | tf_op jit(solution)/shard_map/ppermute | solution.py:41
  11.0 0.0 copy-done.2
  11.1 17.4 %all_to_all.75 = bf16[8,3,1024]{2,1,0:T(4,128)(2,1)S(1)} all-to-all(bf16[8,3,1024]{2,1,0:T(4,128)(2,1)S(1)} %broadcast_in_dim.36), channel_id=1, replica_groups=mesh['y_hi'=2,'z'=8,'core'=2,'y_lo'=4,'x'=4] {'z'}, dimensions={0} | all-to-all | bytes 98304 | tf_op jit(solution)/shard_map/all_to_all | solution.py:21
  28.4 0.0 copy-done.1
  28.4 0.6 broadcast_in_dim.37
  29.0 4.5 %all-to-all-start.1 = ((s32[16,1,128]{2,1,0:T(1,128)}), s32[16,1,128]{2,1,0:T(1,128)S(1)}, u32[]{:S(2)}, u32[]{:S(2)}) async-start(s32[16,1,128]{2,1,0:T(1,128)} %broadcast_in_dim.37), calls=%async_computation.1 | async-start | bytes 16384 | tf_op jit(solution)/shard_map/all_to_all | solution.py:21
  33.5 6.7 %all-to-all-done.1 = s32[16,1,128]{2,1,0:T(1,128)S(1)} async-done(((s32[16,1,128]{2,1,0:T(1,128)}), s32[16,1,128]{2,1,0:T(1,128)S(1)}, u32[]{:S(2)}, u32[]{:S(2)}) %all-to-all-start.1) | async-done | bytes 8224 | tf_op jit(solution)/shard_map/all_to_all | solution.py:21
  40.2 0.6 reduce_sum.19
  41.6 0.0 collective-permute-done
  41.6 0.3 select_bitcast_fusion.1
  41.8 0.1 pad_add_fusion
  41.9 6.5 %all-gather.2 = s16[4,264,1024]{2,1,0:T(8,128)(2,1)S(1)} all-gather(s16[2,264,1024]{2,1,0:T(8,128)(2,1)S(1)} %pad_add_fusion), channel_id=2, replica_groups=mesh['y_hi'=2,'z'=8,'core'=2,'y_lo'=4,'x'=4] {'core'}, dimensions={0}, use_global_device_ids=true | all-gather | bytes 3244032 | tf_op jit(solution)/shard_map/all_gather | solution.py:53
  48.5 1.6 fusion.1
  50.1 0.7 convolution_convert_fusion.9
  50.7 8.6 %all_to_all.76 = bf16[4,24,1024]{2,1,0:T(8,128)(2,1)S(1)} all-to-all(bf16[4,24,1024]{2,1,0:T(8,128)(2,1)S(1)} %broadcast_in_dim.38), channel_id=1, replica_groups=mesh['y_hi'=2,'z'=8,'core'=2,'y_lo'=4,'x'=4] {'y_lo'}, dimensions={0} | all-to-all | bytes 393216 | tf_op jit(solution)/shard_map/all_to_all | solution.py:21
  59.4 7.5 %all_to_all.77 = bf16[4,24,1024]{2,1,0:T(8,128)(2,1)S(1)} all-to-all(bf16[4,24,1024]{2,1,0:T(8,128)(2,1)S(1)} %broadcast_in_dim.40), channel_id=1, replica_groups=mesh['y_hi'=2,'z'=8,'core'=2,'y_lo'=4,'x'=4] {'x'}, dimensions={0} | all-to-all | bytes 393216 | tf_op jit(solution)/shard_map/all_to_all | solution.py:21
  66.9 0.4 convolution_convert_fusion.8
  67.4 17.0 %all_to_all.78 = bf16[8,24,1024]{2,1,0:T(8,128)(2,1)S(1)} all-to-all(bf16[8,24,1024]{2,1,0:T(8,128)(2,1)S(1)} %broadcast_in_dim.41), channel_id=1, replica_groups=mesh['y_hi'=2,'z'=8,'core'=2,'y_lo'=4,'x'=4] {'z'}, dimensions={0} | all-to-all | bytes 786432 | tf_op jit(solution)/shard_map/all_to_all | solution.py:21
  84.4 0.7 convolution_convert_fusion.7
  85.1 10.5 %all_to_all.79 = bf16[4,24,1024]{2,1,0:T(8,128)(2,1)S(1)} all-to-all(bf16[4,24,1024]{2,1,0:T(8,128)(2,1)S(1)} %broadcast_in_dim.42), channel_id=1, replica_groups=mesh['y_hi'=2,'z'=8,'core'=2,'y_lo'=4,'x'=4] {'y_lo'}, dimensions={0} | all-to-all | bytes 393216 | tf_op jit(solution)/shard_map/all_to_all | solution.py:21
  95.6 7.5 %all_to_all.80 = bf16[4,24,1024]{2,1,0:T(8,128)(2,1)S(1)} all-to-all(bf16[4,24,1024]{2,1,0:T(8,128)(2,1)S(1)} %broadcast_in_dim.44), channel_id=1, replica_groups=mesh['y_hi'=2,'z'=8,'core'=2,'y_lo'=4,'x'=4] {'x'}, dimensions={0} | all-to-all | bytes 393216 | tf_op jit(solution)/shard_map/all_to_all | solution.py:21
  103.1 0.4 convolution_convert_fusion.6
  103.6 14.6 %all_to_all.81 = bf16[8,24,1024]{2,1,0:T(8,128)(2,1)S(1)} all-to-all(bf16[8,24,1024]{2,1,0:T(8,128)(2,1)S(1)} %broadcast_in_dim.45), channel_id=1, replica_groups=mesh['y_hi'=2,'z'=8,'core'=2,'y_lo'=4,'x'=4] {'z'}, dimensions={0} | all-to-all | bytes 786432 | tf_op jit(solution)/shard_map/all_to_all | solution.py:21
  118.2 0.7 convolution_convert_fusion.5
  118.9 8.9 %all_to_all.82 = bf16[4,24,1024]{2,1,0:T(8,128)(2,1)S(1)} all-to-all(bf16[4,24,1024]{2,1,0:T(8,128)(2,1)S(1)} %broadcast_in_dim.46), channel_id=1, replica_groups=mesh['y_hi'=2,'z'=8,'core'=2,'y_lo'=4,'x'=4] {'y_lo'}, dimensions={0} | all-to-all | bytes 393216 | tf_op jit(solution)/shard_map/all_to_all | solution.py:21
  127.9 7.5 %all_to_all.83 = bf16[4,24,1024]{2,1,0:T(8,128)(2,1)S(1)} all-to-all(bf16[4,24,1024]{2,1,0:T(8,128)(2,1)S(1)} %broadcast_in_dim.48), channel_id=1, replica_groups=mesh['y_hi'=2,'z'=8,'core'=2,'y_lo'=4,'x'=4] {'x'}, dimensions={0} | all-to-all | bytes 393216 | tf_op jit(solution)/shard_map/all_to_all | solution.py:21
  135.4 0.4 convolution_convert_fusion.4
  135.8 13.1 %all_to_all.84 = bf16[8,24,1024]{2,1,0:T(8,128)(2,1)S(1)} all-to-all(bf16[8,24,1024]{2,1,0:T(8,128)(2,1)S(1)} %broadcast_in_dim.49), channel_id=1, replica_groups=mesh['y_hi'=2,'z'=8,'core'=2,'y_lo'=4,'x'=4] {'z'}, dimensions={0} | all-to-all | bytes 786432 | tf_op jit(solution)/shard_map/all_to_all | solution.py:21
  149.0 0.7 convolution_convert_fusion.3
  149.7 8.0 %all_to_all.85 = bf16[4,24,1024]{2,1,0:T(8,128)(2,1)S(1)} all-to-all(bf16[4,24,1024]{2,1,0:T(8,128)(2,1)S(1)} %broadcast_in_dim.50), channel_id=1, replica_groups=mesh['y_hi'=2,'z'=8,'core'=2,'y_lo'=4,'x'=4] {'y_lo'}, dimensions={0} | all-to-all | bytes 393216 | tf_op jit(solution)/shard_map/all_to_all | solution.py:21
  157.7 7.5 %all_to_all.86 = bf16[4,24,1024]{2,1,0:T(8,128)(2,1)S(1)} all-to-all(bf16[4,24,1024]{2,1,0:T(8,128)(2,1)S(1)} %broadcast_in_dim.52), channel_id=1, replica_groups=mesh['y_hi'=2,'z'=8,'core'=2,'y_lo'=4,'x'=4] {'x'}, dimensions={0} | all-to-all | bytes 393216 | tf_op jit(solution)/shard_map/all_to_all | solution.py:21
  165.3 0.4 convolution_convert_fusion.2
  165.7 0.0 copy-start
  165.8 13.1 %all_to_all.87 = bf16[8,24,1024]{2,1,0:T(8,128)(2,1)S(1)} all-to-all(bf16[8,24,1024]{2,1,0:T(8,128)(2,1)S(1)} %broadcast_in_dim.53), channel_id=1, replica_groups=mesh['y_hi'=2,'z'=8,'core'=2,'y_lo'=4,'x'=4] {'z'}, dimensions={0} | all-to-all | bytes 786432 | tf_op jit(solution)/shard_map/all_to_all | solution.py:21
  178.9 0.1 fusion.22
  179.0 23.6 %all_to_all.88 = bf16[4,24,1280]{2,1,0:T(8,128)(2,1)S(1)} all-to-all(bf16[4,24,1280]{2,1,0:T(8,128)(2,1)S(1)} %pad_maximum_fusion), channel_id=1, replica_groups=mesh['y_hi'=2,'z'=8,'core'=2,'y_lo'=4,'x'=4] {'core','y_hi'}, dimensions={0} | all-to-all | bytes 491520 | tf_op jit(solution)/shard_map/all_to_all | solution.py:90
  202.6 0.0 copy-done
  202.6 0.8 convolution_convert_fusion.1
  203.3 0.9 convolution_convert_fusion
  (32 shorter events, 0.7 us)
Async XLA Ops:
  0.6 10.4 %copy-start.2 = (bf16[1024,3]{0,1:T(4,128)(2,1)S(1)}, bf16[1024,3]{0,1:T(4,128)(2,1)}, u32[]{:S(2)}) copy-start(bf16[1024,3]{0,1:T(4,128)(2,1)} %param.10) | copy-start | bytes 18436
  0.6 27.8 %copy-start.1 = (s32[1024]{0:T(1024)S(1)}, s32[1024]{0:T(1024)}, u32[]{:S(2)}) copy-start(s32[1024]{0:T(1024)} %param.9) | copy-start | bytes 12292
  2.7 38.8 %collective-permute-start = (s16[264,1024]{1,0:T(8,128)(2,1)S(1)}, s16[264,1024]{1,0:T(8,128)(2,1)S(1)}, u32[]{:S(2)}, u32[]{:S(2)}) collective-permute-start(s16[264,1024]{1,0:T(8,128)(2,1)S(1)} %pad_add_fusion.1), channel_id=1, source_target_pairs={{0,256},{256,0},{1,257},{257,1},{2,258},{258,2},{3,259},{259,3},{4... | collective-permute-start | bytes 1622024 | tf_op jit(solution)/shard_map/ppermute | solution.py:41
  29.0 11.2 %all-to-all-start.1 = ((s32[16,1,128]{2,1,0:T(1,128)}), s32[16,1,128]{2,1,0:T(1,128)S(1)}, u32[]{:S(2)}, u32[]{:S(2)}) async-start(s32[16,1,128]{2,1,0:T(1,128)} %broadcast_in_dim.37), calls=%async_computation.1 | async-start | bytes 16384 | tf_op jit(solution)/shard_map/all_to_all | solution.py:21
  165.7 36.9 %copy-start = (bf16[96,96]{1,0:T(8,128)(2,1)S(1)}, bf16[96,96]{1,0:T(8,128)(2,1)}, u32[]{:S(2)}) copy-start(bf16[96,96]{1,0:T(8,128)(2,1)} %constant.51.clone) | copy-start | bytes 55300

commit v15 on v11

--- a/solution.py
+++ b/solution.py
@@ -4,11 +4,13 @@
 import jax.numpy as jnp
 import numpy as np
 from jax import lax
+from jax.experimental import pallas as pl
+from jax.experimental.pallas import tpu as pltpu
 from jax.sharding import Mesh, PartitionSpec as P
 
 ITERS = 3
 Y_HI, Z, CORE, Y_LO, X = 2, 8, 2, 4, 4
-BLOCKS = CORE * Y_HI
+BLOCKS, PARTS = CORE * Y_HI, 4
 EXTRA = 8
 F32, BF16, I16 = jnp.float32, jnp.bfloat16, jnp.int16
 
@@ -31,13 +33,47 @@
     return total.astype(BF16)
 
 
+def pack(counts_hbm, totals_hbm, out_ref, counts_ref, totals_ref, sems):
+    rows, cols = counts_hbm.shape
+    whole = [pltpu.make_async_copy(totals_hbm, totals_ref, sems.at[PARTS])]
+    step = rows // PARTS
+    for i in range(PARTS):
+        part = pl.ds(i * step, step)
+        whole.append(pltpu.make_async_copy(counts_hbm.at[part], counts_ref.at[part], sems.at[i]))
+    for copy in whole:
+        copy.start()
+    whole[0].wait()
+    shift = jnp.minimum(11 * lax.broadcasted_iota(jnp.int32, (EXTRA, rows), 0), 31)
+    pieces = jnp.broadcast_to(totals_ref[...], (EXTRA, rows)) >> shift & 2047
+    out_ref[rows:, :rows] = pieces.astype(I16)
+    out_ref[rows:, rows:] = jnp.zeros((EXTRA, cols - rows), I16)
+    for i in range(PARTS):
+        whole[i + 1].wait()
+        out_ref[i * step : (i + 1) * step] = counts_ref[i * step : (i + 1) * step].astype(I16)
+
+
 def shards(counts, cell_totals, gene_totals, test_matrix):
     rows, cols = counts.shape
     scale = 1.0 / math.sqrt(rows * Y_HI * Z * CORE + cols * Y_LO * X)
 
-    pieces = jnp.stack([cell_totals >> shift & 2047 for shift in (0, 11, 22)])
-    extra = jnp.zeros((EXTRA, cols), I16).at[:3, :rows].set(pieces.astype(I16))
-    mine = jnp.concatenate([counts.astype(I16), extra])
+    mine = pl.pallas_call(
+        pack,
+        out_shape=jax.ShapeDtypeStruct((rows + EXTRA, cols), I16),
+        in_specs=[pl.BlockSpec(memory_space=pltpu.HBM)] * 2,
+        out_specs=pl.BlockSpec(memory_space=pltpu.VMEM),
+        scratch_shapes=[
+            pltpu.VMEM((rows, cols), jnp.int32),
+            pltpu.VMEM((1, rows), jnp.int32),
+            pltpu.SemaphoreType.DMA((PARTS + 1,)),
+        ],
+        compiler_params=pltpu.CompilerParams(vmem_limit_bytes=4 << 20),
+        cost_estimate=pl.CostEstimate(
+            flops=rows * cols, bytes_accessed=6 * rows * cols, transcendentals=0
+        ),
+    )(
+        pltpu.with_memory_space_constraint(counts, pltpu.HBM),
+        pltpu.with_memory_space_constraint(cell_totals[None], pltpu.HBM),
+    )
     other = lax.ppermute(mine, "y_hi", [(0, 1), (1, 0)])
 
     test = spread(test_matrix.T, "z", Z)

time: 206 us -> 205 us (level)
  transfers between devices with their start and end apart: 2 -> 2, of which waited for: 1 -> 1; matrix products, arithmetic and copies ran while one was open for 1% -> 2% of each run, Pallas kernels for 0% -> 0%
where the time goes in v15:
time: 205 us; the launch traced here: 203 us
  blocking collectives  169 us (82%)
  starting transfers between devices  12.7 us (6%)
  waiting for transfers between devices  6.68 us (3%)
  matrix products  5.79 us (3%)
  other arithmetic  4.25 us (2%)
    all_to_all x13, blocking collectives, spread(): return lax.all_to_all(copies(x, n), axis, 0, 0)  139 us
    all_to_all x1, blocking collectives, shards(): got = lax.all_to_all(send, ('core', 'y_hi'), 0, 0)  24.1 us
    ppermute x1, starting transfers between devices, shards(): other = lax.ppermute(mine, 'y_hi', [(0, 1), (1, 0)])  8.28 us
    all_to_all x1, waiting for transfers between devices, spread(): return lax.all_to_all(copies(x, n), axis, 0, 0)  6.68 us
    all_gather x1, blocking collectives, shards(): blocks = lax.all_gather(pair, 'core').reshape(BLOCKS, rows + EXTRA, cols)  6.5 us
    all_to_all x1, starting transfers between devices, spread(): return lax.all_to_all(copies(x, n), axis, 0, 0)  4.47 us
  transfers between devices with their start and end apart: 2, of which 1 were waited for; matrix products, arithmetic and copies ran while one was open for 2% of the time, Pallas kernels for 0%

profile of v15, /device:TPU:1, one launch (start us, length us, event | category | flops | bytes accessed | tf_op | source)
XLA Modules:
  0.0 203.2 jit_solution(8301752028062573634)
XLA Ops:
  0.6 1.3 shard_map.68
  1.9 8.3 %collective-permute-start = (s16[264,1024]{1,0:T(8,128)(2,1)S(1)}, s16[264,1024]{1,0:T(8,128)(2,1)S(1)}, u32[]{:S(2)}, u32[]{:S(2)}) collective-permute-start(s16[264,1024]{1,0:T(8,128)(2,1)S(1)} %shard_map.68), channel_id=1, source_target_pairs={{0,256},{256,0},{1,257},{257,1},{2,258},{258,2},{3,259},{259,3},{4... | collective-permute-start | bytes 1622024 | tf_op jit(solution)/shard_map/ppermute | solution.py:77
  10.2 0.7 broadcast_in_dim.38
  10.9 17.4 %all_to_all.75 = bf16[8,3,1024]{2,1,0:T(4,128)(2,1)S(1)} all-to-all(bf16[8,3,1024]{2,1,0:T(4,128)(2,1)S(1)} %broadcast_in_dim.38), channel_id=1, replica_groups=mesh['y_hi'=2,'z'=8,'core'=2,'y_lo'=4,'x'=4] {'z'}, dimensions={0} | all-to-all | bytes 98304 | tf_op jit(solution)/shard_map/all_to_all | solution.py:23
  28.3 0.7 reduce_sum.18
  29.0 0.6 broadcast_in_dim.39
  29.6 4.5 %all-to-all-start.1 = ((s32[16,1,128]{2,1,0:T(1,128)}), s32[16,1,128]{2,1,0:T(1,128)S(1)}, u32[]{:S(2)}, u32[]{:S(2)}) async-start(s32[16,1,128]{2,1,0:T(1,128)} %broadcast_in_dim.39), calls=%async_computation.1 | async-start | bytes 16384 | tf_op jit(solution)/shard_map/all_to_all | solution.py:23
  34.1 6.7 %all-to-all-done.1 = s32[16,1,128]{2,1,0:T(1,128)S(1)} async-done(((s32[16,1,128]{2,1,0:T(1,128)}), s32[16,1,128]{2,1,0:T(1,128)S(1)}, u32[]{:S(2)}, u32[]{:S(2)}) %all-to-all-start.1) | async-done | bytes 8224 | tf_op jit(solution)/shard_map/all_to_all | solution.py:23
  40.7 0.6 reduce_sum.19
  42.1 0.7 convert_divide_fusion
  42.8 0.0 collective-permute-done
  42.8 0.3 select_bitcast_fusion.1
  43.0 0.1 pad_add_fusion
  43.1 6.5 %all-gather.2 = s16[4,264,1024]{2,1,0:T(8,128)(2,1)S(1)} all-gather(s16[2,264,1024]{2,1,0:T(8,128)(2,1)S(1)} %pad_add_fusion), channel_id=2, replica_groups=mesh['y_hi'=2,'z'=8,'core'=2,'y_lo'=4,'x'=4] {'core'}, dimensions={0}, use_global_device_ids=true | all-gather | bytes 3244032 | tf_op jit(solution)/shard_map/all_gather | solution.py:89
  49.7 1.6 fusion.1
  51.3 0.7 convolution_convert_fusion.9
  52.0 7.8 %all_to_all.76 = bf16[4,24,1024]{2,1,0:T(8,128)(2,1)S(1)} all-to-all(bf16[4,24,1024]{2,1,0:T(8,128)(2,1)S(1)} %broadcast_in_dim.41), channel_id=1, replica_groups=mesh['y_hi'=2,'z'=8,'core'=2,'y_lo'=4,'x'=4] {'x'}, dimensions={0} | all-to-all | bytes 393216 | tf_op jit(solution)/shard_map/all_to_all | solution.py:23
  59.8 8.0 %all_to_all.77 = bf16[4,24,1024]{2,1,0:T(8,128)(2,1)S(1)} all-to-all(bf16[4,24,1024]{2,1,0:T(8,128)(2,1)S(1)} %broadcast_in_dim.43), channel_id=1, replica_groups=mesh['y_hi'=2,'z'=8,'core'=2,'y_lo'=4,'x'=4] {'y_lo'}, dimensions={0} | all-to-all | bytes 393216 | tf_op jit(solution)/shard_map/all_to_all | solution.py:23
  67.8 0.4 convolution_convert_fusion.8
  68.3 16.4 %all_to_all.78 = bf16[8,24,1024]{2,1,0:T(8,128)(2,1)S(1)} all-to-all(bf16[8,24,1024]{2,1,0:T(8,128)(2,1)S(1)} %broadcast_in_dim.44), channel_id=1, replica_groups=mesh['y_hi'=2,'z'=8,'core'=2,'y_lo'=4,'x'=4] {'z'}, dimensions={0} | all-to-all | bytes 786432 | tf_op jit(solution)/shard_map/all_to_all | solution.py:23
  84.6 0.7 convolution_convert_fusion.7
  85.3 7.5 %all_to_all.79 = bf16[4,24,1024]{2,1,0:T(8,128)(2,1)S(1)} all-to-all(bf16[4,24,1024]{2,1,0:T(8,128)(2,1)S(1)} %broadcast_in_dim.45), channel_id=1, replica_groups=mesh['y_hi'=2,'z'=8,'core'=2,'y_lo'=4,'x'=4] {'x'}, dimensions={0} | all-to-all | bytes 393216 | tf_op jit(solution)/shard_map/all_to_all | solution.py:23
  92.9 9.5 %all_to_all.80 = bf16[4,24,1024]{2,1,0:T(8,128)(2,1)S(1)} all-to-all(bf16[4,24,1024]{2,1,0:T(8,128)(2,1)S(1)} %broadcast_in_dim.47), channel_id=1, replica_groups=mesh['y_hi'=2,'z'=8,'core'=2,'y_lo'=4,'x'=4] {'y_lo'}, dimensions={0} | all-to-all | bytes 393216 | tf_op jit(solution)/shard_map/all_to_all | solution.py:23
  102.4 0.4 convolution_convert_fusion.6
  102.9 14.4 %all_to_all.81 = bf16[8,24,1024]{2,1,0:T(8,128)(2,1)S(1)} all-to-all(bf16[8,24,1024]{2,1,0:T(8,128)(2,1)S(1)} %broadcast_in_dim.48), channel_id=1, replica_groups=mesh['y_hi'=2,'z'=8,'core'=2,'y_lo'=4,'x'=4] {'z'}, dimensions={0} | all-to-all | bytes 786432 | tf_op jit(solution)/shard_map/all_to_all | solution.py:23
  117.3 0.7 convolution_convert_fusion.5
  118.0 7.5 %all_to_all.82 = bf16[4,24,1024]{2,1,0:T(8,128)(2,1)S(1)} all-to-all(bf16[4,24,1024]{2,1,0:T(8,128)(2,1)S(1)} %broadcast_in_dim.49), channel_id=1, replica_groups=mesh['y_hi'=2,'z'=8,'core'=2,'y_lo'=4,'x'=4] {'x'}, dimensions={0} | all-to-all | bytes 393216 | tf_op jit(solution)/shard_map/all_to_all | solution.py:23
  125.6 8.0 %all_to_all.83 = bf16[4,24,1024]{2,1,0:T(8,128)(2,1)S(1)} all-to-all(bf16[4,24,1024]{2,1,0:T(8,128)(2,1)S(1)} %broadcast_in_dim.51), channel_id=1, replica_groups=mesh['y_hi'=2,'z'=8,'core'=2,'y_lo'=4,'x'=4] {'y_lo'}, dimensions={0} | all-to-all | bytes 393216 | tf_op jit(solution)/shard_map/all_to_all | solution.py:23
  133.6 0.4 convolution_convert_fusion.4
  134.0 13.1 %all_to_all.84 = bf16[8,24,1024]{2,1,0:T(8,128)(2,1)S(1)} all-to-all(bf16[8,24,1024]{2,1,0:T(8,128)(2,1)S(1)} %broadcast_in_dim.52), channel_id=1, replica_groups=mesh['y_hi'=2,'z'=8,'core'=2,'y_lo'=4,'x'=4] {'z'}, dimensions={0} | all-to-all | bytes 786432 | tf_op jit(solution)/shard_map/all_to_all | solution.py:23
  147.1 0.7 convolution_convert_fusion.3
  147.8 7.8 %all_to_all.85 = bf16[4,24,1024]{2,1,0:T(8,128)(2,1)S(1)} all-to-all(bf16[4,24,1024]{2,1,0:T(8,128)(2,1)S(1)} %broadcast_in_dim.53), channel_id=1, replica_groups=mesh['y_hi'=2,'z'=8,'core'=2,'y_lo'=4,'x'=4] {'x'}, dimensions={0} | all-to-all | bytes 393216 | tf_op jit(solution)/shard_map/all_to_all | solution.py:23
  155.7 8.0 %all_to_all.86 = bf16[4,24,1024]{2,1,0:T(8,128)(2,1)S(1)} all-to-all(bf16[4,24,1024]{2,1,0:T(8,128)(2,1)S(1)} %broadcast_in_dim.55), channel_id=1, replica_groups=mesh['y_hi'=2,'z'=8,'core'=2,'y_lo'=4,'x'=4] {'y_lo'}, dimensions={0} | all-to-all | bytes 393216 | tf_op jit(solution)/shard_map/all_to_all | solution.py:23
  163.8 0.4 convolution_convert_fusion.2
  164.2 0.0 copy-start
  164.2 13.1 %all_to_all.87 = bf16[8,24,1024]{2,1,0:T(8,128)(2,1)S(1)} all-to-all(bf16[8,24,1024]{2,1,0:T(8,128)(2,1)S(1)} %broadcast_in_dim.56), channel_id=1, replica_groups=mesh['y_hi'=2,'z'=8,'core'=2,'y_lo'=4,'x'=4] {'z'}, dimensions={0} | all-to-all | bytes 786432 | tf_op jit(solution)/shard_map/all_to_all | solution.py:23
  177.3 0.1 fusion.22
  177.5 24.1 %all_to_all.88 = bf16[4,24,1280]{2,1,0:T(8,128)(2,1)S(1)} all-to-all(bf16[4,24,1280]{2,1,0:T(8,128)(2,1)S(1)} %pad_maximum_fusion), channel_id=1, replica_groups=mesh['y_hi'=2,'z'=8,'core'=2,'y_lo'=4,'x'=4] {'core','y_hi'}, dimensions={0} | all-to-all | bytes 491520 | tf_op jit(solution)/shard_map/all_to_all | solution.py:126
  201.6 0.0 copy-done
  201.6 0.8 convolution_convert_fusion.1
  202.3 0.9 convolution_convert_fusion
  (24 shorter events, 0.6 us)
Async XLA Ops:
  1.9 40.9 %collective-permute-start = (s16[264,1024]{1,0:T(8,128)(2,1)S(1)}, s16[264,1024]{1,0:T(8,128)(2,1)S(1)}, u32[]{:S(2)}, u32[]{:S(2)}) collective-permute-start(s16[264,1024]{1,0:T(8,128)(2,1)S(1)} %shard_map.68), channel_id=1, source_target_pairs={{0,256},{256,0},{1,257},{257,1},{2,258},{258,2},{3,259},{259,3},{4... | collective-permute-start | bytes 1622024 | tf_op jit(solution)/shard_map/ppermute | solution.py:77
  29.6 11.2 %all-to-all-start.1 = ((s32[16,1,128]{2,1,0:T(1,128)}), s32[16,1,128]{2,1,0:T(1,128)S(1)}, u32[]{:S(2)}, u32[]{:S(2)}) async-start(s32[16,1,128]{2,1,0:T(1,128)} %broadcast_in_dim.39), calls=%async_computation.1 | async-start | bytes 16384 | tf_op jit(solution)/shard_map/all_to_all | solution.py:23
  164.2 37.4 %copy-start = (bf16[96,96]{1,0:T(8,128)(2,1)S(1)}, bf16[96,96]{1,0:T(8,128)(2,1)}, u32[]{:S(2)}) copy-start(bf16[96,96]{1,0:T(8,128)(2,1)} %constant.19.clone) | copy-start | bytes 55300

commit v16 on v15

--- a/solution.py
+++ b/solution.py
@@ -33,13 +33,17 @@
     return total.astype(BF16)
 
 
-def pack(counts_hbm, totals_hbm, out_ref, counts_ref, totals_ref, sems):
+def pack(
+    counts_hbm, totals_hbm, genes_hbm, test_hbm, out_ref, genes_ref, test_ref, counts_ref, totals_ref, sems
+):
     rows, cols = counts_hbm.shape
     whole = [pltpu.make_async_copy(totals_hbm, totals_ref, sems.at[PARTS])]
     step = rows // PARTS
     for i in range(PARTS):
         part = pl.ds(i * step, step)
         whole.append(pltpu.make_async_copy(counts_hbm.at[part], counts_ref.at[part], sems.at[i]))
+    whole.append(pltpu.make_async_copy(genes_hbm, genes_ref, sems.at[PARTS + 1]))
+    whole.append(pltpu.make_async_copy(test_hbm, test_ref, sems.at[PARTS + 2]))
     for copy in whole:
         copy.start()
     whole[0].wait()
@@ -50,21 +54,27 @@
     for i in range(PARTS):
         whole[i + 1].wait()
         out_ref[i * step : (i + 1) * step] = counts_ref[i * step : (i + 1) * step].astype(I16)
+    whole[PARTS + 1].wait()
+    whole[PARTS + 2].wait()
 
 
 def shards(counts, cell_totals, gene_totals, test_matrix):
     rows, cols = counts.shape
     scale = 1.0 / math.sqrt(rows * Y_HI * Z * CORE + cols * Y_LO * X)
 
-    mine = pl.pallas_call(
+    mine, gene_totals, test = pl.pallas_call(
         pack,
-        out_shape=jax.ShapeDtypeStruct((rows + EXTRA, cols), I16),
-        in_specs=[pl.BlockSpec(memory_space=pltpu.HBM)] * 2,
-        out_specs=pl.BlockSpec(memory_space=pltpu.VMEM),
+        out_shape=[
+            jax.ShapeDtypeStruct((rows + EXTRA, cols), I16),
+            jax.ShapeDtypeStruct((8, cols // 8), jnp.int32),
+            jax.ShapeDtypeStruct(test_matrix.shape[::-1], BF16),
+        ],
+        in_specs=[pl.BlockSpec(memory_space=pltpu.HBM)] * 4,
+        out_specs=[pl.BlockSpec(memory_space=pltpu.VMEM)] * 3,
         scratch_shapes=[
             pltpu.VMEM((rows, cols), jnp.int32),
             pltpu.VMEM((1, rows), jnp.int32),
-            pltpu.SemaphoreType.DMA((PARTS + 1,)),
+            pltpu.SemaphoreType.DMA((PARTS + 3,)),
         ],
         compiler_params=pltpu.CompilerParams(vmem_limit_bytes=4 << 20),
         cost_estimate=pl.CostEstimate(
@@ -73,10 +83,13 @@
     )(
         pltpu.with_memory_space_constraint(counts, pltpu.HBM),
         pltpu.with_memory_space_constraint(cell_totals[None], pltpu.HBM),
+        pltpu.with_memory_space_constraint(gene_totals.reshape(8, -1), pltpu.HBM),
+        pltpu.with_memory_space_constraint(test_matrix.T, pltpu.HBM),
     )
+    gene_totals = gene_totals.reshape(-1)
     other = lax.ppermute(mine, "y_hi", [(0, 1), (1, 0)])
 
-    test = spread(test_matrix.T, "z", Z)
+    test = spread(test, "z", Z)
     ready, test = lax.optimization_barrier((gene_totals.reshape(8, -1), test))
     totals = spread(jnp.sum(ready, axis=0, keepdims=True), ("y_lo", "x"), Y_LO * X)
     test, totals = lax.optimization_barrier((test, totals))

time: 205 us -> 205 us (level)
  transfers between devices with their start and end apart: 2 -> 2, of which waited for: 1 -> 1; matrix products, arithmetic and copies ran while one was open for 2% -> 1% of each run, Pallas kernels for 0% -> 0%
where the time goes in v16:
time: 205 us; the launch traced here: 203 us
  blocking collectives  171 us (83%)
  starting transfers between devices  12.7 us (6%)
  waiting for transfers between devices  6.68 us (3%)
  matrix products  5.79 us (3%)
  other arithmetic  2.88 us (1%)
    all_to_all x13, blocking collectives, spread(): return lax.all_to_all(copies(x, n), axis, 0, 0)  140 us
    all_to_all x1, blocking collectives, shards(): got = lax.all_to_all(send, ('core', 'y_hi'), 0, 0)  24.2 us
    ppermute x1, starting transfers between devices, shards(): other = lax.ppermute(mine, 'y_hi', [(0, 1), (1, 0)])  8.28 us
    all_to_all x1, waiting for transfers between devices, spread(): return lax.all_to_all(copies(x, n), axis, 0, 0)  6.68 us
    all_gather x1, blocking collectives, shards(): blocks = lax.all_gather(pair, 'core').reshape(BLOCKS, rows + EXTRA, cols)  6.5 us
    all_to_all x1, starting transfers between devices, spread(): return lax.all_to_all(copies(x, n), axis, 0, 0)  4.47 us
  transfers between devices with their start and end apart: 2, of which 1 were waited for; matrix products, arithmetic and copies ran while one was open for 1% of the time, Pallas kernels for 0%

profile of v16, /device:TPU:1, one launch (start us, length us, event | category | flops | bytes accessed | tf_op | source)
XLA Modules:
  0.0 202.6 jit_solution(2806186933092668788)
XLA Ops:
  0.6 1.3 shard_map.68
  1.9 8.3 %collective-permute-start = (s16[264,1024]{1,0:T(8,128)(2,1)S(1)}, s16[264,1024]{1,0:T(8,128)(2,1)S(1)}, u32[]{:S(2)}, u32[]{:S(2)}) collective-permute-start(s16[264,1024]{1,0:T(8,128)(2,1)S(1)} %get-tuple-element.16), channel_id=1, source_target_pairs={{0,256},{256,0},{1,257},{257,1},{2,258},{258,2},{3,259},{259,3},{4... | collective-permute-start | bytes 1622024 | tf_op jit(solution)/shard_map/ppermute | solution.py:90
  10.2 17.4 %all_to_all.75 = bf16[8,3,1024]{2,1,0:T(4,128)(2,1)S(1)} all-to-all(bf16[8,3,1024]{2,1,0:T(4,128)(2,1)S(1)} %broadcast_in_dim.39), channel_id=1, replica_groups=mesh['y_hi'=2,'z'=8,'core'=2,'y_lo'=4,'x'=4] {'z'}, dimensions={0} | all-to-all | bytes 98304 | tf_op jit(solution)/shard_map/all_to_all | solution.py:23
  27.6 0.6 broadcast_in_dim.40
  28.2 4.5 %all-to-all-start.1 = ((s32[16,1,128]{2,1,0:T(1,128)}), s32[16,1,128]{2,1,0:T(1,128)S(1)}, u32[]{:S(2)}, u32[]{:S(2)}) async-start(s32[16,1,128]{2,1,0:T(1,128)} %broadcast_in_dim.40), calls=%async_computation.1 | async-start | bytes 16384 | tf_op jit(solution)/shard_map/all_to_all | solution.py:23
  32.7 6.7 %all-to-all-done.1 = s32[16,1,128]{2,1,0:T(1,128)S(1)} async-done(((s32[16,1,128]{2,1,0:T(1,128)}), s32[16,1,128]{2,1,0:T(1,128)S(1)}, u32[]{:S(2)}, u32[]{:S(2)}) %all-to-all-start.1) | async-done | bytes 8224 | tf_op jit(solution)/shard_map/all_to_all | solution.py:23
  39.4 0.6 reduce_sum.19
  40.7 0.0 collective-permute-done
  40.8 0.3 select_bitcast_fusion.1
  41.0 0.1 pad_add_fusion
  41.1 6.5 %all-gather.2 = s16[4,264,1024]{2,1,0:T(8,128)(2,1)S(1)} all-gather(s16[2,264,1024]{2,1,0:T(8,128)(2,1)S(1)} %pad_add_fusion), channel_id=2, replica_groups=mesh['y_hi'=2,'z'=8,'core'=2,'y_lo'=4,'x'=4] {'core'}, dimensions={0}, use_global_device_ids=true | all-gather | bytes 3244032 | tf_op jit(solution)/shard_map/all_gather | solution.py:102
  47.6 1.6 fusion.1
  49.2 0.7 convolution_convert_fusion.9
  49.9 7.8 %all_to_all.76 = bf16[4,24,1024]{2,1,0:T(8,128)(2,1)S(1)} all-to-all(bf16[4,24,1024]{2,1,0:T(8,128)(2,1)S(1)} %broadcast_in_dim.41), channel_id=1, replica_groups=mesh['y_hi'=2,'z'=8,'core'=2,'y_lo'=4,'x'=4] {'x'}, dimensions={0} | all-to-all | bytes 393216 | tf_op jit(solution)/shard_map/all_to_all | solution.py:23
  57.8 8.0 %all_to_all.77 = bf16[4,24,1024]{2,1,0:T(8,128)(2,1)S(1)} all-to-all(bf16[4,24,1024]{2,1,0:T(8,128)(2,1)S(1)} %broadcast_in_dim.43), channel_id=1, replica_groups=mesh['y_hi'=2,'z'=8,'core'=2,'y_lo'=4,'x'=4] {'y_lo'}, dimensions={0} | all-to-all | bytes 393216 | tf_op jit(solution)/shard_map/all_to_all | solution.py:23
  65.8 0.4 convolution_convert_fusion.8
  66.2 17.7 %all_to_all.78 = bf16[8,24,1024]{2,1,0:T(8,128)(2,1)S(1)} all-to-all(bf16[8,24,1024]{2,1,0:T(8,128)(2,1)S(1)} %broadcast_in_dim.44), channel_id=1, replica_groups=mesh['y_hi'=2,'z'=8,'core'=2,'y_lo'=4,'x'=4] {'z'}, dimensions={0} | all-to-all | bytes 786432 | tf_op jit(solution)/shard_map/all_to_all | solution.py:23
  84.0 0.7 convolution_convert_fusion.7
  84.7 7.5 %all_to_all.79 = bf16[4,24,1024]{2,1,0:T(8,128)(2,1)S(1)} all-to-all(bf16[4,24,1024]{2,1,0:T(8,128)(2,1)S(1)} %broadcast_in_dim.45), channel_id=1, replica_groups=mesh['y_hi'=2,'z'=8,'core'=2,'y_lo'=4,'x'=4] {'x'}, dimensions={0} | all-to-all | bytes 393216 | tf_op jit(solution)/shard_map/all_to_all | solution.py:23
  92.3 9.5 %all_to_all.80 = bf16[4,24,1024]{2,1,0:T(8,128)(2,1)S(1)} all-to-all(bf16[4,24,1024]{2,1,0:T(8,128)(2,1)S(1)} %broadcast_in_dim.47), channel_id=1, replica_groups=mesh['y_hi'=2,'z'=8,'core'=2,'y_lo'=4,'x'=4] {'y_lo'}, dimensions={0} | all-to-all | bytes 393216 | tf_op jit(solution)/shard_map/all_to_all | solution.py:23
  101.8 0.4 convolution_convert_fusion.6
  102.2 14.4 %all_to_all.81 = bf16[8,24,1024]{2,1,0:T(8,128)(2,1)S(1)} all-to-all(bf16[8,24,1024]{2,1,0:T(8,128)(2,1)S(1)} %broadcast_in_dim.48), channel_id=1, replica_groups=mesh['y_hi'=2,'z'=8,'core'=2,'y_lo'=4,'x'=4] {'z'}, dimensions={0} | all-to-all | bytes 786432 | tf_op jit(solution)/shard_map/all_to_all | solution.py:23
  116.6 0.7 convolution_convert_fusion.5
  117.3 7.5 %all_to_all.82 = bf16[4,24,1024]{2,1,0:T(8,128)(2,1)S(1)} all-to-all(bf16[4,24,1024]{2,1,0:T(8,128)(2,1)S(1)} %broadcast_in_dim.49), channel_id=1, replica_groups=mesh['y_hi'=2,'z'=8,'core'=2,'y_lo'=4,'x'=4] {'x'}, dimensions={0} | all-to-all | bytes 393216 | tf_op jit(solution)/shard_map/all_to_all | solution.py:23
  124.9 8.0 %all_to_all.83 = bf16[4,24,1024]{2,1,0:T(8,128)(2,1)S(1)} all-to-all(bf16[4,24,1024]{2,1,0:T(8,128)(2,1)S(1)} %broadcast_in_dim.51), channel_id=1, replica_groups=mesh['y_hi'=2,'z'=8,'core'=2,'y_lo'=4,'x'=4] {'y_lo'}, dimensions={0} | all-to-all | bytes 393216 | tf_op jit(solution)/shard_map/all_to_all | solution.py:23
  132.9 0.4 convolution_convert_fusion.4
  133.4 13.1 %all_to_all.84 = bf16[8,24,1024]{2,1,0:T(8,128)(2,1)S(1)} all-to-all(bf16[8,24,1024]{2,1,0:T(8,128)(2,1)S(1)} %broadcast_in_dim.52), channel_id=1, replica_groups=mesh['y_hi'=2,'z'=8,'core'=2,'y_lo'=4,'x'=4] {'z'}, dimensions={0} | all-to-all | bytes 786432 | tf_op jit(solution)/shard_map/all_to_all | solution.py:23
  146.5 0.7 convolution_convert_fusion.3
  147.2 7.8 %all_to_all.85 = bf16[4,24,1024]{2,1,0:T(8,128)(2,1)S(1)} all-to-all(bf16[4,24,1024]{2,1,0:T(8,128)(2,1)S(1)} %broadcast_in_dim.53), channel_id=1, replica_groups=mesh['y_hi'=2,'z'=8,'core'=2,'y_lo'=4,'x'=4] {'x'}, dimensions={0} | all-to-all | bytes 393216 | tf_op jit(solution)/shard_map/all_to_all | solution.py:23
  155.1 8.0 %all_to_all.86 = bf16[4,24,1024]{2,1,0:T(8,128)(2,1)S(1)} all-to-all(bf16[4,24,1024]{2,1,0:T(8,128)(2,1)S(1)} %broadcast_in_dim.55), channel_id=1, replica_groups=mesh['y_hi'=2,'z'=8,'core'=2,'y_lo'=4,'x'=4] {'y_lo'}, dimensions={0} | all-to-all | bytes 393216 | tf_op jit(solution)/shard_map/all_to_all | solution.py:23
  163.1 0.4 convolution_convert_fusion.2
  163.5 0.0 copy-start
  163.6 13.1 %all_to_all.87 = bf16[8,24,1024]{2,1,0:T(8,128)(2,1)S(1)} all-to-all(bf16[8,24,1024]{2,1,0:T(8,128)(2,1)S(1)} %broadcast_in_dim.56), channel_id=1, replica_groups=mesh['y_hi'=2,'z'=8,'core'=2,'y_lo'=4,'x'=4] {'z'}, dimensions={0} | all-to-all | bytes 786432 | tf_op jit(solution)/shard_map/all_to_all | solution.py:23
  176.7 0.1 fusion.22
  176.8 24.2 %all_to_all.88 = bf16[4,24,1280]{2,1,0:T(8,128)(2,1)S(1)} all-to-all(bf16[4,24,1280]{2,1,0:T(8,128)(2,1)S(1)} %pad_maximum_fusion), channel_id=1, replica_groups=mesh['y_hi'=2,'z'=8,'core'=2,'y_lo'=4,'x'=4] {'core','y_hi'}, dimensions={0} | all-to-all | bytes 491520 | tf_op jit(solution)/shard_map/all_to_all | solution.py:139
  201.0 0.0 copy-done
  201.0 0.8 convolution_convert_fusion.1
  201.7 0.9 convolution_convert_fusion
  (27 shorter events, 0.7 us)
Async XLA Ops:
  1.9 38.8 %collective-permute-start = (s16[264,1024]{1,0:T(8,128)(2,1)S(1)}, s16[264,1024]{1,0:T(8,128)(2,1)S(1)}, u32[]{:S(2)}, u32[]{:S(2)}) collective-permute-start(s16[264,1024]{1,0:T(8,128)(2,1)S(1)} %get-tuple-element.16), channel_id=1, source_target_pairs={{0,256},{256,0},{1,257},{257,1},{2,258},{258,2},{3,259},{259,3},{4... | collective-permute-start | bytes 1622024 | tf_op jit(solution)/shard_map/ppermute | solution.py:90
  28.2 11.2 %all-to-all-start.1 = ((s32[16,1,128]{2,1,0:T(1,128)}), s32[16,1,128]{2,1,0:T(1,128)S(1)}, u32[]{:S(2)}, u32[]{:S(2)}) async-start(s32[16,1,128]{2,1,0:T(1,128)} %broadcast_in_dim.40), calls=%async_computation.1 | async-start | bytes 16384 | tf_op jit(solution)/shard_map/all_to_all | solution.py:23
  163.5 37.5 %copy-start = (bf16[96,96]{1,0:T(8,128)(2,1)S(1)}, bf16[96,96]{1,0:T(8,128)(2,1)}, u32[]{:S(2)}) copy-start(bf16[96,96]{1,0:T(8,128)(2,1)} %constant.19.clone) | copy-start | bytes 55300

commit v17 on v16

--- a/solution.py
+++ b/solution.py
@@ -56,6 +56,20 @@
         out_ref[i * step : (i + 1) * step] = counts_ref[i * step : (i + 1) * step].astype(I16)
     whole[PARTS + 1].wait()
     whole[PARTS + 2].wait()
+
+
+def place(pick_ref, got_ref, sketch_hbm, panel_hbm, sketch_ref, panel_ref, sems):
+    rows = sketch_ref.shape[1]
+    panel = jnp.dot(pick_ref[...], got_ref[:, rows:], preferred_element_type=F32)
+    panel_ref[...] = panel.astype(BF16)
+    first = pltpu.make_async_copy(panel_ref, panel_hbm, sems.at[0])
+    first.start()
+    sketch = jnp.dot(pick_ref[...], got_ref[:, :rows], preferred_element_type=F32)
+    sketch_ref[...] = sketch.astype(BF16)
+    second = pltpu.make_async_copy(sketch_ref, sketch_hbm, sems.at[1])
+    second.start()
+    first.wait()
+    second.wait()
 
 
 def shards(counts, cell_totals, gene_totals, test_matrix):
@@ -139,10 +153,20 @@
     got = lax.all_to_all(send, ("core", "y_hi"), 0, 0)
     got = got.reshape(-1, rows + cols)
 
-    def ordered(block):
-        return jnp.dot(pick, block, preferred_element_type=F32).astype(BF16).T
-
-    return (ordered(got[:, :rows]), ordered(got[:, rows:]))
+    whole, own = (count, cols), (count, rows)
+    sketch, gene_panel = pl.pallas_call(
+        place,
+        out_shape=[jax.ShapeDtypeStruct(own, BF16), jax.ShapeDtypeStruct(whole, BF16)],
+        in_specs=[pl.BlockSpec(memory_space=pltpu.VMEM)] * 2,
+        out_specs=[pl.BlockSpec(memory_space=pltpu.HBM)] * 2,
+        scratch_shapes=[
+            pltpu.VMEM(own, BF16),
+            pltpu.VMEM(whole, BF16),
+            pltpu.SemaphoreType.DMA((2,)),
+        ],
+        compiler_params=pltpu.CompilerParams(vmem_limit_bytes=4 << 20),
+    )(pick, got)
+    return (sketch.T, gene_panel.T)
 
 
 def solution(mesh):

time: 205 us -> 204 us (level)
  no operation moved by 1% of the time
where the time goes in v17:
time: 204 us; the launch traced here: 202 us
  blocking collectives  171 us (84%)
  starting transfers between devices  12.7 us (6%)
  waiting for transfers between devices  6.68 us (3%)
  matrix products  4.16 us (2%)
  other arithmetic  2.88 us (1%)
  Pallas kernels  2.19 us (1%)
    all_to_all x13, blocking collectives, spread(): return lax.all_to_all(copies(x, n), axis, 0, 0)  140 us
    all_to_all x1, blocking collectives, shards(): got = lax.all_to_all(send, ('core', 'y_hi'), 0, 0)  24.2 us
    ppermute x1, starting transfers between devices, shards(): other = lax.ppermute(mine, 'y_hi', [(0, 1), (1, 0)])  8.28 us
    all_to_all x1, waiting for transfers between devices, spread(): return lax.all_to_all(copies(x, n), axis, 0, 0)  6.68 us
    all_gather x1, blocking collectives, shards(): blocks = lax.all_gather(pair, 'core').reshape(BLOCKS, rows + EXTRA, cols)  6.5 us
    all_to_all x1, starting transfers between devices, spread(): return lax.all_to_all(copies(x, n), axis, 0, 0)  4.47 us
  transfers between devices with their start and end apart: 2, of which 1 were waited for; matrix products, arithmetic and copies ran while one was open for 1% of the time, Pallas kernels for 0%

profile of v17, /device:TPU:1, one launch (start us, length us, event | category | flops | bytes accessed | tf_op | source)
XLA Modules:
  0.0 201.9 jit_solution(12053571589219769039)
XLA Ops:
  0.6 1.3 shard_map.68
  1.9 8.3 %collective-permute-start = (s16[264,1024]{1,0:T(8,128)(2,1)S(1)}, s16[264,1024]{1,0:T(8,128)(2,1)S(1)}, u32[]{:S(2)}, u32[]{:S(2)}) collective-permute-start(s16[264,1024]{1,0:T(8,128)(2,1)S(1)} %get-tuple-element.18), channel_id=1, source_target_pairs={{0,256},{256,0},{1,257},{257,1},{2,258},{258,2},{3,259},{259,3},{4... | collective-permute-start | bytes 1622024 | tf_op jit(solution)/shard_map/ppermute | solution.py:104
  10.2 17.4 %all_to_all.75 = bf16[8,3,1024]{2,1,0:T(4,128)(2,1)S(1)} all-to-all(bf16[8,3,1024]{2,1,0:T(4,128)(2,1)S(1)} %broadcast_in_dim.39), channel_id=1, replica_groups=mesh['y_hi'=2,'z'=8,'core'=2,'y_lo'=4,'x'=4] {'z'}, dimensions={0} | all-to-all | bytes 98304 | tf_op jit(solution)/shard_map/all_to_all | solution.py:23
  27.6 0.6 broadcast_in_dim.40
  28.2 4.5 %all-to-all-start.1 = ((s32[16,1,128]{2,1,0:T(1,128)}), s32[16,1,128]{2,1,0:T(1,128)S(1)}, u32[]{:S(2)}, u32[]{:S(2)}) async-start(s32[16,1,128]{2,1,0:T(1,128)} %broadcast_in_dim.40), calls=%async_computation.1 | async-start | bytes 16384 | tf_op jit(solution)/shard_map/all_to_all | solution.py:23
  32.7 6.7 %all-to-all-done.1 = s32[16,1,128]{2,1,0:T(1,128)S(1)} async-done(((s32[16,1,128]{2,1,0:T(1,128)}), s32[16,1,128]{2,1,0:T(1,128)S(1)}, u32[]{:S(2)}, u32[]{:S(2)}) %all-to-all-start.1) | async-done | bytes 8224 | tf_op jit(solution)/shard_map/all_to_all | solution.py:23
  39.4 0.6 reduce_sum.19
  40.7 0.0 collective-permute-done
  40.8 0.3 select_bitcast_fusion.1
  41.0 0.1 pad_add_fusion
  41.1 6.5 %all-gather.2 = s16[4,264,1024]{2,1,0:T(8,128)(2,1)S(1)} all-gather(s16[2,264,1024]{2,1,0:T(8,128)(2,1)S(1)} %pad_add_fusion), channel_id=2, replica_groups=mesh['y_hi'=2,'z'=8,'core'=2,'y_lo'=4,'x'=4] {'core'}, dimensions={0}, use_global_device_ids=true | all-gather | bytes 3244032 | tf_op jit(solution)/shard_map/all_gather | solution.py:116
  47.6 1.6 fusion.1
  49.2 0.7 convolution_convert_fusion.7
  49.9 7.8 %all_to_all.76 = bf16[4,24,1024]{2,1,0:T(8,128)(2,1)S(1)} all-to-all(bf16[4,24,1024]{2,1,0:T(8,128)(2,1)S(1)} %broadcast_in_dim.41), channel_id=1, replica_groups=mesh['y_hi'=2,'z'=8,'core'=2,'y_lo'=4,'x'=4] {'x'}, dimensions={0} | all-to-all | bytes 393216 | tf_op jit(solution)/shard_map/all_to_all | solution.py:23
  57.8 8.0 %all_to_all.77 = bf16[4,24,1024]{2,1,0:T(8,128)(2,1)S(1)} all-to-all(bf16[4,24,1024]{2,1,0:T(8,128)(2,1)S(1)} %broadcast_in_dim.43), channel_id=1, replica_groups=mesh['y_hi'=2,'z'=8,'core'=2,'y_lo'=4,'x'=4] {'y_lo'}, dimensions={0} | all-to-all | bytes 393216 | tf_op jit(solution)/shard_map/all_to_all | solution.py:23
  65.8 0.4 convolution_convert_fusion.6
  66.2 17.7 %all_to_all.78 = bf16[8,24,1024]{2,1,0:T(8,128)(2,1)S(1)} all-to-all(bf16[8,24,1024]{2,1,0:T(8,128)(2,1)S(1)} %broadcast_in_dim.44), channel_id=1, replica_groups=mesh['y_hi'=2,'z'=8,'core'=2,'y_lo'=4,'x'=4] {'z'}, dimensions={0} | all-to-all | bytes 786432 | tf_op jit(solution)/shard_map/all_to_all | solution.py:23
  84.0 0.7 convolution_convert_fusion.5
  84.7 7.5 %all_to_all.79 = bf16[4,24,1024]{2,1,0:T(8,128)(2,1)S(1)} all-to-all(bf16[4,24,1024]{2,1,0:T(8,128)(2,1)S(1)} %broadcast_in_dim.45), channel_id=1, replica_groups=mesh['y_hi'=2,'z'=8,'core'=2,'y_lo'=4,'x'=4] {'x'}, dimensions={0} | all-to-all | bytes 393216 | tf_op jit(solution)/shard_map/all_to_all | solution.py:23
  92.3 9.5 %all_to_all.80 = bf16[4,24,1024]{2,1,0:T(8,128)(2,1)S(1)} all-to-all(bf16[4,24,1024]{2,1,0:T(8,128)(2,1)S(1)} %broadcast_in_dim.47), channel_id=1, replica_groups=mesh['y_hi'=2,'z'=8,'core'=2,'y_lo'=4,'x'=4] {'y_lo'}, dimensions={0} | all-to-all | bytes 393216 | tf_op jit(solution)/shard_map/all_to_all | solution.py:23
  101.8 0.4 convolution_convert_fusion.4
  102.2 14.4 %all_to_all.81 = bf16[8,24,1024]{2,1,0:T(8,128)(2,1)S(1)} all-to-all(bf16[8,24,1024]{2,1,0:T(8,128)(2,1)S(1)} %broadcast_in_dim.48), channel_id=1, replica_groups=mesh['y_hi'=2,'z'=8,'core'=2,'y_lo'=4,'x'=4] {'z'}, dimensions={0} | all-to-all | bytes 786432 | tf_op jit(solution)/shard_map/all_to_all | solution.py:23
  116.6 0.7 convolution_convert_fusion.3
  117.3 7.5 %all_to_all.82 = bf16[4,24,1024]{2,1,0:T(8,128)(2,1)S(1)} all-to-all(bf16[4,24,1024]{2,1,0:T(8,128)(2,1)S(1)} %broadcast_in_dim.49), channel_id=1, replica_groups=mesh['y_hi'=2,'z'=8,'core'=2,'y_lo'=4,'x'=4] {'x'}, dimensions={0} | all-to-all | bytes 393216 | tf_op jit(solution)/shard_map/all_to_all | solution.py:23
  124.9 8.0 %all_to_all.83 = bf16[4,24,1024]{2,1,0:T(8,128)(2,1)S(1)} all-to-all(bf16[4,24,1024]{2,1,0:T(8,128)(2,1)S(1)} %broadcast_in_dim.51), channel_id=1, replica_groups=mesh['y_hi'=2,'z'=8,'core'=2,'y_lo'=4,'x'=4] {'y_lo'}, dimensions={0} | all-to-all | bytes 393216 | tf_op jit(solution)/shard_map/all_to_all | solution.py:23
  132.9 0.4 convolution_convert_fusion.2
  133.4 13.1 %all_to_all.84 = bf16[8,24,1024]{2,1,0:T(8,128)(2,1)S(1)} all-to-all(bf16[8,24,1024]{2,1,0:T(8,128)(2,1)S(1)} %broadcast_in_dim.52), channel_id=1, replica_groups=mesh['y_hi'=2,'z'=8,'core'=2,'y_lo'=4,'x'=4] {'z'}, dimensions={0} | all-to-all | bytes 786432 | tf_op jit(solution)/shard_map/all_to_all | solution.py:23
  146.5 0.7 convolution_convert_fusion.1
  147.2 7.8 %all_to_all.85 = bf16[4,24,1024]{2,1,0:T(8,128)(2,1)S(1)} all-to-all(bf16[4,24,1024]{2,1,0:T(8,128)(2,1)S(1)} %broadcast_in_dim.53), channel_id=1, replica_groups=mesh['y_hi'=2,'z'=8,'core'=2,'y_lo'=4,'x'=4] {'x'}, dimensions={0} | all-to-all | bytes 393216 | tf_op jit(solution)/shard_map/all_to_all | solution.py:23
  155.1 8.0 %all_to_all.86 = bf16[4,24,1024]{2,1,0:T(8,128)(2,1)S(1)} all-to-all(bf16[4,24,1024]{2,1,0:T(8,128)(2,1)S(1)} %broadcast_in_dim.55), channel_id=1, replica_groups=mesh['y_hi'=2,'z'=8,'core'=2,'y_lo'=4,'x'=4] {'y_lo'}, dimensions={0} | all-to-all | bytes 393216 | tf_op jit(solution)/shard_map/all_to_all | solution.py:23
  163.1 0.4 convolution_convert_fusion
  163.5 0.0 copy-start
  163.6 13.1 %all_to_all.87 = bf16[8,24,1024]{2,1,0:T(8,128)(2,1)S(1)} all-to-all(bf16[8,24,1024]{2,1,0:T(8,128)(2,1)S(1)} %broadcast_in_dim.56), channel_id=1, replica_groups=mesh['y_hi'=2,'z'=8,'core'=2,'y_lo'=4,'x'=4] {'z'}, dimensions={0} | all-to-all | bytes 786432 | tf_op jit(solution)/shard_map/all_to_all | solution.py:23
  176.7 0.1 fusion.21
  176.8 24.2 %all_to_all.88 = bf16[4,24,1280]{2,1,0:T(8,128)(2,1)S(1)} all-to-all(bf16[4,24,1280]{2,1,0:T(8,128)(2,1)S(1)} %pad_maximum_fusion), channel_id=1, replica_groups=mesh['y_hi'=2,'z'=8,'core'=2,'y_lo'=4,'x'=4] {'core','y_hi'}, dimensions={0} | all-to-all | bytes 491520 | tf_op jit(solution)/shard_map/all_to_all | solution.py:153
  201.0 0.0 copy-done
  201.0 0.9 shard_map.69
  (27 shorter events, 0.7 us)
Async XLA Ops:
  1.9 38.8 %collective-permute-start = (s16[264,1024]{1,0:T(8,128)(2,1)S(1)}, s16[264,1024]{1,0:T(8,128)(2,1)S(1)}, u32[]{:S(2)}, u32[]{:S(2)}) collective-permute-start(s16[264,1024]{1,0:T(8,128)(2,1)S(1)} %get-tuple-element.18), channel_id=1, source_target_pairs={{0,256},{256,0},{1,257},{257,1},{2,258},{258,2},{3,259},{259,3},{4... | collective-permute-start | bytes 1622024 | tf_op jit(solution)/shard_map/ppermute | solution.py:104
  28.2 11.2 %all-to-all-start.1 = ((s32[16,1,128]{2,1,0:T(1,128)}), s32[16,1,128]{2,1,0:T(1,128)S(1)}, u32[]{:S(2)}, u32[]{:S(2)}) async-start(s32[16,1,128]{2,1,0:T(1,128)} %broadcast_in_dim.40), calls=%async_computation.1 | async-start | bytes 16384 | tf_op jit(solution)/shard_map/all_to_all | solution.py:23
  163.5 37.5 %copy-start = (bf16[96,96]{1,0:T(8,128)(2,1)S(1)}, bf16[96,96]{1,0:T(8,128)(2,1)}, u32[]{:S(2)}) copy-start(bf16[96,96]{1,0:T(8,128)(2,1)} %constant.19.clone.pick_ref) | copy-start | bytes 55300

commit v18 on v17

--- a/solution.py
+++ b/solution.py
@@ -10,7 +10,7 @@
 
 ITERS = 3
 Y_HI, Z, CORE, Y_LO, X = 2, 8, 2, 4, 4
-BLOCKS, PARTS = CORE * Y_HI, 4
+BLOCKS, PARTS = CORE * Y_HI, 2
 EXTRA = 8
 F32, BF16, I16 = jnp.float32, jnp.bfloat16, jnp.int16
 

time: 204 us -> 204 us (level)
  no operation moved by 1% of the time
where the time goes in v18:
time: 204 us; the launch traced here: 202 us
  blocking collectives  171 us (84%)
  starting transfers between devices  12.7 us (6%)
  waiting for transfers between devices  6.68 us (3%)
  matrix products  4.16 us (2%)
  other arithmetic  2.88 us (1%)
  Pallas kernels  2.2 us (1%)
    all_to_all x13, blocking collectives, spread(): return lax.all_to_all(copies(x, n), axis, 0, 0)  140 us
    all_to_all x1, blocking collectives, shards(): got = lax.all_to_all(send, ('core', 'y_hi'), 0, 0)  24.2 us
    ppermute x1, starting transfers between devices, shards(): other = lax.ppermute(mine, 'y_hi', [(0, 1), (1, 0)])  8.28 us
    all_to_all x1, waiting for transfers between devices, spread(): return lax.all_to_all(copies(x, n), axis, 0, 0)  6.68 us
    all_gather x1, blocking collectives, shards(): blocks = lax.all_gather(pair, 'core').reshape(BLOCKS, rows + EXTRA, cols)  6.5 us
    all_to_all x1, starting transfers between devices, spread(): return lax.all_to_all(copies(x, n), axis, 0, 0)  4.47 us
  transfers between devices with their start and end apart: 2, of which 1 were waited for; matrix products, arithmetic and copies ran while one was open for 1% of the time, Pallas kernels for 0%

profile of v18, /device:TPU:1, one launch (start us, length us, event | category | flops | bytes accessed | tf_op | source)
XLA Modules:
  0.0 201.9 jit_solution(8528645525225551726)
XLA Ops:
  0.6 1.3 shard_map.68
  1.9 8.3 %collective-permute-start = (s16[264,1024]{1,0:T(8,128)(2,1)S(1)}, s16[264,1024]{1,0:T(8,128)(2,1)S(1)}, u32[]{:S(2)}, u32[]{:S(2)}) collective-permute-start(s16[264,1024]{1,0:T(8,128)(2,1)S(1)} %get-tuple-element.18), channel_id=1, source_target_pairs={{0,256},{256,0},{1,257},{257,1},{2,258},{258,2},{3,259},{259,3},{4... | collective-permute-start | bytes 1622024 | tf_op jit(solution)/shard_map/ppermute | solution.py:104
  10.2 17.4 %all_to_all.75 = bf16[8,3,1024]{2,1,0:T(4,128)(2,1)S(1)} all-to-all(bf16[8,3,1024]{2,1,0:T(4,128)(2,1)S(1)} %broadcast_in_dim.39), channel_id=1, replica_groups=mesh['y_hi'=2,'z'=8,'core'=2,'y_lo'=4,'x'=4] {'z'}, dimensions={0} | all-to-all | bytes 98304 | tf_op jit(solution)/shard_map/all_to_all | solution.py:23
  27.6 0.6 broadcast_in_dim.40
  28.2 4.5 %all-to-all-start.1 = ((s32[16,1,128]{2,1,0:T(1,128)}), s32[16,1,128]{2,1,0:T(1,128)S(1)}, u32[]{:S(2)}, u32[]{:S(2)}) async-start(s32[16,1,128]{2,1,0:T(1,128)} %broadcast_in_dim.40), calls=%async_computation.1 | async-start | bytes 16384 | tf_op jit(solution)/shard_map/all_to_all | solution.py:23
  32.7 6.7 %all-to-all-done.1 = s32[16,1,128]{2,1,0:T(1,128)S(1)} async-done(((s32[16,1,128]{2,1,0:T(1,128)}), s32[16,1,128]{2,1,0:T(1,128)S(1)}, u32[]{:S(2)}, u32[]{:S(2)}) %all-to-all-start.1) | async-done | bytes 8224 | tf_op jit(solution)/shard_map/all_to_all | solution.py:23
  39.4 0.6 reduce_sum.19
  40.8 0.0 collective-permute-done
  40.8 0.3 select_bitcast_fusion.1
  41.0 0.1 pad_add_fusion
  41.1 6.5 %all-gather.2 = s16[4,264,1024]{2,1,0:T(8,128)(2,1)S(1)} all-gather(s16[2,264,1024]{2,1,0:T(8,128)(2,1)S(1)} %pad_add_fusion), channel_id=2, replica_groups=mesh['y_hi'=2,'z'=8,'core'=2,'y_lo'=4,'x'=4] {'core'}, dimensions={0}, use_global_device_ids=true | all-gather | bytes 3244032 | tf_op jit(solution)/shard_map/all_gather | solution.py:116
  47.7 1.6 fusion.1
  49.2 0.7 convolution_convert_fusion.7
  49.9 7.8 %all_to_all.76 = bf16[4,24,1024]{2,1,0:T(8,128)(2,1)S(1)} all-to-all(bf16[4,24,1024]{2,1,0:T(8,128)(2,1)S(1)} %broadcast_in_dim.41), channel_id=1, replica_groups=mesh['y_hi'=2,'z'=8,'core'=2,'y_lo'=4,'x'=4] {'x'}, dimensions={0} | all-to-all | bytes 393216 | tf_op jit(solution)/shard_map/all_to_all | solution.py:23
  57.8 8.0 %all_to_all.77 = bf16[4,24,1024]{2,1,0:T(8,128)(2,1)S(1)} all-to-all(bf16[4,24,1024]{2,1,0:T(8,128)(2,1)S(1)} %broadcast_in_dim.43), channel_id=1, replica_groups=mesh['y_hi'=2,'z'=8,'core'=2,'y_lo'=4,'x'=4] {'y_lo'}, dimensions={0} | all-to-all | bytes 393216 | tf_op jit(solution)/shard_map/all_to_all | solution.py:23
  65.8 0.4 convolution_convert_fusion.6
  66.3 17.7 %all_to_all.78 = bf16[8,24,1024]{2,1,0:T(8,128)(2,1)S(1)} all-to-all(bf16[8,24,1024]{2,1,0:T(8,128)(2,1)S(1)} %broadcast_in_dim.44), channel_id=1, replica_groups=mesh['y_hi'=2,'z'=8,'core'=2,'y_lo'=4,'x'=4] {'z'}, dimensions={0} | all-to-all | bytes 786432 | tf_op jit(solution)/shard_map/all_to_all | solution.py:23
  84.0 0.7 convolution_convert_fusion.5
  84.7 7.5 %all_to_all.79 = bf16[4,24,1024]{2,1,0:T(8,128)(2,1)S(1)} all-to-all(bf16[4,24,1024]{2,1,0:T(8,128)(2,1)S(1)} %broadcast_in_dim.45), channel_id=1, replica_groups=mesh['y_hi'=2,'z'=8,'core'=2,'y_lo'=4,'x'=4] {'x'}, dimensions={0} | all-to-all | bytes 393216 | tf_op jit(solution)/shard_map/all_to_all | solution.py:23
  92.3 9.5 %all_to_all.80 = bf16[4,24,1024]{2,1,0:T(8,128)(2,1)S(1)} all-to-all(bf16[4,24,1024]{2,1,0:T(8,128)(2,1)S(1)} %broadcast_in_dim.47), channel_id=1, replica_groups=mesh['y_hi'=2,'z'=8,'core'=2,'y_lo'=4,'x'=4] {'y_lo'}, dimensions={0} | all-to-all | bytes 393216 | tf_op jit(solution)/shard_map/all_to_all | solution.py:23
  101.8 0.4 convolution_convert_fusion.4
  102.2 14.4 %all_to_all.81 = bf16[8,24,1024]{2,1,0:T(8,128)(2,1)S(1)} all-to-all(bf16[8,24,1024]{2,1,0:T(8,128)(2,1)S(1)} %broadcast_in_dim.48), channel_id=1, replica_groups=mesh['y_hi'=2,'z'=8,'core'=2,'y_lo'=4,'x'=4] {'z'}, dimensions={0} | all-to-all | bytes 786432 | tf_op jit(solution)/shard_map/all_to_all | solution.py:23
  116.6 0.7 convolution_convert_fusion.3
  117.3 7.5 %all_to_all.82 = bf16[4,24,1024]{2,1,0:T(8,128)(2,1)S(1)} all-to-all(bf16[4,24,1024]{2,1,0:T(8,128)(2,1)S(1)} %broadcast_in_dim.49), channel_id=1, replica_groups=mesh['y_hi'=2,'z'=8,'core'=2,'y_lo'=4,'x'=4] {'x'}, dimensions={0} | all-to-all | bytes 393216 | tf_op jit(solution)/shard_map/all_to_all | solution.py:23
  124.9 8.0 %all_to_all.83 = bf16[4,24,1024]{2,1,0:T(8,128)(2,1)S(1)} all-to-all(bf16[4,24,1024]{2,1,0:T(8,128)(2,1)S(1)} %broadcast_in_dim.51), channel_id=1, replica_groups=mesh['y_hi'=2,'z'=8,'core'=2,'y_lo'=4,'x'=4] {'y_lo'}, dimensions={0} | all-to-all | bytes 393216 | tf_op jit(solution)/shard_map/all_to_all | solution.py:23
  132.9 0.4 convolution_convert_fusion.2
  133.4 13.1 %all_to_all.84 = bf16[8,24,1024]{2,1,0:T(8,128)(2,1)S(1)} all-to-all(bf16[8,24,1024]{2,1,0:T(8,128)(2,1)S(1)} %broadcast_in_dim.52), channel_id=1, replica_groups=mesh['y_hi'=2,'z'=8,'core'=2,'y_lo'=4,'x'=4] {'z'}, dimensions={0} | all-to-all | bytes 786432 | tf_op jit(solution)/shard_map/all_to_all | solution.py:23
  146.5 0.7 convolution_convert_fusion.1
  147.2 7.8 %all_to_all.85 = bf16[4,24,1024]{2,1,0:T(8,128)(2,1)S(1)} all-to-all(bf16[4,24,1024]{2,1,0:T(8,128)(2,1)S(1)} %broadcast_in_dim.53), channel_id=1, replica_groups=mesh['y_hi'=2,'z'=8,'core'=2,'y_lo'=4,'x'=4] {'x'}, dimensions={0} | all-to-all | bytes 393216 | tf_op jit(solution)/shard_map/all_to_all | solution.py:23
  155.1 8.0 %all_to_all.86 = bf16[4,24,1024]{2,1,0:T(8,128)(2,1)S(1)} all-to-all(bf16[4,24,1024]{2,1,0:T(8,128)(2,1)S(1)} %broadcast_in_dim.55), channel_id=1, replica_groups=mesh['y_hi'=2,'z'=8,'core'=2,'y_lo'=4,'x'=4] {'y_lo'}, dimensions={0} | all-to-all | bytes 393216 | tf_op jit(solution)/shard_map/all_to_all | solution.py:23
  163.1 0.4 convolution_convert_fusion
  163.5 0.0 copy-start
  163.6 13.1 %all_to_all.87 = bf16[8,24,1024]{2,1,0:T(8,128)(2,1)S(1)} all-to-all(bf16[8,24,1024]{2,1,0:T(8,128)(2,1)S(1)} %broadcast_in_dim.56), channel_id=1, replica_groups=mesh['y_hi'=2,'z'=8,'core'=2,'y_lo'=4,'x'=4] {'z'}, dimensions={0} | all-to-all | bytes 786432 | tf_op jit(solution)/shard_map/all_to_all | solution.py:23
  176.7 0.1 fusion.21
  176.8 24.2 %all_to_all.88 = bf16[4,24,1280]{2,1,0:T(8,128)(2,1)S(1)} all-to-all(bf16[4,24,1280]{2,1,0:T(8,128)(2,1)S(1)} %pad_maximum_fusion), channel_id=1, replica_groups=mesh['y_hi'=2,'z'=8,'core'=2,'y_lo'=4,'x'=4] {'core','y_hi'}, dimensions={0} | all-to-all | bytes 491520 | tf_op jit(solution)/shard_map/all_to_all | solution.py:153
  201.0 0.0 copy-done
  201.0 0.9 shard_map.69
  (27 shorter events, 0.7 us)
Async XLA Ops:
  1.9 38.8 %collective-permute-start = (s16[264,1024]{1,0:T(8,128)(2,1)S(1)}, s16[264,1024]{1,0:T(8,128)(2,1)S(1)}, u32[]{:S(2)}, u32[]{:S(2)}) collective-permute-start(s16[264,1024]{1,0:T(8,128)(2,1)S(1)} %get-tuple-element.18), channel_id=1, source_target_pairs={{0,256},{256,0},{1,257},{257,1},{2,258},{258,2},{3,259},{259,3},{4... | collective-permute-start | bytes 1622024 | tf_op jit(solution)/shard_map/ppermute | solution.py:104
  28.2 11.2 %all-to-all-start.1 = ((s32[16,1,128]{2,1,0:T(1,128)}), s32[16,1,128]{2,1,0:T(1,128)S(1)}, u32[]{:S(2)}, u32[]{:S(2)}) async-start(s32[16,1,128]{2,1,0:T(1,128)} %broadcast_in_dim.40), calls=%async_computation.1 | async-start | bytes 16384 | tf_op jit(solution)/shard_map/all_to_all | solution.py:23
  163.5 37.5 %copy-start = (bf16[96,96]{1,0:T(8,128)(2,1)S(1)}, bf16[96,96]{1,0:T(8,128)(2,1)}, u32[]{:S(2)}) copy-start(bf16[96,96]{1,0:T(8,128)(2,1)} %constant.19.clone.pick_ref) | copy-start | bytes 55300
